TPU v7x, 32 devices: a whole 2x2x4 slice. The times are simulated.
32 devices in a mesh: dp: 16 (over z, x, core), mp: 2 (over y).
Axes of the slice: x: 2, y: 2, z: 4, core: 2. Of those that a mesh axis runs over, the one named last changes fastest.
Arguments:
- inputs: bfloat16 [2048, 2048], P('dp'), may hold values from -6 to 6
- segments: int32 [16, 128], P('dp'), may hold values from 0 to 1, never falling along the last dimension, each value on 1 to 96 neighbouring positions
- example_of: int32 [16, 2], P('dp'), may hold values from 0 to 1, each once within a row
- patches: bfloat16 [32, 64, 2048], P('dp'), may hold values from -6 to 6
- grad_out: bfloat16 [2048, 2048], P('dp'), may hold values from -6 to 6
- gain_self: bfloat16 [2048], P('dp'), may hold values from 0.5 to 1.5
- wq_self: bfloat16 [2048, 2048], P('dp', 'mp'), may hold values from -0.25 to 0.25
- wk_self: bfloat16 [2048, 2048], P('dp', 'mp'), may hold values from -0.125 to 0.125
- wv_self: bfloat16 [2048, 2048], P('dp', 'mp'), may hold values from -0.125 to 0.125
- wo_self: bfloat16 [2048, 2048], P('mp', 'dp'), may hold values from -0.25 to 0.25
- gain_cross: bfloat16 [2048], P('dp'), may hold values from 0.5 to 1.5
- wq_cross: bfloat16 [2048, 2048], P('dp', 'mp'), may hold values from -0.25 to 0.25
- wk_cross: bfloat16 [2048, 2048], P('dp', 'mp'), may hold values from -0.125 to 0.125
- wv_cross: bfloat16 [2048, 2048], P('dp', 'mp'), may hold values from -0.125 to 0.125
- wo_cross: bfloat16 [2048, 2048], P('mp', 'dp'), may hold values from -0.25 to 0.25
- gain_ffn: bfloat16 [2048], P('dp'), may hold values from 0.5 to 1.5
- w_gate: bfloat16 [2048, 5120], P('dp', 'mp'), may hold values from -0.125 to 0.125
- w_up: bfloat16 [2048, 5120], P('dp', 'mp'), may hold values from -0.125 to 0.125
- w_down: bfloat16 [5120, 2048], P('mp', 'dp'), may hold values from -0.078125 to 0.078125
Outputs:
- output: float32 [2048, 2048], P('dp')
- grad_inputs: float32 [2048, 2048], P('dp')
- grad_patches: float32 [32, 64, 2048], P('dp')
- grad_gain_self: float32 [2048], P('dp')
- grad_wq_self: float32 [2048, 2048], P('dp', 'mp')
- grad_wk_self: float32 [2048, 2048], P('dp', 'mp')
- grad_wv_self: float32 [2048, 2048], P('dp', 'mp')
- grad_wo_self: float32 [2048, 2048], P('mp', 'dp')
- grad_gain_cross: float32 [2048], P('dp')
- grad_wq_cross: float32 [2048, 2048], P('dp', 'mp')
- grad_wk_cross: float32 [2048, 2048], P('dp', 'mp')
- grad_wv_cross: float32 [2048, 2048], P('dp', 'mp')
- grad_wo_cross: float32 [2048, 2048], P('mp', 'dp')
- grad_gain_ffn: float32 [2048], P('dp')
- grad_w_gate: float32 [2048, 5120], P('dp', 'mp')
- grad_w_up: float32 [2048, 5120], P('dp', 'mp')
- grad_w_down: float32 [5120, 2048], P('mp', 'dp')
Inputs may be any that keep to these rules, and one draw needn't show every extreme that they name: In each row the segment numbers never fall and each of the 2 segments holds at least one token. `example_of`: each row holds every number below 2 once.
All inputs are finite; a program needn't handle non-finite values.
Results may differ from a plain program's by a relative error of at most 0.025.
The roundings to bfloat16 on the way count: a program that leaves them out, or rounds other values in their place, can miss the bound.
Values may be sent and summed in bfloat16 or wider, within the bound.
No kernel may reach another device: no remote copies, remote signals or barrier semaphores. Data moves between devices by JAX's collectives and lax.ppermute only.
A program may use at most 320 MiB of HBM per device.

v0:
```python
import jax
import jax.numpy as jnp
from jax import lax
from jax.sharding import PartitionSpec as P

HEAD_DIM = 64


EPS = 1e-06
NEG = -1e30


def rms_norm(values, gain_row):
    return values * lax.rsqrt(jnp.mean(values * values, axis=-1, keepdims=True) + EPS) * gain_row


def gated_unit(gate_values, up_values):
    return jax.nn.gelu(gate_values, approximate=True) * up_values


def linear(first_operand, second_operand):
    return jnp.dot(first_operand, second_operand, preferred_element_type=jnp.float32)


def back_rows(grad_rows, weight):
    return jnp.einsum("tc,dc->td", grad_rows, weight, preferred_element_type=jnp.float32)


def weight_term(source, grad_rows):
    return jnp.einsum("td,tc->dc", source, grad_rows, preferred_element_type=jnp.float32)


def attend_scores(queries, key_rows, allowed):
    score_scale = HEAD_DIM ** (-0.5)
    scores = (
        jnp.einsum("qhe,khe->hqk", queries, key_rows, preferred_element_type=jnp.float32)
        * score_scale
    )
    return jnp.where(allowed[None], scores, NEG)


def attend_forward(queries, key_rows, value_rows, allowed):
    scores = attend_scores(queries, key_rows, allowed)
    row_max = jnp.max(scores, axis=-1, keepdims=True)
    raised = jnp.exp(scores - row_max)
    row_sum = jnp.sum(raised, axis=-1, keepdims=True)
    softmax_rows = (raised / row_sum).astype(jnp.bfloat16)
    attended = jnp.einsum(
        "hqk,khe->qhe", softmax_rows, value_rows, preferred_element_type=jnp.float32
    )
    return (attended, row_max + jnp.log(row_sum))


def attend_backward(queries, key_rows, value_rows, allowed, log_sum, grad_attended):
    score_scale = HEAD_DIM ** (-0.5)
    softmax_rows = jnp.exp(attend_scores(queries, key_rows, allowed) - log_sum)
    grad_softmax = jnp.einsum(
        "qhe,khe->hqk", grad_attended, value_rows, preferred_element_type=jnp.float32
    )
    grad_values = jnp.einsum(
        "hqk,qhe->khe",
        softmax_rows.astype(jnp.bfloat16),
        grad_attended,
        preferred_element_type=jnp.float32,
    )
    centre = jnp.sum(softmax_rows * grad_softmax, axis=-1, keepdims=True)
    grad_scores = (softmax_rows * (grad_softmax - centre)).astype(jnp.bfloat16)
    grad_queries = (
        jnp.einsum("hqk,khe->qhe", grad_scores, key_rows, preferred_element_type=jnp.float32)
        * score_scale
    )
    grad_keys = (
        jnp.einsum("hqk,qhe->khe", grad_scores, queries, preferred_element_type=jnp.float32)
        * score_scale
    )
    return (grad_queries, grad_keys, grad_values)


def on_device(
    inputs,
    segments,
    example_of,
    patches,
    grad_out,
    gain_self,
    wq_self,
    wk_self,
    wv_self,
    wo_self,
    gain_cross,
    wq_cross,
    wk_cross,
    wv_cross,
    wo_cross,
    gain_ffn,
    w_gate,
    w_up,
    w_down,
):
    gathered = (
        lax.all_gather(gain_self, "dp", axis=0, tiled=True),
        lax.all_gather(wq_self, "dp", axis=0, tiled=True),
        lax.all_gather(wk_self, "dp", axis=0, tiled=True),
        lax.all_gather(wv_self, "dp", axis=0, tiled=True),
        lax.all_gather(wo_self, "dp", axis=1, tiled=True),
        lax.all_gather(gain_cross, "dp", axis=0, tiled=True),
        lax.all_gather(wq_cross, "dp", axis=0, tiled=True),
        lax.all_gather(wk_cross, "dp", axis=0, tiled=True),
        lax.all_gather(wv_cross, "dp", axis=0, tiled=True),
        lax.all_gather(wo_cross, "dp", axis=1, tiled=True),
        lax.all_gather(gain_ffn, "dp", axis=0, tiled=True),
        lax.all_gather(w_gate, "dp", axis=0, tiled=True),
        lax.all_gather(w_up, "dp", axis=0, tiled=True),
        lax.all_gather(w_down, "dp", axis=1, tiled=True),
    )
    gain_first = gathered[0].astype(jnp.float32)
    full_wq_self, full_wk_self, full_wv_self, full_wo_self = (
        gathered[1],
        gathered[2],
        gathered[3],
        gathered[4],
    )
    gain_second = gathered[5].astype(jnp.float32)
    full_wq_cross, full_wk_cross, full_wv_cross, full_wo_cross = (
        gathered[6],
        gathered[7],
        gathered[8],
        gathered[9],
    )
    gain_third = gathered[10].astype(jnp.float32)
    row_count, row_length = segments.shape
    token_count, feature_count = inputs.shape
    example_count, patch_count = (patches.shape[0], patches.shape[1])
    memory_count = example_count * patch_count
    slot_rows = memory_count // row_count
    heads_here = full_wq_self.shape[1] // HEAD_DIM

    def reduce_rows(partial_rows):
        return lax.psum(partial_rows, "mp")

    def split_heads(matrix):
        return matrix.reshape(row_count, -1, heads_here, HEAD_DIM)

    positions = jnp.arange(row_length, dtype=jnp.int32)
    causal = positions[:, None] >= positions[None, :]
    slot_of_key = jnp.arange(slot_rows, dtype=jnp.int32) // patch_count

    def self_allowed(seg_row):
        return (seg_row[:, None] == seg_row[None, :]) & causal

    def cross_allowed(seg_row):
        return seg_row[:, None] == slot_of_key[None, :]

    def self_forward(row_items):
        return attend_forward(row_items[0], row_items[1], row_items[2], self_allowed(row_items[3]))

    def cross_forward(row_items):
        return attend_forward(row_items[0], row_items[1], row_items[2], cross_allowed(row_items[3]))

    def self_backward(row_items):
        return attend_backward(
            row_items[0],
            row_items[1],
            row_items[2],
            self_allowed(row_items[3]),
            row_items[4],
            row_items[5],
        )

    def cross_backward(row_items):
        return attend_backward(
            row_items[0],
            row_items[1],
            row_items[2],
            cross_allowed(row_items[3]),
            row_items[4],
            row_items[5],
        )

    start_rows = inputs.astype(jnp.float32)
    normed_value, self_norm_back = jax.vjp(rms_norm, start_rows, gain_first)
    normed_self = normed_value.astype(jnp.bfloat16)
    q_self = split_heads(linear(normed_self, full_wq_self).astype(jnp.bfloat16))
    k_self = split_heads(linear(normed_self, full_wk_self).astype(jnp.bfloat16))
    v_self = split_heads(linear(normed_self, full_wv_self).astype(jnp.bfloat16))
    attended, lse_self = lax.map(self_forward, (q_self, k_self, v_self, segments))
    mixed_self = attended.reshape(token_count, -1).astype(jnp.bfloat16)
    after_self = start_rows + reduce_rows(linear(mixed_self, full_wo_self))
    normed_value, cross_norm_back = jax.vjp(rms_norm, after_self, gain_second)
    normed_cross = normed_value.astype(jnp.bfloat16)
    memory = jnp.take(patches, example_of[0], axis=0).reshape(memory_count, feature_count)
    q_cross = split_heads(linear(normed_cross, full_wq_cross).astype(jnp.bfloat16))
    k_cross = split_heads(linear(memory, full_wk_cross).astype(jnp.bfloat16))
    v_cross = split_heads(linear(memory, full_wv_cross).astype(jnp.bfloat16))
    attended, lse_cross = lax.map(cross_forward, (q_cross, k_cross, v_cross, segments))
    mixed_cross = attended.reshape(token_count, -1).astype(jnp.bfloat16)
    after_cross = after_self + reduce_rows(linear(mixed_cross, full_wo_cross))
    full_w_gate, full_w_up, full_w_down = (gathered[11], gathered[12], gathered[13])
    normed_value, ffn_norm_back = jax.vjp(rms_norm, after_cross, gain_third)
    normed_ffn = normed_value.astype(jnp.bfloat16)
    gate_values = linear(normed_ffn, full_w_gate)
    up_values = linear(normed_ffn, full_w_up)
    hidden_value, gated_back = jax.vjp(gated_unit, gate_values, up_values)
    hidden = hidden_value.astype(jnp.bfloat16)
    output = after_cross + reduce_rows(linear(hidden, full_w_down))
    grad_final = grad_out.astype(jnp.float32)
    grad_w_down = jnp.einsum("tf,td->fd", hidden, grad_out, preferred_element_type=jnp.float32)
    grad_hidden = back_rows(grad_out, full_w_down)
    grad_gate, grad_up = gated_back(grad_hidden)
    grad_gate = grad_gate.astype(jnp.bfloat16)
    grad_up = grad_up.astype(jnp.bfloat16)
    grad_w_gate = weight_term(normed_ffn, grad_gate)
    grad_w_up = weight_term(normed_ffn, grad_up)
    grad_normed = reduce_rows(back_rows(grad_gate, full_w_gate) + back_rows(grad_up, full_w_up))
    grad_rows, grad_gain_ffn = ffn_norm_back(grad_normed)
    grad_after_cross = grad_final + grad_rows
    grad_branch = grad_after_cross.astype(jnp.bfloat16)
    grad_wo_cross = weight_term(mixed_cross, grad_branch)
    grad_mixed = back_rows(grad_branch, full_wo_cross).astype(jnp.bfloat16)
    grad_q, grad_k, grad_v = lax.map(
        cross_backward, (q_cross, k_cross, v_cross, segments, lse_cross, split_heads(grad_mixed))
    )
    grad_q = grad_q.reshape(token_count, -1).astype(jnp.bfloat16)
    grad_k = grad_k.reshape(memory_count, -1).astype(jnp.bfloat16)
    grad_v = grad_v.reshape(memory_count, -1).astype(jnp.bfloat16)
    grad_wq_cross = weight_term(normed_cross, grad_q)
    grad_wk_cross = weight_term(memory, grad_k)
    grad_wv_cross = weight_term(memory, grad_v)
    grad_normed = reduce_rows(back_rows(grad_q, full_wq_cross))
    grad_memory = lax.psum(
        (back_rows(grad_k, full_wk_cross) + back_rows(grad_v, full_wv_cross)).astype(jnp.bfloat16),
        "mp",
    ).astype(jnp.float32)
    grad_patches = (
        jnp.zeros(patches.shape, jnp.float32)
        .at[example_of[0]]
        .set(grad_memory.reshape(patches.shape))
    )
    grad_rows, grad_gain_cross = cross_norm_back(grad_normed)
    grad_after_self = grad_after_cross + grad_rows
    grad_branch = grad_after_self.astype(jnp.bfloat16)
    grad_wo_self = weight_term(mixed_self, grad_branch)
    grad_mixed = back_rows(grad_branch, full_wo_self).astype(jnp.bfloat16)
    grad_q, grad_k, grad_v = lax.map(
        self_backward, (q_self, k_self, v_self, segments, lse_self, split_heads(grad_mixed))
    )
    grad_q = grad_q.reshape(token_count, -1).astype(jnp.bfloat16)
    grad_k = grad_k.reshape(token_count, -1).astype(jnp.bfloat16)
    grad_v = grad_v.reshape(token_count, -1).astype(jnp.bfloat16)
    grad_wq_self = weight_term(normed_self, grad_q)
    grad_wk_self = weight_term(normed_self, grad_k)
    grad_wv_self = weight_term(normed_self, grad_v)
    grad_normed = reduce_rows(
        back_rows(grad_q, full_wq_self)
        + back_rows(grad_k, full_wk_self)
        + back_rows(grad_v, full_wv_self)
    )
    grad_rows, grad_gain_self = self_norm_back(grad_normed)
    grad_inputs = grad_after_self + grad_rows
    summed = (
        lax.psum_scatter(grad_gain_self, "dp", scatter_dimension=0, tiled=True),
        lax.psum_scatter(grad_wq_self, "dp", scatter_dimension=0, tiled=True),
        lax.psum_scatter(grad_wk_self, "dp", scatter_dimension=0, tiled=True),
        lax.psum_scatter(grad_wv_self, "dp", scatter_dimension=0, tiled=True),
        lax.psum_scatter(grad_wo_self, "dp", scatter_dimension=1, tiled=True),
        lax.psum_scatter(grad_gain_cross, "dp", scatter_dimension=0, tiled=True),
        lax.psum_scatter(grad_wq_cross, "dp", scatter_dimension=0, tiled=True),
        lax.psum_scatter(grad_wk_cross, "dp", scatter_dimension=0, tiled=True),
        lax.psum_scatter(grad_wv_cross, "dp", scatter_dimension=0, tiled=True),
        lax.psum_scatter(grad_wo_cross, "dp", scatter_dimension=1, tiled=True),
        lax.psum_scatter(grad_gain_ffn, "dp", scatter_dimension=0, tiled=True),
        lax.psum_scatter(grad_w_gate, "dp", scatter_dimension=0, tiled=True),
        lax.psum_scatter(grad_w_up, "dp", scatter_dimension=0, tiled=True),
        lax.psum_scatter(grad_w_down, "dp", scatter_dimension=1, tiled=True),
    )
    return (
        output,
        grad_inputs,
        grad_patches,
        summed[0],
        summed[1],
        summed[2],
        summed[3],
        summed[4],
        summed[5],
        summed[6],
        summed[7],
        summed[8],
        summed[9],
        summed[10],
        summed[11],
        summed[12],
        summed[13],
    )


def solution(mesh):
    return jax.shard_map(
        on_device,
        mesh=mesh,
        in_specs=(
            P("dp", None),
            P("dp", None),
            P("dp", None),
            P("dp", None, None),
            P("dp", None),
            P("dp"),
            P("dp", "mp"),
            P("dp", "mp"),
            P("dp", "mp"),
            P("mp", "dp"),
            P("dp"),
            P("dp", "mp"),
            P("dp", "mp"),
            P("dp", "mp"),
            P("mp", "dp"),
            P("dp"),
            P("dp", "mp"),
            P("dp", "mp"),
            P("mp", "dp"),
        ),
        out_specs=(
            P("dp", None),
            P("dp", None),
            P("dp", None, None),
            P("dp"),
            P("dp", "mp"),
            P("dp", "mp"),
            P("dp", "mp"),
            P("mp", "dp"),
            P("dp"),
            P("dp", "mp"),
            P("dp", "mp"),
            P("dp", "mp"),
            P("mp", "dp"),
            P("dp"),
            P("dp", "mp"),
            P("dp", "mp"),
            P("mp", "dp"),
        ),
        check_vma=False,
    )
```

profile of v0, /device:TPU:0, one launch (start us, length us, event | category | flops | bytes accessed | tf_op | source)
XLA Modules:
  0.0 2519.9 jit_solution(11993706297733434479)
XLA Ops:
  11.2 23.3 all-gather
  37.1 26.4 %all-gather.15.cloned.1.call-done = bf16[2048,1024]{1,0:T(8,128)(2,1)} async-done(((bf16[128,1024]{1,0:T(8,128)(2,1)}), bf16[2048,1024]{1,0:T(8,128)(2,1)}) %all-gather.15.cloned.1.call-update) | async-done | bytes 4194320 | tf_op jit(solution)/shard_map/all_gather | solution.py:104
  66.8 47.9 %all-gather.17.cloned.1.call-done = bf16[2048,1024]{1,0:T(8,128)(2,1)} async-done(((bf16[128,1024]{1,0:T(8,128)(2,1)}), bf16[2048,1024]{1,0:T(8,128)(2,1)}) %all-gather.17.cloned.1.call-update) | async-done | bytes 4194320 | tf_op jit(solution)/shard_map/all_gather | solution.py:102
  117.9 48.1 %all-gather.19.cloned.1.call-done = bf16[2048,1024]{1,0:T(8,128)(2,1)} async-done(((bf16[128,1024]{1,0:T(8,128)(2,1)}), bf16[2048,1024]{1,0:T(8,128)(2,1)}) %all-gather.19.cloned.1.call-update) | async-done | bytes 4194320 | tf_op jit(solution)/shard_map/all_gather | solution.py:103
  170.1 49.7 %all-gather.21.cloned.1.call-done = bf16[1024,2048]{1,0:T(8,128)(2,1)} async-done(((bf16[1024,128]{1,0:T(8,128)(2,1)}), bf16[1024,2048]{1,0:T(8,128)(2,1)}) %all-gather.21.cloned.1.call-update) | async-done | bytes 4194320 | tf_op jit(solution)/shard_map/all_gather | solution.py:105
  225.4 18.6 all-gather.1
  244.8 25.8 %all-gather.23.cloned.1.call-done = bf16[2048,1024]{1,0:T(8,128)(2,1)} async-done(((bf16[128,1024]{1,0:T(8,128)(2,1)}), bf16[2048,1024]{1,0:T(8,128)(2,1)}) %all-gather.23.cloned.1.call-update) | async-done | bytes 4194320 | tf_op jit(solution)/shard_map/all_gather | solution.py:109
  273.6 48.0 %all-gather.27.cloned.1.call-done = bf16[2048,1024]{1,0:T(8,128)(2,1)} async-done(((bf16[128,1024]{1,0:T(8,128)(2,1)}), bf16[2048,1024]{1,0:T(8,128)(2,1)}) %all-gather.27.cloned.1.call-update) | async-done | bytes 4194320 | tf_op jit(solution)/shard_map/all_gather | solution.py:108
  324.8 38.3 %all-reduce.12.cloned.1.call-done = f32[128,2048]{1,0:T(8,128)} async-done(((f32[128,2048]{1,0:T(8,128)}), f32[128,2048]{1,0:T(8,128)}) %all-reduce.12.cloned.1.call-update) | async-done | bytes 1048592 | tf_op jit(solution)/shard_map/psum | solution.py:139
  364.5 51.7 %all-gather.25.cloned.1.call-done = bf16[2048,1024]{1,0:T(8,128)(2,1)} async-done(((bf16[128,1024]{1,0:T(8,128)(2,1)}), bf16[2048,1024]{1,0:T(8,128)(2,1)}) %all-gather.25.cloned.1.call-update) | async-done | bytes 4194320 | tf_op jit(solution)/shard_map/all_gather | solution.py:107
  422.7 47.7 %all-gather.29.cloned.1.call-done = bf16[1024,2048]{1,0:T(8,128)(2,1)} async-done(((bf16[1024,128]{1,0:T(8,128)(2,1)}), bf16[1024,2048]{1,0:T(8,128)(2,1)}) %all-gather.29.cloned.1.call-update) | async-done | bytes 4194320 | tf_op jit(solution)/shard_map/all_gather | solution.py:110
  476.4 19.0 all-gather.2
  495.5 17.2 all-reduce.14.cloned.1.call-done
  515.2 87.6 %all-gather.31.cloned.1.call-done = bf16[2048,2560]{1,0:T(8,128)(2,1)} async-done(((bf16[128,2560]{1,0:T(8,128)(2,1)}), bf16[2048,2560]{1,0:T(8,128)(2,1)}) %all-gather.31.cloned.1.call-update) | async-done | bytes 10485776 | tf_op jit(solution)/shard_map/all_gather | solution.py:112
  609.5 81.7 %all-gather.33.cloned.1.call-done = bf16[2048,2560]{1,0:T(8,128)(2,1)} async-done(((bf16[128,2560]{1,0:T(8,128)(2,1)}), bf16[2048,2560]{1,0:T(8,128)(2,1)}) %all-gather.33.cloned.1.call-update) | async-done | bytes 10485776 | tf_op jit(solution)/shard_map/all_gather | solution.py:113
  697.7 84.6 %all-gather.35.cloned.1.call-done = bf16[2560,2048]{1,0:T(8,128)(2,1)} async-done(((bf16[2560,128]{1,0:T(8,128)(2,1)}), bf16[2560,2048]{1,0:T(8,128)(2,1)}) %all-gather.35.cloned.1.call-update) | async-done | bytes 10485776 | tf_op jit(solution)/shard_map/all_gather | solution.py:114
  782.2 10.0 multiply_convert_fusion
  812.1 31.1 %all-reduce.16.cloned.1.call-done = f32[128,2048]{1,0:T(8,128)} async-done(((f32[128,2048]{1,0:T(8,128)}), f32[128,2048]{1,0:T(8,128)}) %all-reduce.16.cloned.1.call-update) | async-done | bytes 1048592 | tf_op jit(solution)/shard_map/psum | solution.py:139
  868.9 29.7 %all-reduce.18.cloned.1.call-done = f32[128,2048]{1,0:T(8,128)} async-done(((f32[128,2048]{1,0:T(8,128)}), f32[128,2048]{1,0:T(8,128)}) %all-reduce.18.cloned.1.call-update) | async-done | bytes 1048592 | tf_op jit(solution)/shard_map/psum | solution.py:139
  962.3 9.0 fusion.65
  1003.4 63.5 %all-reduce.3 = (f32[2048]{0:T(1024)S(1)}, f32[2048]{0:T(1024)S(1)}, f32[2048]{0:T(1024)S(1)}) all-reduce(f32[2048]{0:T(1024)S(1)} %get-tuple-element.113, f32[2048]{0:T(1024)S(1)} %get-tuple-element.111, f32[2048]{0:T(1024)S(1)} %get-tuple-element.109), channel_id=2, replica_groups=mesh['dp'=16,'mp'=2] {'dp'}, use_global_device_ids=true, to_apply=%region_21.22.clone | all-reduce | flops 6144 | bytes 49152
  1071.1 33.8 %reduce-scatter.20.cloned.1.call-done = f32[128,1024]{1,0:T(8,128)} async-done(((f32[2048,1024]{1,0:T(8,128)}), f32[128,1024]{1,0:T(8,128)}) %reduce-scatter.20.cloned.1.call-update) | async-done | bytes 524304 | tf_op jit(solution)/shard_map/reduce_scatter | solution.py:267
  1104.9 109.1 %reduce-scatter.22.cloned.1.call-done = f32[128,1024]{1,0:T(8,128)} async-done(((f32[2048,1024]{1,0:T(8,128)}), f32[128,1024]{1,0:T(8,128)}) %reduce-scatter.22.cloned.1.call-update) | async-done | bytes 524304 | tf_op jit(solution)/shard_map/reduce_scatter | solution.py:268
  1214.0 108.8 %reduce-scatter.24.cloned.1.call-done = f32[128,1024]{1,0:T(8,128)} async-done(((f32[2048,1024]{1,0:T(8,128)}), f32[128,1024]{1,0:T(8,128)}) %reduce-scatter.24.cloned.1.call-update) | async-done | bytes 524304 | tf_op jit(solution)/shard_map/reduce_scatter | solution.py:269
  1322.9 109.3 %reduce-scatter.26.cloned.1.call-done = f32[1024,128]{1,0:T(8,128)} async-done(((f32[1024,2048]{1,0:T(8,128)}), f32[1024,128]{1,0:T(8,128)}) %reduce-scatter.26.cloned.1.call-update) | async-done | bytes 524304 | tf_op jit(solution)/shard_map/reduce_scatter | solution.py:270
  1432.1 109.0 %reduce-scatter.12.cloned.1.call-done = f32[128,1024]{1,0:T(8,128)} async-done(((f32[2048,1024]{1,0:T(8,128)}), f32[128,1024]{1,0:T(8,128)}) %reduce-scatter.12.cloned.1.call-update) | async-done | bytes 524304 | tf_op jit(solution)/shard_map/reduce_scatter | solution.py:262
  1541.1 109.0 %reduce-scatter.14.cloned.1.call-done = f32[128,1024]{1,0:T(8,128)} async-done(((f32[2048,1024]{1,0:T(8,128)}), f32[128,1024]{1,0:T(8,128)}) %reduce-scatter.14.cloned.1.call-update) | async-done | bytes 524304 | tf_op jit(solution)/shard_map/reduce_scatter | solution.py:263
  1650.1 108.9 %reduce-scatter.16.cloned.1.call-done = f32[128,1024]{1,0:T(8,128)} async-done(((f32[2048,1024]{1,0:T(8,128)}), f32[128,1024]{1,0:T(8,128)}) %reduce-scatter.16.cloned.1.call-update) | async-done | bytes 524304 | tf_op jit(solution)/shard_map/reduce_scatter | solution.py:264
  1759.0 109.3 %reduce-scatter.18.cloned.1.call-done = f32[1024,128]{1,0:T(8,128)} async-done(((f32[1024,2048]{1,0:T(8,128)}), f32[1024,128]{1,0:T(8,128)}) %reduce-scatter.18.cloned.1.call-update) | async-done | bytes 524304 | tf_op jit(solution)/shard_map/reduce_scatter | solution.py:265
  1868.3 215.2 %reduce-scatter.28.cloned.1.call-done = f32[128,2560]{1,0:T(8,128)} async-done(((f32[2048,2560]{1,0:T(8,128)}), f32[128,2560]{1,0:T(8,128)}) %reduce-scatter.28.cloned.1.call-update) | async-done | bytes 1310736 | tf_op jit(solution)/shard_map/reduce_scatter | solution.py:272
  2083.4 214.5 %reduce-scatter.30.cloned.1.call-done = f32[128,2560]{1,0:T(8,128)} async-done(((f32[2048,2560]{1,0:T(8,128)}), f32[128,2560]{1,0:T(8,128)}) %reduce-scatter.30.cloned.1.call-update) | async-done | bytes 1310736 | tf_op jit(solution)/shard_map/reduce_scatter | solution.py:273
  2297.9 214.7 %reduce-scatter.32.cloned.1.call-done = f32[2560,128]{1,0:T(8,128)} async-done(((f32[2560,2048]{1,0:T(8,128)}), f32[2560,128]{1,0:T(8,128)}) %reduce-scatter.32.cloned.1.call-update) | async-done | bytes 1310736 | tf_op jit(solution)/shard_map/reduce_scatter | solution.py:274
  (273 shorter events, 203.0 us)
Async XLA Ops:
  7.2 236.8 %copy-start = (bf16[2,64,2048]{2,1,0:T(8,128)(2,1)S(1)}, bf16[2,64,2048]{2,1,0:T(8,128)(2,1)}, u32[]{:S(2)}) copy-start(bf16[2,64,2048]{2,1,0:T(8,128)(2,1)} %param.22) | copy-start | bytes 1572868
  7.2 107.6 %copy-start.2 = (bf16[128,2048]{1,0:T(8,128)(2,1)S(1)}, bf16[128,2048]{1,0:T(8,128)(2,1)}, u32[]{:S(2)}) copy-start(bf16[128,2048]{1,0:T(8,128)(2,1)} %param.19) | copy-start | bytes 1572868
  7.2 56.3 %all-gather.15.cloned.1.call-start = ((), (), s32[]{:S(2)}) async-start(), calls=%async_computation.11 | async-start | bytes 4456448 | tf_op jit(solution)/shard_map/all_gather | solution.py:104
  8.0 106.8 %all-gather.17.cloned.1.call-start = ((), (), s32[]{:S(2)}) async-start(), calls=%async_computation.12 | async-start | bytes 4456448 | tf_op jit(solution)/shard_map/all_gather | solution.py:102
  8.7 157.3 %all-gather.19.cloned.1.call-start = ((), (), s32[]{:S(2)}) async-start(), calls=%async_computation.13 | async-start | bytes 4456448 | tf_op jit(solution)/shard_map/all_gather | solution.py:103
  9.4 210.3 %all-gather.21.cloned.1.call-start = ((), (), s32[]{:S(2)}) async-start(), calls=%async_computation.14 | async-start | bytes 4456448 | tf_op jit(solution)/shard_map/all_gather | solution.py:105
  10.0 260.5 %all-gather.23.cloned.1.call-start = ((), (), s32[]{:S(2)}) async-start(), calls=%async_computation.16 | async-start | bytes 4456448 | tf_op jit(solution)/shard_map/all_gather | solution.py:109
  10.6 311.1 %all-gather.27.cloned.1.call-start = ((), (), s32[]{:S(2)}) async-start(), calls=%async_computation.18 | async-start | bytes 4456448 | tf_op jit(solution)/shard_map/all_gather | solution.py:108
  11.2 351.9 %all-reduce.12.cloned.1.call-start = ((), (), s32[]{:S(2)}) async-start(), calls=%async_computation.15 | async-start | bytes 2097152 | tf_op jit(solution)/shard_map/psum | solution.py:139
  223.7 192.5 %all-gather.25.cloned.1.call-start = ((), (), s32[]{:S(2)}) async-start(), calls=%async_computation.17 | async-start | bytes 4456448 | tf_op jit(solution)/shard_map/all_gather | solution.py:107
  224.5 245.9 %all-gather.29.cloned.1.call-start = ((), (), s32[]{:S(2)}) async-start(), calls=%async_computation.19 | async-start | bytes 4456448 | tf_op jit(solution)/shard_map/all_gather | solution.py:110
  225.2 287.5 %all-reduce.14.cloned.1.call-start = ((), (), s32[]{:S(2)}) async-start(), calls=%async_computation.20 | async-start | bytes 2097152 | tf_op jit(solution)/shard_map/psum | solution.py:139
  273.6 147.9 %copy-start.50 = (bf16[128,1024]{0,1:T(8,128)(2,1)}, bf16[128,1024]{0,1:T(8,128)(2,1)S(1)}, u32[]{:S(2)}) copy-start(bf16[128,1024]{0,1:T(8,128)(2,1)S(1)} %copy.80) | copy-start | bytes 786436
  474.3 128.6 %all-gather.31.cloned.1.call-start = ((), (), s32[]{:S(2)}) async-start(), calls=%async_computation.21 | async-start | bytes 11141120 | tf_op jit(solution)/shard_map/all_gather | solution.py:112
  475.0 216.1 %all-gather.33.cloned.1.call-start = ((), (), s32[]{:S(2)}) async-start(), calls=%async_computation.22 | async-start | bytes 11141120 | tf_op jit(solution)/shard_map/all_gather | solution.py:113
  475.6 306.6 %all-gather.35.cloned.1.call-start = ((), (), s32[]{:S(2)}) async-start(), calls=%async_computation.23 | async-start | bytes 11141120 | tf_op jit(solution)/shard_map/all_gather | solution.py:114
  476.4 366.8 %all-reduce.16.cloned.1.call-start = ((), (), s32[]{:S(2)}) async-start(), calls=%async_computation.24 | async-start | bytes 2097152 | tf_op jit(solution)/shard_map/psum | solution.py:139
  804.8 93.8 %all-reduce.18.cloned.1.call-start = ((), (), s32[]{:S(2)}) async-start(), calls=%async_computation.25 | async-start | bytes 2097152 | tf_op jit(solution)/shard_map/psum | solution.py:139
  858.4 134.6 %all-reduce.20.cloned.1.call-start = ((), (), s32[]{:S(2)}) async-start(), calls=%async_computation.26 | async-start | bytes 1048576 | tf_op jit(solution)/shard_map/psum | solution.py:230
  868.6 130.7 %all-reduce.22.cloned.1.call-start = ((), (), s32[]{:S(2)}) async-start(), calls=%async_computation.38 | async-start | bytes 4194304 | tf_op jit(solution)/shard_map/psum | solution.py:139
  916.7 188.2 %reduce-scatter.20.cloned.1.call-start = ((), (), s32[]{:S(2)}) async-start(), calls=%async_computation.31 | async-start | bytes 8912896 | tf_op jit(solution)/shard_map/reduce_scatter | solution.py:267
  921.4 292.6 %reduce-scatter.22.cloned.1.call-start = ((), (), s32[]{:S(2)}) async-start(), calls=%async_computation.32 | async-start | bytes 8912896 | tf_op jit(solution)/shard_map/reduce_scatter | solution.py:268
  927.3 395.6 %reduce-scatter.24.cloned.1.call-start = ((), (), s32[]{:S(2)}) async-start(), calls=%async_computation.33 | async-start | bytes 8912896 | tf_op jit(solution)/shard_map/reduce_scatter | solution.py:269
  932.8 499.4 %reduce-scatter.26.cloned.1.call-start = ((), (), s32[]{:S(2)}) async-start(), calls=%async_computation.34 | async-start | bytes 8912896 | tf_op jit(solution)/shard_map/reduce_scatter | solution.py:270
  938.8 602.4 %reduce-scatter.12.cloned.1.call-start = ((), (), s32[]{:S(2)}) async-start(), calls=%async_computation.27 | async-start | bytes 8912896 | tf_op jit(solution)/shard_map/reduce_scatter | solution.py:262
  944.4 705.7 %reduce-scatter.14.cloned.1.call-start = ((), (), s32[]{:S(2)}) async-start(), calls=%async_computation.28 | async-start | bytes 8912896 | tf_op jit(solution)/shard_map/reduce_scatter | solution.py:263
  950.0 809.0 %reduce-scatter.16.cloned.1.call-start = ((), (), s32[]{:S(2)}) async-start(), calls=%async_computation.29 | async-start | bytes 8912896 | tf_op jit(solution)/shard_map/reduce_scatter | solution.py:264
  955.5 912.7 %reduce-scatter.18.cloned.1.call-start = ((), (), s32[]{:S(2)}) async-start(), calls=%async_computation.30 | async-start | bytes 8912896 | tf_op jit(solution)/shard_map/reduce_scatter | solution.py:265
  961.3 1122.1 %reduce-scatter.28.cloned.1.call-start = ((), (), s32[]{:S(2)}) async-start(), calls=%async_computation.35 | async-start | bytes 22282240 | tf_op jit(solution)/shard_map/reduce_scatter | solution.py:272
  971.4 1326.5 %reduce-scatter.30.cloned.1.call-start = ((), (), s32[]{:S(2)}) async-start(), calls=%async_computation.36 | async-start | bytes 22282240 | tf_op jit(solution)/shard_map/reduce_scatter | solution.py:273
  981.3 1531.4 %reduce-scatter.32.cloned.1.call-start = ((), (), s32[]{:S(2)}) async-start(), calls=%async_computation.37 | async-start | bytes 22282240 | tf_op jit(solution)/shard_map/reduce_scatter | solution.py:274
  999.4 1513.3 %copy-start.1 = (bf16[2,64,2048]{2,1,0:T(8,128)(2,1)S(1)}, bf16[2,64,2048]{2,1,0:T(8,128)(2,1)}, u32[]{:S(2)}) copy-start(bf16[2,64,2048]{2,1,0:T(8,128)(2,1)} %param.22) | copy-start | bytes 1572868
  (56 other events, 900.6 us)
Sparse Core Ops, SparseCore 0:
  10.2 53.2 all-gather.14
  65.7 49.0 all-gather.16
  116.9 49.0 all-gather.18
  168.0 51.7 all-gather.20
  221.8 48.7 all-gather.22
  272.6 49.0 all-gather.26
  324.5 38.5 all-reduce.11
  365.5 50.7 all-gather.24
  418.6 51.7 all-gather.28
  474.4 38.2 all-reduce.13
  515.0 87.8 all-gather.30
  605.0 86.0 all-gather.32
  693.3 88.9 all-gather.34
  804.9 38.2 all-reduce.15
  858.5 40.0 all-reduce.17
  900.8 28.5 all-reduce.19
  932.3 63.0 all-reduce.21
  999.9 104.9 reduce-scatter.19
  1109.6 104.4 reduce-scatter.21
  1218.5 104.3 reduce-scatter.23
  1327.5 104.5 reduce-scatter.25
  1436.8 104.3 reduce-scatter.11
  1545.8 104.3 reduce-scatter.13
  1654.6 104.3 reduce-scatter.15
  1763.6 104.5 reduce-scatter.17
  1872.8 210.5 reduce-scatter.27
  2088.0 209.9 reduce-scatter.29
  2302.6 209.9 reduce-scatter.31
where the time goes:
time: 2530 us; the launch traced here: 2520 us
  waiting for transfers between devices  2160 us (85%)
  matrix products  161 us (6%)
  blocking collectives  124 us (5%)
  local copies, waits for them, and re-layouts  28.7 us (1%)
    reduce_scatter x1, waiting for transfers between devices, on_device(): lax.psum_scatter(grad_w_gate, 'dp', scatter_dimension=0, tiled=True)  215 us
    reduce_scatter x1, waiting for transfers between devices, on_device(): lax.psum_scatter(grad_w_down, 'dp', scatter_dimension=1, tiled=True)  215 us
    reduce_scatter x1, waiting for transfers between devices, on_device(): lax.psum_scatter(grad_w_up, 'dp', scatter_dimension=0, tiled=True)  215 us
    psum x5, waiting for transfers between devices, reduce_rows(): return lax.psum(partial_rows, 'mp')  116 us
    reduce_scatter x1, waiting for transfers between devices, on_device(): lax.psum_scatter(grad_wo_cross, 'dp', scatter_dimension=1, tiled=True)  109 us
    reduce_scatter x1, waiting for transfers between devices, on_device(): lax.psum_scatter(grad_wo_self, 'dp', scatter_dimension=1, tiled=True)  109 us
    reduce_scatter x1, waiting for transfers between devices, on_device(): lax.psum_scatter(grad_wk_cross, 'dp', scatter_dimension=0, tiled=True)  109 us
    reduce_scatter x1, waiting for transfers between devices, on_device(): lax.psum_scatter(grad_wk_self, 'dp', scatter_dimension=0, tiled=True)  109 us
  transfers between devices with their start and end apart: 28, of which 26 were waited for; matrix products, arithmetic and copies ran while one was open for 6% of the time, Pallas kernels for 0%

commit v1 on v0

v1 whole, which is shorter than its diff:
```python
import functools

import jax
import jax.numpy as jnp
from jax import lax
from jax.experimental import pallas as pl
from jax.experimental.pallas import tpu as pltpu
from jax.sharding import PartitionSpec as P

HEAD_DIM = 64
INNER = 4
EPS = 1e-06
NEG = -1e30
BF = jnp.bfloat16
F32 = jnp.float32


def dot(a, b, da, db):
    return lax.dot_general(a, b, (((da,), (db,)), ((), ())), preferred_element_type=F32)


def mask_of(qid_ref, kid_ref, causal):
    allowed = qid_ref[...] == kid_ref[...]
    if causal:
        rows = lax.broadcasted_iota(jnp.int32, allowed.shape, 0)
        cols = lax.broadcasted_iota(jnp.int32, allowed.shape, 1)
        allowed = allowed & (rows >= cols)
    return allowed


def soft(q, k, allowed):
    scores = jnp.where(allowed, dot(q, k, 1, 1) * HEAD_DIM ** (-0.5), NEG)
    raised = jnp.exp(scores - jnp.max(scores, axis=-1, keepdims=True))
    return raised / jnp.sum(raised, axis=-1, keepdims=True)


def attend_kernel(causal, qid_ref, kid_ref, q_ref, k_ref, v_ref, out_ref):
    allowed = mask_of(qid_ref, kid_ref, causal)
    pieces = []
    for first in range(0, q_ref.shape[1], HEAD_DIM):
        cut = slice(first, first + HEAD_DIM)
        probs = soft(q_ref[:, cut], k_ref[:, cut], allowed).astype(BF)
        pieces.append(dot(probs, v_ref[:, cut], 1, 0).astype(BF))
    out_ref[...] = jnp.concatenate(pieces, axis=1)


def attend_back_kernel(causal, qid_ref, kid_ref, q_ref, k_ref, v_ref, g_ref, dq_ref, dkv_ref):
    allowed = mask_of(qid_ref, kid_ref, causal)
    scale = HEAD_DIM ** (-0.5)
    dqs, dks, dvs = [], [], []
    for first in range(0, q_ref.shape[1], HEAD_DIM):
        cut = slice(first, first + HEAD_DIM)
        q, k, v, g = q_ref[:, cut], k_ref[:, cut], v_ref[:, cut], g_ref[:, cut]
        probs = soft(q, k, allowed)
        grad_probs = dot(g, v, 1, 1)
        dvs.append(dot(probs.astype(BF), g, 0, 0).astype(BF))
        centre = jnp.sum(probs * grad_probs, axis=-1, keepdims=True)
        ds = (probs * (grad_probs - centre)).astype(BF)
        dqs.append((dot(ds, k, 1, 0) * scale).astype(BF))
        dks.append((dot(ds, q, 0, 0) * scale).astype(BF))
    dq_ref[...] = jnp.concatenate(dqs, axis=1)
    dkv_ref[...] = jnp.concatenate(dks + dvs, axis=1)


def id_specs(length, keys):
    return [
        pl.BlockSpec((None, length, 1), lambda r: (r, 0, 0)),
        pl.BlockSpec((None, 1, keys), lambda r: (r, 0, 0)),
    ]


def attend(causal, qid, kid, q, k, v):
    rows, length, _ = qid.shape
    keys = kid.shape[2]
    width = q[2]
    specs = [
        pl.BlockSpec((n, width), functools.partial(lambda c, r: (r, c), col))
        for n, col in ((length, q[1]), (keys, k[1]), (keys, v[1]))
    ]
    return pl.pallas_call(
        functools.partial(attend_kernel, causal),
        grid=(rows,),
        in_specs=id_specs(length, keys) + specs,
        out_specs=pl.BlockSpec((length, width), lambda r: (r, 0)),
        out_shape=jax.ShapeDtypeStruct((rows * length, width), BF),
        cost_estimate=pl.CostEstimate(
            flops=4 * rows * length * keys * width,
            transcendentals=rows * length * keys * width // HEAD_DIM,
            bytes_accessed=8 * rows * length * width,
        ),
    )(qid, kid, q[0], k[0], v[0])


def attend_back(causal, qid, kid, q, k, v, g):
    rows, length, _ = qid.shape
    keys = kid.shape[2]
    width = q[2]
    specs = [
        pl.BlockSpec((n, width), functools.partial(lambda c, r: (r, c), col))
        for n, col in ((length, q[1]), (keys, k[1]), (keys, v[1]), (length, 0))
    ]
    return pl.pallas_call(
        functools.partial(attend_back_kernel, causal),
        grid=(rows,),
        in_specs=id_specs(length, keys) + specs,
        out_specs=[
            pl.BlockSpec((length, width), lambda r: (r, 0)),
            pl.BlockSpec((keys, 2 * width), lambda r: (r, 0)),
        ],
        out_shape=[
            jax.ShapeDtypeStruct((rows * length, width), BF),
            jax.ShapeDtypeStruct((rows * keys, 2 * width), BF),
        ],
        cost_estimate=pl.CostEstimate(
            flops=10 * rows * length * keys * width,
            transcendentals=rows * length * keys * width // HEAD_DIM,
            bytes_accessed=14 * rows * length * width,
        ),
    )(qid, kid, q[0], k[0], v[0], g)


def rms(values, gain):
    scale = lax.rsqrt(jnp.mean(values * values, axis=-1, keepdims=True) + EPS)
    return (values * scale * gain).astype(BF), scale


def rms_back(values, scale, gain, grad):
    weighted = grad * gain
    mean = jnp.mean(weighted * values, axis=-1, keepdims=True)
    return (
        scale * weighted - values * (scale * scale * scale) * mean,
        jnp.sum(grad * values * scale, axis=0, keepdims=True),
    )


def gelu_parts(gate):
    c = (2.0 / jnp.pi) ** 0.5
    inner = jnp.tanh(c * (gate + 0.044715 * gate * gate * gate))
    value = 0.5 * gate * (1.0 + inner)
    slope = 0.5 * (1.0 + inner) + 0.5 * gate * (1.0 - inner * inner) * c * (
        1.0 + 3 * 0.044715 * gate * gate
    )
    return value, slope


def on_device(
    inputs,
    segments,
    example_of,
    patches,
    grad_out,
    gain_self,
    wq_self,
    wk_self,
    wv_self,
    wo_self,
    gain_cross,
    wq_cross,
    wk_cross,
    wv_cross,
    wo_cross,
    gain_ffn,
    w_gate,
    w_up,
    w_down,
):
    dp = lax.axis_size("dp")
    outer = dp // INNER
    place = lax.axis_index("dp")
    mine, plane = place % INNER, place // INNER
    odd, far = (mine & 1) == 1, (mine & 2) == 2
    tokens, width = inputs.shape
    part = width // dp
    block = INNER * part

    def swap(value, bit):
        return lax.ppermute(value, "dp", [(i, i ^ bit) for i in range(dp)])

    def swap_mp(value):
        return lax.ppermute(value, "mp", [(0, 1), (1, 0)])

    sent = []

    def hop(value):
        if len(sent) >= 2:
            value, _ = lax.optimization_barrier((value, sent[-2]))
        sent.append(lax.ppermute(value, "dp", [(i, (i + INNER) % dp) for i in range(dp)]))
        return sent[-1]

    def small_hop(value):
        return lax.ppermute(value, "dp", [(i, (i + INNER) % dp) for i in range(dp)])

    def natural(p0, p1, p2, p3):
        a0, a1 = jnp.where(odd, p1, p0), jnp.where(odd, p0, p1)
        a2, a3 = jnp.where(odd, p3, p2), jnp.where(odd, p2, p3)
        return (
            jnp.where(far, a2, a0),
            jnp.where(far, a3, a1),
            jnp.where(far, a0, a2),
            jnp.where(far, a1, a3),
        )

    def exchange(blocks):
        to = [lax.dynamic_index_in_dim(blocks, mine ^ j, 0, keepdims=False) for j in range(INNER)]
        first = swap(jnp.stack([to[2], to[3]]), 2)
        second = swap(jnp.stack([to[1], first[1]]), 1)
        return natural(to[0], second[0], first[0], second[1])

    def rows_of(value):
        away = swap(value, 2)
        near = swap(jnp.stack([value, away]), 1)
        return jnp.concatenate([value, near[0], away, near[1]], axis=0)

    def reduce_rows(partial):
        parts = partial.reshape(INNER, -1, partial.shape[1])
        near = swap(jnp.stack([parts[1], parts[3]]).astype(BF), 1).astype(F32)
        away = swap((parts[2] + near[1]).astype(BF), 2).astype(F32)
        total = (parts[0] + near[0] + away).astype(BF)
        return total.astype(F32) + swap_mp(total).astype(F32)

    def pack(weights):
        return jnp.stack(
            [
                jnp.concatenate(
                    [
                        w[:, i * (w.shape[1] // INNER) : (i + 1) * (w.shape[1] // INNER)]
                        for w in weights
                    ],
                    axis=1,
                )
                for i in range(INNER)
            ]
        )

    def gather_weights(weights):
        pieces = exchange(pack(weights))
        halves = [
            jnp.concatenate(pieces[:2], axis=0),
            jnp.concatenate(pieces[2:], axis=0),
        ]
        full = jnp.zeros((outer, 2, block // 2, halves[0].shape[1]), BF)
        held = halves
        for step in range(outer):
            if step:
                held = [hop(h) for h in held]
            where = (plane - step) % outer
            for i in range(2):
                full = lax.dynamic_update_slice(full, held[i][None, None], (where, i, 0, 0))
        return full.reshape(width, -1)

    def scatter_weights(partials):
        views = [p.reshape(outer, 2, block // 2, p.shape[1]) for p in partials]

        def own(step, i):
            where = (plane - 1 - step) % outer
            return jnp.concatenate(
                [
                    lax.dynamic_slice(v, (where, i, 0, 0), (1, 1) + v.shape[2:])[0, 0]
                    for v in views
                ],
                axis=1,
            )

        held = [own(0, 0), own(0, 1)]
        for step in range(1, outer):
            held = [hop(h) for h in held]
            held = [(held[i].astype(F32) + own(step, i).astype(F32)).astype(BF) for i in range(2)]
        pieces = exchange(jnp.concatenate(held, axis=0).reshape(INNER, part, -1))
        out, at = [], 0
        for p in partials:
            cut = slice(at, at + p.shape[1])
            out.append(jnp.concatenate([x[:, cut] for x in pieces], axis=1).astype(F32))
            at += p.shape[1]
        return out

    gains = jnp.stack([gain_self, gain_cross, gain_ffn]).astype(F32)
    away = swap(gains, 2)
    near = swap(jnp.stack([gains, away]), 1)
    held = jnp.concatenate(natural(gains, near[0], away, near[1]), axis=1)
    all_gains = jnp.zeros((outer, 3, block), F32)
    for step in range(outer):
        if step:
            held = small_hop(held)
        all_gains = lax.dynamic_update_slice(
            all_gains, held[None], ((plane - step) % outer, 0, 0)
        )
    gain_first, gain_second, gain_third = (all_gains[:, i].reshape(1, width) for i in range(3))

    row_count, length = segments.shape
    examples, patch_count, _ = patches.shape
    slot = jnp.take_along_axis(example_of, segments, axis=1)
    ids = rows_of(jnp.concatenate([segments, slot], axis=0))
    ids = ids.reshape(INNER, 2, row_count * length)
    seg_rows = ids[:, 0].reshape(INNER * row_count, length)
    slot_rows = ids[:, 1].reshape(INNER * row_count, length)
    key_slots = jnp.broadcast_to(
        (jnp.arange(examples * patch_count // row_count, dtype=jnp.int32) // patch_count),
        (INNER * row_count, 1, examples * patch_count // row_count),
    )
    self_ids = (seg_rows[:, :, None], seg_rows[:, None, :])
    cross_ids = (slot_rows[:, :, None], key_slots)

    w_self = gather_weights([wq_self, wk_self, wv_self, wo_self.T])
    w_cross = gather_weights([wq_cross, wk_cross, wv_cross, wo_cross.T])
    w_gu = gather_weights([w_gate, w_up])
    w_dn = gather_weights([w_down.T])
    hw = w_self.shape[1] // 4
    fw = w_dn.shape[1]

    start = inputs.astype(F32)
    normed, scale_self = rms(start, gain_first)
    normed_self = rows_of(normed)
    memory = rows_of(patches.reshape(-1, width))
    qkv = dot(normed_self, w_self[:, : 3 * hw], 1, 0).astype(BF)
    self_args = ((qkv, 0, hw), (qkv, 1, hw), (qkv, 2, hw))
    mixed_self = attend(True, *self_ids, *self_args)
    after_self = start + reduce_rows(dot(mixed_self, w_self[:, 3 * hw :], 1, 1))
    normed, scale_cross = rms(after_self, gain_second)
    normed_cross = rows_of(normed)
    kv = dot(memory, w_cross[:, hw : 3 * hw], 1, 0).astype(BF)
    q = dot(normed_cross, w_cross[:, :hw], 1, 0).astype(BF)
    cross_args = ((q, 0, hw), (kv, 0, hw), (kv, 1, hw))
    mixed_cross = attend(False, *cross_ids, *cross_args)
    after_cross = after_self + reduce_rows(dot(mixed_cross, w_cross[:, 3 * hw :], 1, 1))
    normed, scale_ffn = rms(after_cross, gain_third)
    normed_ffn = rows_of(normed)
    gu = dot(normed_ffn, w_gu, 1, 0)
    gate, up = gu[:, :fw], gu[:, fw:]
    value, slope = gelu_parts(gate)
    hidden = (value * up).astype(BF)
    output = after_cross + reduce_rows(dot(hidden, w_dn, 1, 1))

    grad_rows = rows_of(grad_out)
    term_down = dot(grad_rows, hidden, 0, 0).astype(BF)
    grad_hidden = dot(grad_rows, w_dn, 1, 0)
    grad_gu = jnp.concatenate(
        [(grad_hidden * up * slope).astype(BF), (grad_hidden * value).astype(BF)], axis=1
    )
    (grad_w_down,) = scatter_weights([term_down])
    term_gu = dot(normed_ffn, grad_gu, 0, 0).astype(BF)
    grad_w_gate, grad_w_up = scatter_weights([term_gu[:, :fw], term_gu[:, fw:]])
    grad, gain_grad_ffn = rms_back(
        after_cross, scale_ffn, gain_third, reduce_rows(dot(grad_gu, w_gu, 1, 1))
    )
    grad_after_cross = grad_out.astype(F32) + grad
    branch = rows_of(grad_after_cross.astype(BF))
    term_o = dot(branch, mixed_cross, 0, 0).astype(BF)
    grad_mixed = dot(branch, w_cross[:, 3 * hw :], 1, 0).astype(BF)
    grad_q, grad_kv = attend_back(False, *cross_ids, *cross_args, grad_mixed)
    term_q = dot(normed_cross, grad_q, 0, 0).astype(BF)
    term_kv = dot(memory, grad_kv, 0, 0).astype(BF)
    grad_normed = reduce_rows(dot(grad_q, w_cross[:, :hw], 1, 1))
    grad_wq_cross, grad_wk_cross, grad_wv_cross, grad_wo_cross = scatter_weights(
        [term_q, term_kv[:, :hw], term_kv[:, hw:], term_o]
    )
    grad_memory = reduce_rows(dot(grad_kv, w_cross[:, hw : 3 * hw], 1, 1))
    grad_patches = grad_memory.reshape(patches.shape)
    grad, gain_grad_cross = rms_back(after_self, scale_cross, gain_second, grad_normed)
    grad_after_self = grad_after_cross + grad
    branch = rows_of(grad_after_self.astype(BF))
    term_o = dot(branch, mixed_self, 0, 0).astype(BF)
    grad_mixed = dot(branch, w_self[:, 3 * hw :], 1, 0).astype(BF)
    grad_q, grad_kv = attend_back(True, *self_ids, *self_args, grad_mixed)
    grad_qkv = jnp.concatenate([grad_q, grad_kv], axis=1)
    term_qkv = dot(normed_self, grad_qkv, 0, 0).astype(BF)
    grad_wq_self, grad_wk_self, grad_wv_self, grad_wo_self = scatter_weights(
        [term_qkv[:, :hw], term_qkv[:, hw : 2 * hw], term_qkv[:, 2 * hw :], term_o]
    )
    grad_normed = reduce_rows(dot(grad_qkv, w_self[:, : 3 * hw], 1, 1))
    grad, gain_grad_self = rms_back(start, scale_self, gain_first, grad_normed)
    grad_inputs = grad_after_self + grad

    gain_grads = jnp.concatenate([gain_grad_self, gain_grad_cross, gain_grad_ffn], axis=0)
    gain_grads = gain_grads + swap(gain_grads, 2)
    gain_grads = gain_grads + swap(gain_grads, 1)

    def gain_block(step):
        return lax.dynamic_slice_in_dim(
            gain_grads, ((plane - 1 - step) % outer) * block, block, axis=1
        )

    held = gain_block(0)
    for step in range(1, outer):
        held = small_hop(held) + gain_block(step)
    held = lax.dynamic_slice_in_dim(held, mine * part, part, axis=1)

    return (
        output,
        grad_inputs,
        grad_patches,
        held[0],
        grad_wq_self,
        grad_wk_self,
        grad_wv_self,
        grad_wo_self.T,
        held[1],
        grad_wq_cross,
        grad_wk_cross,
        grad_wv_cross,
        grad_wo_cross.T,
        held[2],
        grad_w_gate,
        grad_w_up,
        grad_w_down.T,
    )


def solution(mesh):
    rows, cut, turned, gain = P("dp", None), P("dp", "mp"), P("mp", "dp"), P("dp")
    attention = (gain, cut, cut, cut, turned)
    weights = attention + attention + (gain, cut, cut, turned)
    return jax.shard_map(
        on_device,
        mesh=mesh,
        in_specs=(rows, rows, rows, P("dp", None, None), rows) + weights,
        out_specs=(rows, rows, P("dp", None, None)) + weights,
        check_vma=False,
    )
```

time: 2530 us -> 831 us (0.33)
  waiting for transfers between devices: 2160 us -> 561 us
  blocking collectives: 124 us -> 0 us
  matrix products: 161 us -> 47.4 us
  starting transfers between devices: 1.76 us -> 57.3 us
  other arithmetic: 23.5 us -> 63.6 us
  Pallas kernels: 0 us -> 34.6 us
    reduce_scatter x11 -> x0, waiting for transfers between devices: 1440 us -> none  [the longest x1 215 us: on_device(): lax.psum_scatter(grad_w_gate, 'dp', scatter_dimension=0, tiled=True)]
    all_gather x11 -> x0, waiting for transfers between devices: 599 us -> none  [the longest x1 87.6 us: on_device(): lax.all_gather(w_gate, 'dp', axis=0, tiled=True)]
    ppermute x0 -> x111, waiting for transfers between devices: none -> 561 us  [the longest x48 422 us: hop(): lax.ppermute(value, 'dp', [(i, (i + INNER) % dp) for i in range(dp)])]
    psum x6 -> x0, waiting for transfers between devices: 116 us -> none  [the longest x5 116 us: reduce_rows(): return lax.psum(partial_rows, 'mp')]
    dot_general x45 -> x21, matrix products: 161 us -> 47.4 us  [dot(): lax.dot_general(a, b, (((da,), (db,)), ((), ())), preferred_element_type=...]
    unnamed x1 -> x0, blocking collectives: 63.5 us -> none
    all_gather x3 -> x0, blocking collectives: 60.9 us -> none  [the longest x1 23.3 us: on_device(): lax.all_gather(gain_self, 'dp', axis=0, tiled=True)]
    ppermute x0 -> x111, starting transfers between devices: none -> 57.3 us  [the longest x50 36.7 us: swap(): return lax.ppermute(value, 'dp', [(i, i ^ bit) for i in range(dp)])]
  transfers between devices with their start and end apart: 28 -> 111, of which waited for: 26 -> 66; matrix products, arithmetic and copies ran while one was open for 6% -> 15% of each run, Pallas kernels for 0% -> 3%
where the time goes in v1:
time: 831 us; the launch traced here: 820 us
  waiting for transfers between devices  561 us (68%)
  other arithmetic  63.6 us (8%)
  starting transfers between devices  57.3 us (7%)
  local copies, waits for them, and re-layouts  52 us (6%)
  matrix products  47.4 us (6%)
  Pallas kernels  34.6 us (4%)
    ppermute x48, waiting for transfers between devices, hop(): lax.ppermute(value, 'dp', [(i, (i + INNER) % dp) for i in range(dp)])  422 us
    ppermute x50, waiting for transfers between devices, swap(): return lax.ppermute(value, 'dp', [(i, i ^ bit) for i in range(dp)])  101 us
    dot_general x21, matrix products, dot(): lax.dot_general(a, b, (((da,), (db,)), ((), ())), preferred_element_type=...  47.4 us
    ppermute x50, starting transfers between devices, swap(): return lax.ppermute(value, 'dp', [(i, i ^ bit) for i in range(dp)])  36.7 us
    ppermute x6, waiting for transfers between devices, small_hop(): return lax.ppermute(value, 'dp', [(i, (i + INNER) % dp) for i in range(dp)])  28.2 us
    pallas_call x2, Pallas kernels, attend_back(): pl.pallas_call(functools.partial(attend_back_kernel, causal), grid=(rows,...  18.8 us
    unnamed x213, local copies, waits for them, and re-layouts  17.7 us
  transfers between devices with their start and end apart: 111, of which 66 were waited for; matrix products, arithmetic and copies ran while one was open for 15% of the time, Pallas kernels for 3%

profile of v1, /device:TPU:0, one launch (start us, length us, event | category | flops | bytes accessed | tf_op | source)
XLA Modules:
  0.0 820.5 jit_solution(6400106138736167807)
XLA Ops:
  73.0 16.4 %collective-permute-done.7 = bf16[128,2048]{1,0:T(8,128)(2,1)S(1)} collective-permute-done((bf16[128,2048]{1,0:T(8,128)(2,1)S(1)}, bf16[128,2048]{1,0:T(8,128)(2,1)S(1)}, u32[]{:S(2)}, u32[]{:S(2)}) %collective-permute-start.7) | collective-permute-done | bytes 524320 | tf_op jit(solution)/shard_map/ppermute | solution.py:177
  100.2 11.7 %collective-permute-done.11 = bf16[256,1024]{1,0:T(8,128)(2,1)S(1)} collective-permute-done((bf16[256,1024]{1,0:T(8,128)(2,1)S(1)}, bf16[256,1024]{1,0:T(8,128)(2,1)S(1)}, u32[]{:S(2)}, u32[]{:S(2)}) %collective-permute-start.11) | collective-permute-done | bytes 524320 | tf_op jit(solution)/shard_map/ppermute | solution.py:187
  112.7 10.4 %collective-permute-done.12 = bf16[256,1024]{1,0:T(8,128)(2,1)S(1)} collective-permute-done((bf16[256,1024]{1,0:T(8,128)(2,1)S(1)}, bf16[256,1024]{1,0:T(8,128)(2,1)S(1)}, u32[]{:S(2)}, u32[]{:S(2)}) %collective-permute-start.12) | collective-permute-done | bytes 524320 | tf_op jit(solution)/shard_map/ppermute | solution.py:187
  123.3 11.1 %collective-permute-done.13 = bf16[256,1024]{1,0:T(8,128)(2,1)S(1)} collective-permute-done((bf16[256,1024]{1,0:T(8,128)(2,1)S(1)}, bf16[256,1024]{1,0:T(8,128)(2,1)S(1)}, u32[]{:S(2)}, u32[]{:S(2)}) %collective-permute-start.13) | collective-permute-done | bytes 524320 | tf_op jit(solution)/shard_map/ppermute | solution.py:187
  134.6 11.0 %collective-permute-done.14 = bf16[256,1024]{1,0:T(8,128)(2,1)S(1)} collective-permute-done((bf16[256,1024]{1,0:T(8,128)(2,1)S(1)}, bf16[256,1024]{1,0:T(8,128)(2,1)S(1)}, u32[]{:S(2)}, u32[]{:S(2)}) %collective-permute-start.14) | collective-permute-done | bytes 524320 | tf_op jit(solution)/shard_map/ppermute | solution.py:187
  145.7 11.1 %collective-permute-done.15 = bf16[256,1024]{1,0:T(8,128)(2,1)S(1)} collective-permute-done((bf16[256,1024]{1,0:T(8,128)(2,1)S(1)}, bf16[256,1024]{1,0:T(8,128)(2,1)S(1)}, u32[]{:S(2)}, u32[]{:S(2)}) %collective-permute-start.15) | collective-permute-done | bytes 524320 | tf_op jit(solution)/shard_map/ppermute | solution.py:187
  156.9 10.3 %collective-permute-done.16 = bf16[256,1024]{1,0:T(8,128)(2,1)S(1)} collective-permute-done((bf16[256,1024]{1,0:T(8,128)(2,1)S(1)}, bf16[256,1024]{1,0:T(8,128)(2,1)S(1)}, u32[]{:S(2)}, u32[]{:S(2)}) %collective-permute-start.16) | collective-permute-done | bytes 524320 | tf_op jit(solution)/shard_map/ppermute | solution.py:187
  188.3 12.7 %collective-permute-done.24 = bf16[256,1024]{1,0:T(8,128)(2,1)S(1)} collective-permute-done((bf16[256,1024]{1,0:T(8,128)(2,1)S(1)}, bf16[256,1024]{1,0:T(8,128)(2,1)S(1)}, u32[]{:S(2)}, u32[]{:S(2)}) %collective-permute-start.24) | collective-permute-done | bytes 524320 | tf_op jit(solution)/shard_map/ppermute | solution.py:187
  201.0 11.2 %collective-permute-done.25 = bf16[256,1024]{1,0:T(8,128)(2,1)S(1)} collective-permute-done((bf16[256,1024]{1,0:T(8,128)(2,1)S(1)}, bf16[256,1024]{1,0:T(8,128)(2,1)S(1)}, u32[]{:S(2)}, u32[]{:S(2)}) %collective-permute-start.25) | collective-permute-done | bytes 524320 | tf_op jit(solution)/shard_map/ppermute | solution.py:187
  223.5 11.2 %collective-permute-done.27 = bf16[256,1024]{1,0:T(8,128)(2,1)S(1)} collective-permute-done((bf16[256,1024]{1,0:T(8,128)(2,1)S(1)}, bf16[256,1024]{1,0:T(8,128)(2,1)S(1)}, u32[]{:S(2)}, u32[]{:S(2)}) %collective-permute-start.27) | collective-permute-done | bytes 524320 | tf_op jit(solution)/shard_map/ppermute | solution.py:187
  237.6 10.6 %collective-permute-done.20 = bf16[128,2048]{1,0:T(8,128)(2,1)S(1)} collective-permute-done((bf16[128,2048]{1,0:T(8,128)(2,1)S(1)}, bf16[128,2048]{1,0:T(8,128)(2,1)S(1)}, u32[]{:S(2)}, u32[]{:S(2)}) %collective-permute-start.20) | collective-permute-done | bytes 524320 | tf_op jit(solution)/shard_map/ppermute | solution.py:177
  276.0 13.9 %collective-permute-done.40 = bf16[256,1280]{1,0:T(8,128)(2,1)S(1)} collective-permute-done((bf16[256,1280]{1,0:T(8,128)(2,1)S(1)}, bf16[256,1280]{1,0:T(8,128)(2,1)S(1)}, u32[]{:S(2)}, u32[]{:S(2)}) %collective-permute-start.40) | collective-permute-done | bytes 655392 | tf_op jit(solution)/shard_map/ppermute | solution.py:187
  292.8 11.1 %collective-permute-done.41 = bf16[256,1280]{1,0:T(8,128)(2,1)S(1)} collective-permute-done((bf16[256,1280]{1,0:T(8,128)(2,1)}, bf16[256,1280]{1,0:T(8,128)(2,1)S(1)}, u32[]{:S(2)}, u32[]{:S(2)}) %collective-permute-start.41) | collective-permute-done | bytes 655392 | tf_op jit(solution)/shard_map/ppermute | solution.py:187
  303.9 14.0 %collective-permute-done.42 = bf16[256,1280]{1,0:T(8,128)(2,1)S(1)} collective-permute-done((bf16[256,1280]{1,0:T(8,128)(2,1)S(1)}, bf16[256,1280]{1,0:T(8,128)(2,1)S(1)}, u32[]{:S(2)}, u32[]{:S(2)}) %collective-permute-start.42) | collective-permute-done | bytes 655392 | tf_op jit(solution)/shard_map/ppermute | solution.py:187
  320.1 12.0 %collective-permute-done.43 = bf16[256,1280]{1,0:T(8,128)(2,1)S(1)} collective-permute-done((bf16[256,1280]{1,0:T(8,128)(2,1)S(1)}, bf16[256,1280]{1,0:T(8,128)(2,1)S(1)}, u32[]{:S(2)}, u32[]{:S(2)}) %collective-permute-start.43) | collective-permute-done | bytes 655392 | tf_op jit(solution)/shard_map/ppermute | solution.py:187
  332.0 14.0 %collective-permute-done.44 = bf16[256,1280]{1,0:T(8,128)(2,1)S(1)} collective-permute-done((bf16[256,1280]{1,0:T(8,128)(2,1)S(1)}, bf16[256,1280]{1,0:T(8,128)(2,1)S(1)}, u32[]{:S(2)}, u32[]{:S(2)}) %collective-permute-start.44) | collective-permute-done | bytes 655392 | tf_op jit(solution)/shard_map/ppermute | solution.py:187
  372.9 10.8 %collective-permute-done.51 = bf16[256,640]{1,0:T(8,128)(2,1)S(1)} collective-permute-done((bf16[256,640]{1,0:T(8,128)(2,1)S(1)}, bf16[256,640]{1,0:T(8,128)(2,1)S(1)}, u32[]{:S(2)}, u32[]{:S(2)}) %collective-permute-start.51) | collective-permute-done | bytes 327712 | tf_op jit(solution)/shard_map/ppermute | solution.py:187
  423.1 11.8 %collective-permute-done.92 = bf16[256,640]{1,0:T(8,128)(2,1)S(1)} collective-permute-done((bf16[256,640]{1,0:T(8,128)(2,1)S(1)}, bf16[256,640]{1,0:T(8,128)(2,1)S(1)}, u32[]{:S(2)}, u32[]{:S(2)}) %collective-permute-start.92) | collective-permute-done | bytes 327712 | tf_op jit(solution)/shard_map/ppermute | solution.py:187
  440.2 12.2 %collective-permute-done.93 = bf16[256,640]{1,0:T(8,128)(2,1)S(1)} collective-permute-done((bf16[256,640]{1,0:T(8,128)(2,1)S(1)}, bf16[256,640]{1,0:T(8,128)(2,1)S(1)}, u32[]{:S(2)}, u32[]{:S(2)}) %collective-permute-start.93) | collective-permute-done | bytes 327712 | tf_op jit(solution)/shard_map/ppermute | solution.py:187
  468.1 10.5 %collective-permute-done.59 = bf16[128,2048]{1,0:T(8,128)(2,1)S(1)} collective-permute-done((bf16[128,2048]{1,0:T(8,128)(2,1)S(1)}, bf16[128,2048]{1,0:T(8,128)(2,1)S(1)}, u32[]{:S(2)}, u32[]{:S(2)}) %collective-permute-start.59) | collective-permute-done | bytes 524320 | tf_op jit(solution)/shard_map/ppermute | solution.py:177
  507.5 13.8 %collective-permute-done.95 = bf16[256,1280]{1,0:T(8,128)(2,1)S(1)} collective-permute-done((bf16[256,1280]{1,0:T(8,128)(2,1)S(1)}, bf16[256,1280]{1,0:T(8,128)(2,1)S(1)}, u32[]{:S(2)}, u32[]{:S(2)}) %collective-permute-start.95) | collective-permute-done | bytes 655392 | tf_op jit(solution)/shard_map/ppermute | solution.py:187
  522.9 12.4 %collective-permute-done.84 = bf16[256,1280]{1,0:T(8,128)(2,1)S(1)} collective-permute-done((bf16[256,1280]{1,0:T(8,128)(2,1)S(1)}, bf16[256,1280]{1,0:T(8,128)(2,1)S(1)}, u32[]{:S(2)}, u32[]{:S(2)}) %collective-permute-start.84) | collective-permute-done | bytes 655392 | tf_op jit(solution)/shard_map/ppermute | solution.py:187
  565.1 9.4 %shard_map.316 = (bf16[512,256]{1,0:T(8,128)(2,1)}, bf16[512,512]{1,0:T(8,128)(2,1)}) custom-call(s32[4,128,1]{2,1,0:T(8,128)} %copy.73.qid_ref, s32[4,1,128]{2,1,0:T(1,128)} %broadcast_in_dim.157.kid_ref, bf16[512,256]{1,0:T(8,128)(2,1)} %convolution_convert_fusion.9.q_ref, bf16[512,512]{1,0:T(8,128)(2,1)} %fusion.18.k_ref.v_ref, ...), custom_call_target="tpu_custom_call" | custom-call | flops 167772160 | bytes 1835008 | tf_op jit(solution)/shard_map/pallas_call | solution.py:102
  585.9 15.4 %collective-permute-done.85 = bf16[256,1024]{1,0:T(8,128)(2,1)S(1)} collective-permute-done((bf16[256,1024]{1,0:T(8,128)(2,1)S(1)}, bf16[256,1024]{1,0:T(8,128)(2,1)S(1)}, u32[]{:S(2)}, u32[]{:S(2)}) %collective-permute-start.85) | collective-permute-done | bytes 524320 | tf_op jit(solution)/shard_map/ppermute | solution.py:187
  601.5 11.0 %collective-permute-done.97 = bf16[256,1024]{1,0:T(8,128)(2,1)S(1)} collective-permute-done((bf16[256,1024]{1,0:T(8,128)(2,1)S(1)}, bf16[256,1024]{1,0:T(8,128)(2,1)S(1)}, u32[]{:S(2)}, u32[]{:S(2)}) %collective-permute-start.97) | collective-permute-done | bytes 524320 | tf_op jit(solution)/shard_map/ppermute | solution.py:187
  646.3 10.7 %collective-permute-done.99 = bf16[256,1024]{1,0:T(8,128)(2,1)S(1)} collective-permute-done((bf16[256,1024]{1,0:T(8,128)(2,1)S(1)}, bf16[256,1024]{1,0:T(8,128)(2,1)S(1)}, u32[]{:S(2)}, u32[]{:S(2)}) %collective-permute-start.99) | collective-permute-done | bytes 524320 | tf_op jit(solution)/shard_map/ppermute | solution.py:187
  672.5 9.8 %collective-permute-done.66 = bf16[128,2048]{1,0:T(8,128)(2,1)S(1)} collective-permute-done((bf16[128,2048]{1,0:T(8,128)(2,1)S(1)}, bf16[128,2048]{1,0:T(8,128)(2,1)S(1)}, u32[]{:S(2)}, u32[]{:S(2)}) %collective-permute-start.66) | collective-permute-done | bytes 524320 | tf_op jit(solution)/shard_map/ppermute | solution.py:177
  689.2 9.4 %shard_map.317 = (bf16[512,256]{1,0:T(8,128)(2,1)}, bf16[512,512]{1,0:T(8,128)(2,1)}) custom-call(s32[4,128,1]{2,1,0:T(8,128)} %copy.71.qid_ref, s32[4,1,128]{2,1,0:T(1,128)} %copy-done.87, bf16[512,768]{1,0:T(8,128)(2,1)} %fusion.8.q_ref.k_ref.v_ref, bf16[512,768]{1,0:T(8,128)(2,1)} %fusion.8.q_ref.k_ref.v_ref, bf16[512,768]{1,0:T(8,128)(2,1)} %fusion.8.q_ref.k_ref.v_ref, ...), custom_call_target="tpu_custom_call" | custom-call | flops 167772160 | bytes 1835008 | tf_op jit(solution)/shard_map/pallas_call | solution.py:102
  708.8 13.8 %collective-permute-done.88 = bf16[256,1024]{1,0:T(8,128)(2,1)S(1)} collective-permute-done((bf16[256,1024]{1,0:T(8,128)(2,1)S(1)}, bf16[256,1024]{1,0:T(8,128)(2,1)S(1)}, u32[]{:S(2)}, u32[]{:S(2)}) %collective-permute-start.88) | collective-permute-done | bytes 524320 | tf_op jit(solution)/shard_map/ppermute | solution.py:187
  722.8 11.0 %collective-permute-done.100 = bf16[256,1024]{1,0:T(8,128)(2,1)S(1)} collective-permute-done((bf16[256,1024]{1,0:T(8,128)(2,1)S(1)}, bf16[256,1024]{1,0:T(8,128)(2,1)S(1)}, u32[]{:S(2)}, u32[]{:S(2)}) %collective-permute-start.100) | collective-permute-done | bytes 524320 | tf_op jit(solution)/shard_map/ppermute | solution.py:187
  745.3 11.0 %collective-permute-done.101 = bf16[256,1024]{1,0:T(8,128)(2,1)S(1)} collective-permute-done((bf16[256,1024]{1,0:T(8,128)(2,1)S(1)}, bf16[256,1024]{1,0:T(8,128)(2,1)S(1)}, u32[]{:S(2)}, u32[]{:S(2)}) %collective-permute-start.101) | collective-permute-done | bytes 524320 | tf_op jit(solution)/shard_map/ppermute | solution.py:187
  767.7 10.7 %collective-permute-done.102 = bf16[256,1024]{1,0:T(8,128)(2,1)S(1)} collective-permute-done((bf16[256,1024]{1,0:T(8,128)(2,1)S(1)}, bf16[256,1024]{1,0:T(8,128)(2,1)S(1)}, u32[]{:S(2)}, u32[]{:S(2)}) %collective-permute-start.102) | collective-permute-done | bytes 524320 | tf_op jit(solution)/shard_map/ppermute | solution.py:187
  (704 shorter events, 439.5 us)
Async XLA Ops:
  9.4 61.5 %collective-permute-start.30 = (bf16[128,2048]{1,0:T(8,128)(2,1)}, bf16[128,2048]{1,0:T(8,128)(2,1)}, u32[]{:S(2)}, u32[]{:S(2)}) collective-permute-start(bf16[128,2048]{1,0:T(8,128)(2,1)} %bitcast.669), channel_id=1, source_target_pairs={{0,4},{2,6},{4,0},{6,2},{8,12},{10,14},{12,8},{14,10},{16,20},{18,... | collective-permute-start | bytes 1572872 | tf_op jit(solution)/shard_map/ppermute | solution.py:177
  11.4 56.8 %collective-permute-start.56 = (bf16[128,2048]{1,0:T(8,128)(2,1)}, bf16[128,2048]{1,0:T(8,128)(2,1)}, u32[]{:S(2)}, u32[]{:S(2)}) collective-permute-start(bf16[128,2048]{1,0:T(8,128)(2,1)} %param.23), channel_id=1, source_target_pairs={{0,4},{2,6},{4,0},{6,2},{8,12},{10,14},{12,8},{14,10},{16,20},{18,... | collective-permute-start | bytes 1572872 | tf_op jit(solution)/shard_map/ppermute | solution.py:177
  14.5 42.0 %collective-permute-start.45 = (bf16[2,128,640]{2,1,0:T(8,128)(2,1)}, bf16[2,128,640]{2,1,0:T(8,128)(2,1)}, u32[]{:S(2)}, u32[]{:S(2)}) collective-permute-start(bf16[2,128,640]{2,1,0:T(8,128)(2,1)} %pad_maximum_fusion.70), channel_id=1, source_target_pairs={{0,4},{2,6},{4,0},{6,2},{8,12},{10,14},{12,8},{14,10},{16,20},{18,... | collective-permute-start | bytes 983048 | tf_op jit(solution)/shard_map/ppermute | solution.py:177
  29.0 28.9 %collective-permute-start.22 = (bf16[2,128,1024]{2,1,0:T(8,128)(2,1)}, bf16[2,128,1024]{2,1,0:T(8,128)(2,1)}, u32[]{:S(2)}, u32[]{:S(2)}) collective-permute-start(bf16[2,128,1024]{2,1,0:T(8,128)(2,1)} %pad_maximum_fusion.44), channel_id=1, source_target_pairs={{0,4},{2,6},{4,0},{6,2},{8,12},{10,14},{12,8},{14,10},{16,20},{18,... | collective-permute-start | bytes 1572872 | tf_op jit(solution)/shard_map/ppermute | solution.py:177
  56.5 35.6 %collective-permute-start.37 = (bf16[2,128,1280]{2,1,0:T(8,128)(2,1)}, bf16[2,128,1280]{2,1,0:T(8,128)(2,1)S(1)}, u32[]{:S(2)}, u32[]{:S(2)}) collective-permute-start(bf16[2,128,1280]{2,1,0:T(8,128)(2,1)} %pad_maximum_fusion.30), channel_id=1, source_target_pairs={{0,4},{2,6},{4,0},{6,2},{8,12},{10,14},{12,8},{14,10},{16,20},{18,... | collective-permute-start | bytes 1966088 | tf_op jit(solution)/shard_map/ppermute | solution.py:177
  57.9 31.4 %collective-permute-start.7 = (bf16[128,2048]{1,0:T(8,128)(2,1)S(1)}, bf16[128,2048]{1,0:T(8,128)(2,1)S(1)}, u32[]{:S(2)}, u32[]{:S(2)}) collective-permute-start(bf16[128,2048]{1,0:T(8,128)(2,1)S(1)} %fusion.23), channel_id=1, source_target_pairs={{0,4},{2,6},{4,0},{6,2},{8,12},{10,14},{12,8},{14,10},{16,20},{18,... | collective-permute-start | bytes 1572872 | tf_op jit(solution)/shard_map/ppermute | solution.py:177
  68.2 30.9 %collective-permute-start.23 = (bf16[2,128,1024]{2,1,0:T(8,128)(2,1)S(1)}, bf16[2,128,1024]{2,1,0:T(8,128)(2,1)S(1)}, u32[]{:S(2)}, u32[]{:S(2)}) collective-permute-start(bf16[2,128,1024]{2,1,0:T(8,128)(2,1)S(1)} %pad_maximum_fusion.45), channel_id=1, source_target_pairs={{0,2},{2,0},{4,6},{6,4},{8,10},{10,8},{12,14},{14,12},{16,18},{18,... | collective-permute-start | bytes 1572872 | tf_op jit(solution)/shard_map/ppermute | solution.py:177
  89.4 124.7 %collective-permute-start.31 = (bf16[2,128,2048]{2,1,0:T(8,128)(2,1)}, bf16[2,128,2048]{2,1,0:T(8,128)(2,1)}, u32[]{:S(2)}, u32[]{:S(2)}) collective-permute-start(bf16[2,128,2048]{2,1,0:T(8,128)(2,1)} %pad_maximum_fusion.15), channel_id=1, source_target_pairs={{0,2},{2,0},{4,6},{6,4},{8,10},{10,8},{12,14},{14,12},{16,18},{18,... | collective-permute-start | bytes 3145736 | tf_op jit(solution)/shard_map/ppermute | solution.py:177
  89.5 44.9 %collective-permute-start.8 = (bf16[2,128,2048]{2,1,0:T(8,128)(2,1)S(1)}, bf16[2,128,2048]{2,1,0:T(8,128)(2,1)S(1)}, u32[]{:S(2)}, u32[]{:S(2)}) collective-permute-start(bf16[2,128,2048]{2,1,0:T(8,128)(2,1)S(1)} %pad_maximum_fusion.10), channel_id=1, source_target_pairs={{0,2},{2,0},{4,6},{6,4},{8,10},{10,8},{12,14},{14,12},{16,18},{18,... | collective-permute-start | bytes 3145736 | tf_op jit(solution)/shard_map/ppermute | solution.py:177
  99.1 173.3 %collective-permute-start.57 = (bf16[2,128,2048]{2,1,0:T(8,128)(2,1)}, bf16[2,128,2048]{2,1,0:T(8,128)(2,1)}, u32[]{:S(2)}, u32[]{:S(2)}) collective-permute-start(bf16[2,128,2048]{2,1,0:T(8,128)(2,1)} %pad_maximum_fusion.19), channel_id=1, source_target_pairs={{0,2},{2,0},{4,6},{6,4},{8,10},{10,8},{12,14},{14,12},{16,18},{18,... | collective-permute-start | bytes 3145736 | tf_op jit(solution)/shard_map/ppermute | solution.py:177
  134.4 48.9 %collective-permute-start.38 = (bf16[2,128,1280]{2,1,0:T(8,128)(2,1)}, bf16[2,128,1280]{2,1,0:T(8,128)(2,1)S(1)}, u32[]{:S(2)}, u32[]{:S(2)}) collective-permute-start(bf16[2,128,1280]{2,1,0:T(8,128)(2,1)} %pad_maximum_fusion.31), channel_id=1, source_target_pairs={{0,2},{2,0},{4,6},{6,4},{8,10},{10,8},{12,14},{14,12},{16,18},{18,... | collective-permute-start | bytes 1966088 | tf_op jit(solution)/shard_map/ppermute | solution.py:177
  184.5 27.8 %collective-permute-start.25 = (bf16[256,1024]{1,0:T(8,128)(2,1)S(1)}, bf16[256,1024]{1,0:T(8,128)(2,1)S(1)}, u32[]{:S(2)}, u32[]{:S(2)}) collective-permute-start(bf16[256,1024]{1,0:T(8,128)(2,1)S(1)} %pad_maximum_fusion.47), channel_id=1, source_target_pairs={{0,8},{2,10},{4,12},{6,14},{8,16},{10,18},{12,20},{14,22},{16,24},... | collective-permute-start | bytes 1572872 | tf_op jit(solution)/shard_map/ppermute | solution.py:187
  223.5 32.9 %collective-permute-start.28 = (bf16[256,1024]{1,0:T(8,128)(2,1)S(1)}, bf16[256,1024]{1,0:T(8,128)(2,1)S(1)}, u32[]{:S(2)}, u32[]{:S(2)}) collective-permute-start(bf16[256,1024]{1,0:T(8,128)(2,1)S(1)} %collective-permute-done.26), channel_id=1, source_target_pairs={{0,8},{2,10},{4,12},{6,14},{8,16},{10,18},{12,20},{14,22},{16,24},... | collective-permute-start | bytes 1572872 | tf_op jit(solution)/shard_map/ppermute | solution.py:187
  256.4 33.5 %collective-permute-start.40 = (bf16[256,1280]{1,0:T(8,128)(2,1)S(1)}, bf16[256,1280]{1,0:T(8,128)(2,1)S(1)}, u32[]{:S(2)}, u32[]{:S(2)}) collective-permute-start(bf16[256,1280]{1,0:T(8,128)(2,1)S(1)} %pad_maximum_fusion.33), channel_id=1, source_target_pairs={{0,8},{2,10},{4,12},{6,14},{8,16},{10,18},{12,20},{14,22},{16,24},... | collective-permute-start | bytes 1966088 | tf_op jit(solution)/shard_map/ppermute | solution.py:187
  272.3 45.7 %collective-permute-start.32 = (bf16[2,128,2048]{2,1,0:T(8,128)(2,1)S(1)}, bf16[2,128,2048]{2,1,0:T(8,128)(2,1)S(1)}, u32[]{:S(2)}, u32[]{:S(2)}) collective-permute-start(bf16[2,128,2048]{2,1,0:T(8,128)(2,1)S(1)} %pad_maximum_fusion.16), channel_id=1, source_target_pairs={{0,2},{2,0},{4,6},{6,4},{8,10},{10,8},{12,14},{14,12},{16,18},{18,... | collective-permute-start | bytes 3145736 | tf_op jit(solution)/shard_map/ppermute | solution.py:177
  276.0 28.0 %collective-permute-start.41 = (bf16[256,1280]{1,0:T(8,128)(2,1)}, bf16[256,1280]{1,0:T(8,128)(2,1)S(1)}, u32[]{:S(2)}, u32[]{:S(2)}) collective-permute-start(bf16[256,1280]{1,0:T(8,128)(2,1)} %collective-permute-done.39), channel_id=1, source_target_pairs={{0,8},{2,10},{4,12},{6,14},{8,16},{10,18},{12,20},{14,22},{16,24},... | collective-permute-start | bytes 1966088 | tf_op jit(solution)/shard_map/ppermute | solution.py:187
  289.9 28.1 %collective-permute-start.42 = (bf16[256,1280]{1,0:T(8,128)(2,1)S(1)}, bf16[256,1280]{1,0:T(8,128)(2,1)S(1)}, u32[]{:S(2)}, u32[]{:S(2)}) collective-permute-start(bf16[256,1280]{1,0:T(8,128)(2,1)S(1)} %collective-permute-done.40), channel_id=1, source_target_pairs={{0,8},{2,10},{4,12},{6,14},{8,16},{10,18},{12,20},{14,22},{16,24},... | collective-permute-start | bytes 1966088 | tf_op jit(solution)/shard_map/ppermute | solution.py:187
  303.9 28.1 %collective-permute-start.43 = (bf16[256,1280]{1,0:T(8,128)(2,1)S(1)}, bf16[256,1280]{1,0:T(8,128)(2,1)S(1)}, u32[]{:S(2)}, u32[]{:S(2)}) collective-permute-start(bf16[256,1280]{1,0:T(8,128)(2,1)S(1)} %collective-permute-done.41), channel_id=1, source_target_pairs={{0,8},{2,10},{4,12},{6,14},{8,16},{10,18},{12,20},{14,22},{16,24},... | collective-permute-start | bytes 1966088 | tf_op jit(solution)/shard_map/ppermute | solution.py:187
  318.0 28.1 %collective-permute-start.44 = (bf16[256,1280]{1,0:T(8,128)(2,1)S(1)}, bf16[256,1280]{1,0:T(8,128)(2,1)S(1)}, u32[]{:S(2)}, u32[]{:S(2)}) collective-permute-start(bf16[256,1280]{1,0:T(8,128)(2,1)S(1)} %collective-permute-done.42), channel_id=1, source_target_pairs={{0,8},{2,10},{4,12},{6,14},{8,16},{10,18},{12,20},{14,22},{16,24},... | collective-permute-start | bytes 1966088 | tf_op jit(solution)/shard_map/ppermute | solution.py:187
  406.4 51.8 %collective-permute-start.58 = (bf16[2,128,2048]{2,1,0:T(8,128)(2,1)S(1)}, bf16[2,128,2048]{2,1,0:T(8,128)(2,1)S(1)}, u32[]{:S(2)}, u32[]{:S(2)}) collective-permute-start(bf16[2,128,2048]{2,1,0:T(8,128)(2,1)S(1)} %pad_maximum_fusion.20), channel_id=1, source_target_pairs={{0,2},{2,0},{4,6},{6,4},{8,10},{10,8},{12,14},{14,12},{16,18},{18,... | collective-permute-start | bytes 3145736 | tf_op jit(solution)/shard_map/ppermute | solution.py:177
  406.7 52.5 %collective-permute-start.53 = (bf16[2,128,2048]{2,1,0:T(8,128)(2,1)S(1)}, bf16[2,128,2048]{2,1,0:T(8,128)(2,1)S(1)}, u32[]{:S(2)}, u32[]{:S(2)}) collective-permute-start(bf16[2,128,2048]{2,1,0:T(8,128)(2,1)S(1)} %pad_maximum_fusion.18), channel_id=1, source_target_pairs={{0,2},{2,0},{4,6},{6,4},{8,10},{10,8},{12,14},{14,12},{16,18},{18,... | collective-permute-start | bytes 3145736 | tf_op jit(solution)/shard_map/ppermute | solution.py:177
  458.2 29.3 %collective-permute-start.82 = (bf16[256,1280]{1,0:T(8,128)(2,1)S(1)}, bf16[256,1280]{1,0:T(8,128)(2,1)S(1)}, u32[]{:S(2)}, u32[]{:S(2)}) collective-permute-start(bf16[256,1280]{1,0:T(8,128)(2,1)S(1)} %pad_maximum_fusion.35), channel_id=1, source_target_pairs={{0,8},{2,10},{4,12},{6,14},{8,16},{10,18},{12,20},{14,22},{16,24},... | collective-permute-start | bytes 1966088 | tf_op jit(solution)/shard_map/ppermute | solution.py:187
  458.2 29.6 %collective-permute-start.94 = (bf16[256,1280]{1,0:T(8,128)(2,1)S(1)}, bf16[256,1280]{1,0:T(8,128)(2,1)S(1)}, u32[]{:S(2)}, u32[]{:S(2)}) collective-permute-start(bf16[256,1280]{1,0:T(8,128)(2,1)S(1)} %pad_maximum_fusion.36), channel_id=1, source_target_pairs={{0,8},{2,10},{4,12},{6,14},{8,16},{10,18},{12,20},{14,22},{16,24},... | collective-permute-start | bytes 1966088 | tf_op jit(solution)/shard_map/ppermute | solution.py:187
  467.4 80.5 %collective-permute-start.110 = (bf16[2,128,640]{2,1,0:T(8,128)(2,1)S(1)}, bf16[2,128,640]{2,1,0:T(8,128)(2,1)}, u32[]{:S(2)}, u32[]{:S(2)}) collective-permute-start(bf16[2,128,640]{2,1,0:T(8,128)(2,1)S(1)} %pad_maximum_fusion.75), channel_id=1, source_target_pairs={{0,2},{2,0},{4,6},{6,4},{8,10},{10,8},{12,14},{14,12},{16,18},{18,... | collective-permute-start | bytes 983048 | tf_op jit(solution)/shard_map/ppermute | solution.py:177
  487.9 33.3 %collective-permute-start.95 = (bf16[256,1280]{1,0:T(8,128)(2,1)S(1)}, bf16[256,1280]{1,0:T(8,128)(2,1)S(1)}, u32[]{:S(2)}, u32[]{:S(2)}) collective-permute-start(bf16[256,1280]{1,0:T(8,128)(2,1)S(1)} %add_convert_fusion.3), channel_id=1, source_target_pairs={{0,8},{2,10},{4,12},{6,14},{8,16},{10,18},{12,20},{14,22},{16,24},... | collective-permute-start | bytes 1966088 | tf_op jit(solution)/shard_map/ppermute | solution.py:187
  507.4 27.9 %collective-permute-start.84 = (bf16[256,1280]{1,0:T(8,128)(2,1)S(1)}, bf16[256,1280]{1,0:T(8,128)(2,1)S(1)}, u32[]{:S(2)}, u32[]{:S(2)}) collective-permute-start(bf16[256,1280]{1,0:T(8,128)(2,1)S(1)} %add_convert_fusion.4), channel_id=1, source_target_pairs={{0,8},{2,10},{4,12},{6,14},{8,16},{10,18},{12,20},{14,22},{16,24},... | collective-permute-start | bytes 1966088 | tf_op jit(solution)/shard_map/ppermute | solution.py:187
  522.9 37.2 %collective-permute-start.62 = (bf16[2,128,2048]{2,1,0:T(8,128)(2,1)}, bf16[2,128,2048]{2,1,0:T(8,128)(2,1)}, u32[]{:S(2)}, u32[]{:S(2)}) collective-permute-start(bf16[2,128,2048]{2,1,0:T(8,128)(2,1)} %pad_maximum_fusion.21), channel_id=1, source_target_pairs={{0,2},{2,0},{4,6},{6,4},{8,10},{10,8},{12,14},{14,12},{16,18},{18,... | collective-permute-start | bytes 3145736 | tf_op jit(solution)/shard_map/ppermute | solution.py:177
  560.1 52.6 %collective-permute-start.108 = (bf16[2,128,1280]{2,1,0:T(8,128)(2,1)}, bf16[2,128,1280]{2,1,0:T(8,128)(2,1)S(1)}, u32[]{:S(2)}, u32[]{:S(2)}) collective-permute-start(bf16[2,128,1280]{2,1,0:T(8,128)(2,1)} %pad_maximum_fusion.38), channel_id=1, source_target_pairs={{0,2},{2,0},{4,6},{6,4},{8,10},{10,8},{12,14},{14,12},{16,18},{18,... | collective-permute-start | bytes 1966088 | tf_op jit(solution)/shard_map/ppermute | solution.py:177
  584.7 27.7 %collective-permute-start.97 = (bf16[256,1024]{1,0:T(8,128)(2,1)S(1)}, bf16[256,1024]{1,0:T(8,128)(2,1)S(1)}, u32[]{:S(2)}, u32[]{:S(2)}) collective-permute-start(bf16[256,1024]{1,0:T(8,128)(2,1)S(1)} %pad_maximum_fusion.51), channel_id=1, source_target_pairs={{0,8},{2,10},{4,12},{6,14},{8,16},{10,18},{12,20},{14,22},{16,24},... | collective-permute-start | bytes 1572872 | tf_op jit(solution)/shard_map/ppermute | solution.py:187
  585.0 50.4 %collective-permute-start.71 = (bf16[2,128,2048]{2,1,0:T(8,128)(2,1)S(1)}, bf16[2,128,2048]{2,1,0:T(8,128)(2,1)S(1)}, u32[]{:S(2)}, u32[]{:S(2)}) collective-permute-start(bf16[2,128,2048]{2,1,0:T(8,128)(2,1)S(1)} %pad_maximum_fusion.25), channel_id=1, source_target_pairs={{0,2},{2,0},{4,6},{6,4},{8,10},{10,8},{12,14},{14,12},{16,18},{18,... | collective-permute-start | bytes 3145736 | tf_op jit(solution)/shard_map/ppermute | solution.py:177
  585.8 38.1 %collective-permute-start.63 = (bf16[2,128,2048]{2,1,0:T(8,128)(2,1)S(1)}, bf16[2,128,2048]{2,1,0:T(8,128)(2,1)S(1)}, u32[]{:S(2)}, u32[]{:S(2)}) collective-permute-start(bf16[2,128,2048]{2,1,0:T(8,128)(2,1)S(1)} %pad_maximum_fusion.22), channel_id=1, source_target_pairs={{0,2},{2,0},{4,6},{6,4},{8,10},{10,8},{12,14},{14,12},{16,18},{18,... | collective-permute-start | bytes 3145736 | tf_op jit(solution)/shard_map/ppermute | solution.py:177
  706.3 27.7 %collective-permute-start.68 = (bf16[2,128,2048]{2,1,0:T(8,128)(2,1)S(1)}, bf16[2,128,2048]{2,1,0:T(8,128)(2,1)S(1)}, u32[]{:S(2)}, u32[]{:S(2)}) collective-permute-start(bf16[2,128,2048]{2,1,0:T(8,128)(2,1)S(1)} %pad_maximum_fusion.24), channel_id=1, source_target_pairs={{0,2},{2,0},{4,6},{6,4},{8,10},{10,8},{12,14},{14,12},{16,18},{18,... | collective-permute-start | bytes 3145736 | tf_op jit(solution)/shard_map/ppermute | solution.py:177
  (182 other events, 2285.0 us)

commit v2 on v1

v2 whole, which is shorter than its diff:
```python
import functools

import jax
import jax.numpy as jnp
from jax import lax
from jax.experimental import pallas as pl
from jax.experimental.pallas import tpu as pltpu
from jax.sharding import PartitionSpec as P

HEAD_DIM = 64
ATTN = 4
FFN = 4
EPS = 1e-06
NEG = -1e30
BF = jnp.bfloat16
F32 = jnp.float32


def dot(a, b, da, db):
    return lax.dot_general(a, b, (((da,), (db,)), ((), ())), preferred_element_type=F32)


def mask_of(qid_ref, kid_ref, causal):
    allowed = qid_ref[...] == kid_ref[...]
    if causal:
        rows = lax.broadcasted_iota(jnp.int32, allowed.shape, 0)
        cols = lax.broadcasted_iota(jnp.int32, allowed.shape, 1)
        allowed = allowed & (rows >= cols)
    return allowed


def soft(scores, allowed):
    scores = jnp.where(allowed, scores * HEAD_DIM ** (-0.5), NEG)
    raised = jnp.exp(scores - jnp.max(scores, axis=-1, keepdims=True))
    return raised * (1.0 / jnp.sum(raised, axis=-1, keepdims=True))


def heads_of(ref):
    return [ref[:, first : first + HEAD_DIM] for first in range(0, ref.shape[1], HEAD_DIM)]


def attend_kernel(causal, qid_ref, kid_ref, q_ref, k_ref, v_ref, out_ref):
    allowed = mask_of(qid_ref, kid_ref, causal)
    scores = jnp.stack([dot(q, k, 1, 1) for q, k in zip(heads_of(q_ref), heads_of(k_ref))])
    probs = soft(scores, allowed[None]).astype(BF)
    pieces = [dot(probs[h], v, 1, 0).astype(BF) for h, v in enumerate(heads_of(v_ref))]
    out_ref[...] = jnp.concatenate(pieces, axis=1)


def attend_back_kernel(causal, qid_ref, kid_ref, q_ref, k_ref, v_ref, g_ref, dq_ref, dkv_ref):
    allowed = mask_of(qid_ref, kid_ref, causal)
    scale = HEAD_DIM ** (-0.5)
    qs, ks, vs, gs = heads_of(q_ref), heads_of(k_ref), heads_of(v_ref), heads_of(g_ref)
    scores = jnp.stack([dot(q, k, 1, 1) for q, k in zip(qs, ks)])
    grad_probs = jnp.stack([dot(g, v, 1, 1) for g, v in zip(gs, vs)])
    probs = soft(scores, allowed[None])
    centre = jnp.sum(probs * grad_probs, axis=-1, keepdims=True)
    ds = (probs * (grad_probs - centre)).astype(BF)
    probs = probs.astype(BF)
    dvs = [dot(probs[h], g, 0, 0).astype(BF) for h, g in enumerate(gs)]
    dqs = [(dot(ds[h], k, 1, 0) * scale).astype(BF) for h, k in enumerate(ks)]
    dks = [(dot(ds[h], q, 0, 0) * scale).astype(BF) for h, q in enumerate(qs)]
    dq_ref[...] = jnp.concatenate(dqs, axis=1)
    dkv_ref[...] = jnp.concatenate(dks + dvs, axis=1)


def id_specs(length, keys):
    return [
        pl.BlockSpec((None, length, 1), lambda r: (r, 0, 0)),
        pl.BlockSpec((None, 1, keys), lambda r: (r, 0, 0)),
    ]


def attend(causal, qid, kid, q, k, v):
    rows, length, _ = qid.shape
    keys = kid.shape[2]
    width = q[2]
    specs = [
        pl.BlockSpec((n, width), functools.partial(lambda c, r: (r, c), col))
        for n, col in ((length, q[1]), (keys, k[1]), (keys, v[1]))
    ]
    return pl.pallas_call(
        functools.partial(attend_kernel, causal),
        grid=(rows,),
        in_specs=id_specs(length, keys) + specs,
        out_specs=pl.BlockSpec((length, width), lambda r: (r, 0)),
        out_shape=jax.ShapeDtypeStruct((rows * length, width), BF),
        cost_estimate=pl.CostEstimate(
            flops=4 * rows * length * keys * width,
            transcendentals=rows * length * keys * width // HEAD_DIM,
            bytes_accessed=8 * rows * length * width,
        ),
    )(qid, kid, q[0], k[0], v[0])


def attend_back(causal, qid, kid, q, k, v, g):
    rows, length, _ = qid.shape
    keys = kid.shape[2]
    width = q[2]
    specs = [
        pl.BlockSpec((n, width), functools.partial(lambda c, r: (r, c), col))
        for n, col in ((length, q[1]), (keys, k[1]), (keys, v[1]), (length, 0))
    ]
    return pl.pallas_call(
        functools.partial(attend_back_kernel, causal),
        grid=(rows,),
        in_specs=id_specs(length, keys) + specs,
        out_specs=[
            pl.BlockSpec((length, width), lambda r: (r, 0)),
            pl.BlockSpec((keys, 2 * width), lambda r: (r, 0)),
        ],
        out_shape=[
            jax.ShapeDtypeStruct((rows * length, width), BF),
            jax.ShapeDtypeStruct((rows * keys, 2 * width), BF),
        ],
        cost_estimate=pl.CostEstimate(
            flops=10 * rows * length * keys * width,
            transcendentals=rows * length * keys * width // HEAD_DIM,
            bytes_accessed=14 * rows * length * width,
        ),
    )(qid, kid, q[0], k[0], v[0], g)


def rms(values, gain):
    scale = lax.rsqrt(jnp.mean(values * values, axis=-1, keepdims=True) + EPS)
    return (values * scale * gain).astype(BF), scale


def rms_back(values, scale, gain, grad):
    weighted = grad * gain
    mean = jnp.mean(weighted * values, axis=-1, keepdims=True)
    return (
        scale * weighted - values * (scale * scale * scale) * mean,
        jnp.sum(grad * values * scale, axis=0, keepdims=True),
    )


def gelu_parts(gate):
    c = (2.0 / jnp.pi) ** 0.5
    inner = jnp.tanh(c * (gate + 0.044715 * gate * gate * gate))
    value = 0.5 * gate * (1.0 + inner)
    slope = 0.5 * (1.0 + inner) + 0.5 * gate * (1.0 - inner * inner) * c * (
        1.0 + 3 * 0.044715 * gate * gate
    )
    return value, slope


def on_device(
    inputs,
    segments,
    example_of,
    patches,
    grad_out,
    gain_self,
    wq_self,
    wk_self,
    wv_self,
    wo_self,
    gain_cross,
    wq_cross,
    wk_cross,
    wv_cross,
    wo_cross,
    gain_ffn,
    w_gate,
    w_up,
    w_down,
):
    dp = lax.axis_size("dp")
    place = lax.axis_index("dp")
    tokens, width = inputs.shape
    part = width // dp

    def tie(*values):
        return lax.optimization_barrier(values)

    def swap(value, distance):
        return lax.ppermute(value, "dp", [(i, i ^ distance) for i in range(dp)])

    def swap_mp(value):
        return lax.ppermute(value, "mp", [(0, 1), (1, 0)])

    def planes(inner):
        return [[m + inner * i for i in range(dp // inner)] for m in range(inner)]

    def rows_of(value, inner):
        even = [value] + [swap(value, d) for d in range(2, inner, 2)]
        odd = swap(jnp.stack(even), 1)
        return jnp.concatenate(
            [odd[d // 2] if d % 2 else even[d // 2] for d in range(inner)], axis=0
        )

    def reduce_rows(partial, inner):
        parts = partial.astype(BF).reshape(inner, -1, partial.shape[1])
        near = swap(jnp.stack([parts[d] for d in range(1, inner, 2)]), 1)
        total = parts[0].astype(F32) + near[0].astype(F32)
        for d in range(2, inner, 2):
            term = (parts[d].astype(F32) + near[d // 2].astype(F32)).astype(BF)
            total = total + swap(term, d).astype(F32)
        total = total.astype(BF)
        return total.astype(F32) + swap_mp(total).astype(F32)

    def exchange(blocks, inner):
        groups = [[m + inner * i for m in range(inner)] for i in range(dp // inner)]
        return lax.all_to_all(blocks, "dp", 0, 0, axis_index_groups=groups, tiled=True)

    def pack(weights, inner):
        return jnp.stack(
            [
                jnp.concatenate(
                    [
                        w[:, i * (w.shape[1] // inner) : (i + 1) * (w.shape[1] // inner)]
                        for w in weights
                    ],
                    axis=1,
                )
                for i in range(inner)
            ]
        )

    def over_planes(shard, inner):
        shard = shard.reshape(inner * part, -1)
        return lax.all_gather(shard, "dp", axis_index_groups=planes(inner), tiled=True)

    def scatter_weights(whole, widths, inner):
        held = lax.psum_scatter(whole, "dp", axis_index_groups=planes(inner), tiled=True)
        pieces = exchange(held.reshape(inner, part, -1), inner)
        out, at = [], 0
        for w in widths:
            cut = slice(at, at + w)
            out.append(jnp.concatenate([x[:, cut] for x in pieces], axis=1).astype(F32))
            at += w
        return out

    shard_self = exchange(pack([wq_self, wk_self, wv_self, wo_self.T], ATTN), ATTN)
    packed_cross = pack([wq_cross, wk_cross, wv_cross, wo_cross.T], ATTN)
    shard_self, inputs, packed_cross = tie(shard_self, inputs, packed_cross)
    w_self = over_planes(shard_self, ATTN)
    start_rows = rows_of(inputs, ATTN)
    shard_cross = exchange(packed_cross, ATTN)
    packed_ffn = pack([w_gate, w_up, w_down.T], FFN)
    shard_cross, patch_rows, packed_ffn = tie(shard_cross, patches.reshape(-1, width), packed_ffn)
    w_cross = over_planes(shard_cross, ATTN)
    memory = rows_of(patch_rows, ATTN)
    shard_ffn = exchange(packed_ffn, FFN)
    shard_ffn, grad_out = tie(shard_ffn, grad_out)
    grad_rows = rows_of(grad_out, FFN)
    start_rows, memory, grad_rows, shard_ffn = tie(start_rows, memory, grad_rows, shard_ffn)
    hw = w_self.shape[1] // 4

    gains = jnp.stack([gain_self, gain_cross, gain_ffn]).astype(F32)
    held = rows_of(jnp.stack([gains] + [swap(gains, d) for d in range(ATTN, dp, ATTN)])[None], ATTN)
    all_gains = jnp.zeros((dp, 3, part), F32)
    for i in range(dp // ATTN):
        for j in range(ATTN):
            all_gains = lax.dynamic_update_slice(
                all_gains, held[j, i][None], (place ^ (i * ATTN + j), 0, 0)
            )
    gain_first, gain_second, gain_third = (all_gains[:, i].reshape(1, width) for i in range(3))

    row_count, length = segments.shape
    examples, patch_count, _ = patches.shape
    slot = jnp.take_along_axis(example_of, segments, axis=1)
    ids = rows_of(jnp.concatenate([segments, slot], axis=0)[None], ATTN)
    seg_rows = ids[:, :row_count].reshape(ATTN * row_count, length)
    slot_rows = ids[:, row_count:].reshape(ATTN * row_count, length)
    key_slots = jnp.broadcast_to(
        (jnp.arange(examples * patch_count // row_count, dtype=jnp.int32) // patch_count),
        (ATTN * row_count, 1, examples * patch_count // row_count),
    )
    self_ids = (seg_rows[:, :, None], seg_rows[:, None, :])
    cross_ids = (slot_rows[:, :, None], key_slots)

    start = inputs.astype(F32)
    _, scale_self = rms(start, gain_first)
    normed_self, _ = rms(start_rows.astype(F32), gain_first)
    qkv = dot(normed_self, w_self[:, : 3 * hw], 1, 0).astype(BF)
    self_args = ((qkv, 0, hw), (qkv, 1, hw), (qkv, 2, hw))
    mixed_self = attend(True, *self_ids, *self_args)
    after_self = start + reduce_rows(dot(mixed_self, w_self[:, 3 * hw :], 1, 1), ATTN)
    normed, scale_cross = rms(after_self, gain_second)
    normed, shard_ffn = tie(normed, shard_ffn)
    normed_cross = rows_of(normed, ATTN)
    w_ffn = over_planes(shard_ffn, FFN)
    fw = w_ffn.shape[1] // 3
    w_gu, w_dn = w_ffn[:, : 2 * fw], w_ffn[:, 2 * fw :]
    kv = dot(memory, w_cross[:, hw : 3 * hw], 1, 0).astype(BF)
    q = dot(normed_cross, w_cross[:, :hw], 1, 0).astype(BF)
    cross_args = ((q, 0, hw), (kv, 0, hw), (kv, 1, hw))
    mixed_cross = attend(False, *cross_ids, *cross_args)
    after_cross = after_self + reduce_rows(dot(mixed_cross, w_cross[:, 3 * hw :], 1, 1), ATTN)
    normed, scale_ffn = rms(after_cross, gain_third)
    normed_ffn = rows_of(normed, FFN)
    gu = dot(normed_ffn, w_gu, 1, 0)
    gate, up = gu[:, :fw], gu[:, fw:]
    value, slope = gelu_parts(gate)
    hidden = (value * up).astype(BF)

    term_down = dot(grad_rows, hidden, 0, 0).astype(BF)
    grad_hidden = dot(grad_rows, w_dn, 1, 0)
    grad_gu = jnp.concatenate(
        [(grad_hidden * up * slope).astype(BF), (grad_hidden * value).astype(BF)], axis=1
    )
    term_gu = dot(normed_ffn, grad_gu, 0, 0).astype(BF)
    grad_gu, term_down, term_gu = tie(grad_gu, term_down, term_gu)
    (grad_w_down,) = scatter_weights(term_down, [fw], FFN)
    grad_w_gate, grad_w_up = scatter_weights(term_gu, [fw, fw], FFN)
    grad_normed = reduce_rows(dot(grad_gu, w_gu, 1, 1), FFN)
    grad, gain_grad_ffn = rms_back(after_cross, scale_ffn, gain_third, grad_normed)
    grad_after_cross = grad_out.astype(F32) + grad
    branch = rows_of(grad_after_cross.astype(BF), ATTN)
    branch, hidden = tie(branch, hidden)
    output = after_cross + reduce_rows(dot(hidden, w_dn, 1, 1), FFN)
    term_o = dot(branch, mixed_cross, 0, 0).astype(BF)
    grad_mixed = dot(branch, w_cross[:, 3 * hw :], 1, 0).astype(BF)
    grad_q, grad_kv = attend_back(False, *cross_ids, *cross_args, grad_mixed)
    term_q = dot(normed_cross, grad_q, 0, 0).astype(BF)
    term_kv = dot(memory, grad_kv, 0, 0).astype(BF)
    grad_normed = reduce_rows(dot(grad_q, w_cross[:, :hw], 1, 1), ATTN)
    grad_wq_cross, grad_wk_cross, grad_wv_cross, grad_wo_cross = scatter_weights(
        jnp.concatenate([term_q, term_kv, term_o], axis=1), [hw] * 4, ATTN
    )
    grad, gain_grad_cross = rms_back(after_self, scale_cross, gain_second, grad_normed)
    grad_after_self = grad_after_cross + grad
    branch = rows_of(grad_after_self.astype(BF), ATTN)
    branch, grad_kv = tie(branch, grad_kv)
    grad_memory = reduce_rows(dot(grad_kv, w_cross[:, hw : 3 * hw], 1, 1), ATTN)
    grad_patches = grad_memory.reshape(patches.shape)
    term_o = dot(branch, mixed_self, 0, 0).astype(BF)
    grad_mixed = dot(branch, w_self[:, 3 * hw :], 1, 0).astype(BF)
    grad_q, grad_kv = attend_back(True, *self_ids, *self_args, grad_mixed)
    grad_qkv = jnp.concatenate([grad_q, grad_kv], axis=1)
    term_qkv = dot(normed_self, grad_qkv, 0, 0).astype(BF)
    term_self = jnp.concatenate([term_qkv, term_o], axis=1)
    grad_qkv, term_self = tie(grad_qkv, term_self)
    grad_wq_self, grad_wk_self, grad_wv_self, grad_wo_self = scatter_weights(
        term_self, [hw] * 4, ATTN
    )
    grad_normed = reduce_rows(dot(grad_qkv, w_self[:, : 3 * hw], 1, 1), ATTN)
    grad, gain_grad_self = rms_back(start, scale_self, gain_first, grad_normed)
    grad_inputs = grad_after_self + grad

    gain_grads = jnp.concatenate([gain_grad_self, gain_grad_cross, gain_grad_ffn], axis=0)
    gain_grads, grad_w_down, grad_wo_cross = tie(gain_grads, grad_w_down, grad_wo_cross)
    bit = 1
    while bit < dp:
        gain_grads = gain_grads + swap(gain_grads, bit)
        bit *= 2
    held = lax.dynamic_slice_in_dim(gain_grads, place * part, part, axis=1)

    return (
        output,
        grad_inputs,
        grad_patches,
        held[0],
        grad_wq_self,
        grad_wk_self,
        grad_wv_self,
        grad_wo_self.T,
        held[1],
        grad_wq_cross,
        grad_wk_cross,
        grad_wv_cross,
        grad_wo_cross.T,
        held[2],
        grad_w_gate,
        grad_w_up,
        grad_w_down.T,
    )


def solution(mesh):
    rows, cut, turned, gain = P("dp", None), P("dp", "mp"), P("mp", "dp"), P("dp")
    attention = (gain, cut, cut, cut, turned)
    weights = attention + attention + (gain, cut, cut, turned)
    return jax.shard_map(
        on_device,
        mesh=mesh,
        in_specs=(rows, rows, rows, P("dp", None, None), rows) + weights,
        out_specs=(rows, rows, P("dp", None, None)) + weights,
        check_vma=False,
    )
```

time: 831 us -> 725 us (0.87)
  waiting for transfers between devices: 561 us -> 430 us
  matrix products: 47.4 us -> 66.9 us
  starting transfers between devices: 57.3 us -> 76.3 us
  Pallas kernels: 34.6 us -> 20.4 us
  between operations: 4.25 us -> 16.1 us
    ppermute x104 -> x39, waiting for transfers between devices: 551 us -> 198 us  [swap(): return lax.ppermute(value, 'dp', [(i, i ^ distance) for i in range(dp)])]
    all_gather x0 -> x3, waiting for transfers between devices: none -> 82.4 us  [over_planes(): lax.all_gather(shard, 'dp', axis_index_groups=planes(inner), tiled=True)]
    reduce_scatter x0 -> x4, waiting for transfers between devices: none -> 52.6 us  [scatter_weights(): lax.psum_scatter(whole, 'dp', axis_index_groups=planes(inner), tiled=True)]
    ppermute x7, waiting for transfers between devices: 10.3 us -> 55.3 us  [swap_mp(): return lax.ppermute(value, 'mp', [(0, 1), (1, 0)])]
    all_to_all x0 -> x7, waiting for transfers between devices: none -> 41.2 us  [exchange(): lax.all_to_all(blocks, 'dp', 0, 0, axis_index_groups=groups, tiled=True)]
    all_to_all x0 -> x7, starting transfers between devices: none -> 25 us  [exchange(): lax.all_to_all(blocks, 'dp', 0, 0, axis_index_groups=groups, tiled=True)]
    dot_general x21, matrix products: 47.4 us -> 66.9 us  [dot(): lax.dot_general(a, b, (((da,), (db,)), ((), ())), preferred_element_type=...]
    ppermute x104 -> x39, starting transfers between devices: 46.4 us -> 31.7 us  [swap(): return lax.ppermute(value, 'dp', [(i, i ^ distance) for i in range(dp)])]
  transfers between devices with their start and end apart: 111 -> 60, of which waited for: 66 -> 37; matrix products, arithmetic and copies ran while one was open for 15% -> 18% of each run, Pallas kernels for 3% -> 3%
where the time goes in v2:
time: 725 us; the launch traced here: 714 us
  waiting for transfers between devices  430 us (59%)
  starting transfers between devices  76.3 us (11%)
  matrix products  66.9 us (9%)
  other arithmetic  57.6 us (8%)
  local copies, waits for them, and re-layouts  46.5 us (6%)
  Pallas kernels  20.4 us (3%)
  between operations  16.1 us (2%)
    ppermute x39, waiting for transfers between devices, swap(): return lax.ppermute(value, 'dp', [(i, i ^ distance) for i in range(dp)])  198 us
    all_gather x3, waiting for transfers between devices, over_planes(): lax.all_gather(shard, 'dp', axis_index_groups=planes(inner), tiled=True)  82.4 us
    dot_general x21, matrix products, dot(): lax.dot_general(a, b, (((da,), (db,)), ((), ())), preferred_element_type=...  66.9 us
    ppermute x7, waiting for transfers between devices, swap_mp(): return lax.ppermute(value, 'mp', [(0, 1), (1, 0)])  55.3 us
    reduce_scatter x4, waiting for transfers between devices, scatter_weights(): lax.psum_scatter(whole, 'dp', axis_index_groups=planes(inner), tiled=True)  52.6 us
    all_to_all x7, waiting for transfers between devices, exchange(): lax.all_to_all(blocks, 'dp', 0, 0, axis_index_groups=groups, tiled=True)  41.2 us
    ppermute x39, starting transfers between devices, swap(): return lax.ppermute(value, 'dp', [(i, i ^ distance) for i in range(dp)])  31.7 us
    all_to_all x7, starting transfers between devices, exchange(): lax.all_to_all(blocks, 'dp', 0, 0, axis_index_groups=groups, tiled=True)  25 us
  transfers between devices with their start and end apart: 60, of which 37 were waited for; matrix products, arithmetic and copies ran while one was open for 18% of the time, Pallas kernels for 3%

profile of v2, /device:TPU:0, one launch (start us, length us, event | category | flops | bytes accessed | tf_op | source)
XLA Modules:
  0.0 714.2 jit_solution(9475392628763010725)
XLA Ops:
  29.6 6.4 all-to-all-done
  48.4 14.4 %all-to-all-done.1 = bf16[4,128,1024]{2,1,0:T(8,128)(2,1)S(1)} async-done(((bf16[4,128,1024]{2,1,0:T(8,128)(2,1)}), bf16[4,128,1024]{2,1,0:T(8,128)(2,1)S(1)}, u32[]{:S(2)}, u32[]{:S(2)}) %all-to-all-start.1) | async-done | bytes 1048608 | tf_op jit(solution)/shard_map/all_to_all | solution.py:205
  69.6 33.7 %collective-permute-done.2 = bf16[128,2048]{1,0:T(8,128)(2,1)S(1)} collective-permute-done((bf16[128,2048]{1,0:T(8,128)(2,1)S(1)}, bf16[128,2048]{1,0:T(8,128)(2,1)S(1)}, u32[]{:S(2)}, u32[]{:S(2)}) %collective-permute-start.2) | collective-permute-done | bytes 524320 | tf_op jit(solution)/shard_map/ppermute | solution.py:178
  104.7 10.0 %collective-permute-done.4 = bf16[128,2048]{1,0:T(8,128)(2,1)} collective-permute-done((bf16[128,2048]{1,0:T(8,128)(2,1)}, bf16[128,2048]{1,0:T(8,128)(2,1)}, u32[]{:S(2)}, u32[]{:S(2)}) %collective-permute-start.4) | collective-permute-done | bytes 524320 | tf_op jit(solution)/shard_map/ppermute | solution.py:178
  117.0 8.4 %collective-permute-done.6 = bf16[128,2048]{1,0:T(8,128)(2,1)} collective-permute-done((bf16[128,2048]{1,0:T(8,128)(2,1)S(1)}, bf16[128,2048]{1,0:T(8,128)(2,1)}, u32[]{:S(2)}, u32[]{:S(2)}) %collective-permute-start.6) | collective-permute-done | bytes 524320 | tf_op jit(solution)/shard_map/ppermute | solution.py:178
  151.2 13.8 %collective-permute-done.14 = bf16[128,2048]{1,0:T(8,128)(2,1)S(1)} collective-permute-done((bf16[128,2048]{1,0:T(8,128)(2,1)S(1)}, bf16[128,2048]{1,0:T(8,128)(2,1)S(1)}, u32[]{:S(2)}, u32[]{:S(2)}) %collective-permute-start.14) | collective-permute-done | bytes 524320 | tf_op jit(solution)/shard_map/ppermute | solution.py:178
  167.1 11.8 %collective-permute-done.15 = bf16[128,2048]{1,0:T(8,128)(2,1)S(1)} collective-permute-done((bf16[128,2048]{1,0:T(8,128)(2,1)S(1)}, bf16[128,2048]{1,0:T(8,128)(2,1)S(1)}, u32[]{:S(2)}, u32[]{:S(2)}) %collective-permute-start.15) | collective-permute-done | bytes 524320 | tf_op jit(solution)/shard_map/ppermute | solution.py:181
  179.9 12.3 %collective-permute-done.16 = bf16[128,2048]{1,0:T(8,128)(2,1)S(1)} collective-permute-done((bf16[128,2048]{1,0:T(8,128)(2,1)S(1)}, bf16[128,2048]{1,0:T(8,128)(2,1)S(1)}, u32[]{:S(2)}, u32[]{:S(2)}) %collective-permute-start.16) | collective-permute-done | bytes 524320 | tf_op jit(solution)/shard_map/ppermute | solution.py:178
  194.3 5.7 all-gather.6.cloned.1.call-done
  220.7 12.5 %collective-permute-done.19 = bf16[128,2048]{1,0:T(8,128)(2,1)S(1)} collective-permute-done((bf16[128,2048]{1,0:T(8,128)(2,1)S(1)}, bf16[128,2048]{1,0:T(8,128)(2,1)S(1)}, u32[]{:S(2)}, u32[]{:S(2)}) %collective-permute-start.19) | collective-permute-done | bytes 524320 | tf_op jit(solution)/shard_map/ppermute | solution.py:178
  235.0 11.7 %collective-permute-done.20 = bf16[128,2048]{1,0:T(8,128)(2,1)S(1)} collective-permute-done((bf16[128,2048]{1,0:T(8,128)(2,1)S(1)}, bf16[128,2048]{1,0:T(8,128)(2,1)S(1)}, u32[]{:S(2)}, u32[]{:S(2)}) %collective-permute-start.20) | collective-permute-done | bytes 524320 | tf_op jit(solution)/shard_map/ppermute | solution.py:181
  249.0 10.8 %collective-permute-done.21 = bf16[128,2048]{1,0:T(8,128)(2,1)S(1)} collective-permute-done((bf16[128,2048]{1,0:T(8,128)(2,1)S(1)}, bf16[128,2048]{1,0:T(8,128)(2,1)S(1)}, u32[]{:S(2)}, u32[]{:S(2)}) %collective-permute-start.21) | collective-permute-done | bytes 524320 | tf_op jit(solution)/shard_map/ppermute | solution.py:178
  264.4 76.7 %all-gather.8.cloned.1.call-done = bf16[2048,1920]{1,0:T(8,128)(2,1)} async-done(((bf16[512,1920]{1,0:T(8,128)(2,1)}), bf16[2048,1920]{1,0:T(8,128)(2,1)}) %all-gather.8.cloned.1.call-update) | async-done | bytes 7864336 | tf_op jit(solution)/shard_map/all_gather | solution.py:223
  341.1 6.1 fusion.2
  359.5 6.5 convolution_convert_fusion
  366.6 10.0 %reduce-scatter.7.cloned.1.call-start = ((), (), s32[]{:S(2)}) async-start(), calls=%async_computation.15 | async-start | bytes 5242880 | tf_op jit(solution)/shard_map/reduce_scatter | solution.py:226
  376.7 5.8 fusion.7
  387.1 12.5 %collective-permute-done.24 = bf16[128,2048]{1,0:T(8,128)(2,1)S(1)} collective-permute-done((bf16[128,2048]{1,0:T(8,128)(2,1)S(1)}, bf16[128,2048]{1,0:T(8,128)(2,1)S(1)}, u32[]{:S(2)}, u32[]{:S(2)}) %collective-permute-start.24) | collective-permute-done | bytes 524320 | tf_op jit(solution)/shard_map/ppermute | solution.py:178
  401.4 11.8 %collective-permute-done.25 = bf16[128,2048]{1,0:T(8,128)(2,1)S(1)} collective-permute-done((bf16[128,2048]{1,0:T(8,128)(2,1)S(1)}, bf16[128,2048]{1,0:T(8,128)(2,1)S(1)}, u32[]{:S(2)}, u32[]{:S(2)}) %collective-permute-start.25) | collective-permute-done | bytes 524320 | tf_op jit(solution)/shard_map/ppermute | solution.py:181
  416.5 11.0 %collective-permute-done.26 = bf16[128,2048]{1,0:T(8,128)(2,1)S(1)} collective-permute-done((bf16[128,2048]{1,0:T(8,128)(2,1)S(1)}, bf16[128,2048]{1,0:T(8,128)(2,1)S(1)}, u32[]{:S(2)}, u32[]{:S(2)}) %collective-permute-start.26) | collective-permute-done | bytes 524320 | tf_op jit(solution)/shard_map/ppermute | solution.py:178
  456.2 6.4 collective-permute-done.32
  465.8 11.4 %collective-permute-done.33 = bf16[128,2048]{1,0:T(8,128)(2,1)S(1)} collective-permute-done((bf16[128,2048]{1,0:T(8,128)(2,1)S(1)}, bf16[128,2048]{1,0:T(8,128)(2,1)S(1)}, u32[]{:S(2)}, u32[]{:S(2)}) %collective-permute-start.33) | collective-permute-done | bytes 524320 | tf_op jit(solution)/shard_map/ppermute | solution.py:181
  480.5 10.8 %collective-permute-done.34 = bf16[128,2048]{1,0:T(8,128)(2,1)S(1)} collective-permute-done((bf16[128,2048]{1,0:T(8,128)(2,1)S(1)}, bf16[128,2048]{1,0:T(8,128)(2,1)S(1)}, u32[]{:S(2)}, u32[]{:S(2)}) %collective-permute-start.34) | collective-permute-done | bytes 524320 | tf_op jit(solution)/shard_map/ppermute | solution.py:178
  500.9 7.8 %collective-permute-done.29 = bf16[128,2048]{1,0:T(8,128)(2,1)} collective-permute-done((bf16[128,2048]{1,0:T(8,128)(2,1)}, bf16[128,2048]{1,0:T(8,128)(2,1)}, u32[]{:S(2)}, u32[]{:S(2)}) %collective-permute-start.29) | collective-permute-done | bytes 524320 | tf_op jit(solution)/shard_map/ppermute | solution.py:178
  518.2 5.7 shard_map.317
  548.7 11.3 %collective-permute-done.37 = bf16[128,2048]{1,0:T(8,128)(2,1)S(1)} collective-permute-done((bf16[128,2048]{1,0:T(8,128)(2,1)S(1)}, bf16[128,2048]{1,0:T(8,128)(2,1)S(1)}, u32[]{:S(2)}, u32[]{:S(2)}) %collective-permute-start.37) | collective-permute-done | bytes 524320 | tf_op jit(solution)/shard_map/ppermute | solution.py:178
  564.5 6.4 collective-permute-done.40
  580.0 6.2 collective-permute-done.41
  590.0 7.3 %all-to-all-done.6 = bf16[4,128,1280]{2,1,0:T(8,128)(2,1)S(1)} async-done(((bf16[4,128,1280]{2,1,0:T(8,128)(2,1)}), bf16[4,128,1280]{2,1,0:T(8,128)(2,1)S(1)}, u32[]{:S(2)}, u32[]{:S(2)}) %all-to-all-start.6) | async-done | bytes 1310752 | tf_op jit(solution)/shard_map/all_to_all | solution.py:205
  604.6 13.2 %all-to-all-done.4 = bf16[4,128,1024]{1,2,0:T(8,128)(2,1)S(1)} async-done(((bf16[4,128,1024]{1,2,0:T(8,128)(2,1)}), bf16[4,128,1024]{1,2,0:T(8,128)(2,1)S(1)}, u32[]{:S(2)}, u32[]{:S(2)}) %all-to-all-start.4) | async-done | bytes 1048608 | tf_op jit(solution)/shard_map/all_to_all | solution.py:205
  618.8 52.5 %reduce-scatter.9.cloned.1.call-done = bf16[512,1024]{0,1:T(8,128)(2,1)} async-done(((bf16[2048,1024]{0,1:T(8,128)(2,1)}), bf16[512,1024]{0,1:T(8,128)(2,1)}) %reduce-scatter.9.cloned.1.call-update) | async-done | bytes 1048592 | tf_op jit(solution)/shard_map/reduce_scatter | solution.py:226
  680.5 11.8 %collective-permute-done.43 = f32[3,2048]{1,0:T(4,128)S(1)} collective-permute-done((f32[3,2048]{1,0:T(4,128)S(1)}, f32[3,2048]{1,0:T(4,128)S(1)}, u32[]{:S(2)}, u32[]{:S(2)}) %collective-permute-start.43) | collective-permute-done | bytes 24608 | tf_op jit(solution)/shard_map/ppermute | solution.py:178
  (426 shorter events, 255.5 us)
Async XLA Ops:
  7.9 31.8 %collective-permute-start.8 = (f32[3,128]{1,0:T(4,128)S(1)}, f32[3,128]{1,0:T(4,128)S(1)}, u32[]{:S(2)}, u32[]{:S(2)}) collective-permute-start(f32[3,128]{1,0:T(4,128)S(1)} %maximum_convert_fusion.11), channel_id=1, source_target_pairs={{0,8},{2,10},{4,12},{6,14},{8,0},{10,2},{12,4},{14,6},{16,24},{18,... | collective-permute-start | bytes 4616 | tf_op jit(solution)/shard_map/ppermute | solution.py:178
  11.0 28.8 %collective-permute-start.9 = (f32[3,128]{1,0:T(4,128)S(1)}, f32[3,128]{1,0:T(4,128)S(1)}, u32[]{:S(2)}, u32[]{:S(2)}) collective-permute-start(f32[3,128]{1,0:T(4,128)S(1)} %maximum_convert_fusion.11), channel_id=1, source_target_pairs={{0,16},{2,18},{4,20},{6,22},{8,24},{10,26},{12,28},{14,30},{16,0},... | collective-permute-start | bytes 4616 | tf_op jit(solution)/shard_map/ppermute | solution.py:178
  13.6 26.2 %collective-permute-start.10 = (f32[3,128]{1,0:T(4,128)S(1)}, f32[3,128]{1,0:T(4,128)S(1)}, u32[]{:S(2)}, u32[]{:S(2)}) collective-permute-start(f32[3,128]{1,0:T(4,128)S(1)} %maximum_convert_fusion.11), channel_id=1, source_target_pairs={{0,24},{2,26},{4,28},{6,30},{8,16},{10,18},{12,20},{14,22},{16,8},... | collective-permute-start | bytes 4616 | tf_op jit(solution)/shard_map/ppermute | solution.py:178
  17.9 18.1 %all-to-all-start = ((bf16[4,128,1024]{2,1,0:T(8,128)(2,1)}), bf16[4,128,1024]{2,1,0:T(8,128)(2,1)S(1)}, u32[]{:S(2)}, u32[]{:S(2)}) async-start(bf16[4,128,1024]{2,1,0:T(8,128)(2,1)} %pad_maximum_fusion.11), calls=%async_computation | async-start | bytes 2097152 | tf_op jit(solution)/shard_map/all_to_all | solution.py:205
  21.6 114.8 %all-gather.4.cloned.1.call-start = ((), (), s32[]{:S(2)}) async-start(), calls=%async_computation.11 | async-start | bytes 5242880 | tf_op jit(solution)/shard_map/all_gather | solution.py:223
  23.5 16.2 %collective-permute-start = (s32[1,2,128]{2,1,0:T(2,128)S(1)}, s32[1,2,128]{2,1,0:T(2,128)S(1)}, u32[]{:S(2)}, u32[]{:S(2)}) collective-permute-start(s32[1,2,128]{2,1,0:T(2,128)S(1)} %get-tuple-element.272), channel_id=1, source_target_pairs={{0,4},{2,6},{4,0},{6,2},{8,12},{10,14},{12,8},{14,10},{16,20},{18,... | collective-permute-start | bytes 3080 | tf_op jit(solution)/shard_map/ppermute | solution.py:178
  44.8 18.0 %all-to-all-start.1 = ((bf16[4,128,1024]{2,1,0:T(8,128)(2,1)}), bf16[4,128,1024]{2,1,0:T(8,128)(2,1)S(1)}, u32[]{:S(2)}, u32[]{:S(2)}) async-start(bf16[4,128,1024]{2,1,0:T(8,128)(2,1)} %pad_maximum_fusion.12), calls=%async_computation.1 | async-start | bytes 2097152 | tf_op jit(solution)/shard_map/all_to_all | solution.py:205
  63.7 40.7 %all-to-all-start.2 = ((bf16[4,128,1920]{2,1,0:T(8,128)(2,1)}), bf16[4,128,1920]{2,1,0:T(8,128)(2,1)S(1)}, u32[]{:S(2)}, u32[]{:S(2)}) async-start(bf16[4,128,1920]{2,1,0:T(8,128)(2,1)} %pad_maximum_fusion.9), calls=%async_computation.2 | async-start | bytes 3932160 | tf_op jit(solution)/shard_map/all_to_all | solution.py:205
  67.3 132.6 %all-gather.6.cloned.1.call-start = ((), (), s32[]{:S(2)}) async-start(), calls=%async_computation.12 | async-start | bytes 5242880 | tf_op jit(solution)/shard_map/all_gather | solution.py:223
  67.4 35.9 %collective-permute-start.2 = (bf16[128,2048]{1,0:T(8,128)(2,1)S(1)}, bf16[128,2048]{1,0:T(8,128)(2,1)S(1)}, u32[]{:S(2)}, u32[]{:S(2)}) collective-permute-start(bf16[128,2048]{1,0:T(8,128)(2,1)S(1)} %copy-done), channel_id=1, source_target_pairs={{0,4},{2,6},{4,0},{6,2},{8,12},{10,14},{12,8},{14,10},{16,20},{18,... | collective-permute-start | bytes 1572872 | tf_op jit(solution)/shard_map/ppermute | solution.py:178
  69.4 45.2 %collective-permute-start.4 = (bf16[128,2048]{1,0:T(8,128)(2,1)}, bf16[128,2048]{1,0:T(8,128)(2,1)}, u32[]{:S(2)}, u32[]{:S(2)}) collective-permute-start(bf16[128,2048]{1,0:T(8,128)(2,1)} %bitcast.358), channel_id=1, source_target_pairs={{0,4},{2,6},{4,0},{6,2},{8,12},{10,14},{12,8},{14,10},{16,20},{18,... | collective-permute-start | bytes 1572872 | tf_op jit(solution)/shard_map/ppermute | solution.py:178
  104.5 22.3 %collective-permute-start.3 = (bf16[2,128,2048]{2,1,0:T(8,128)(2,1)}, bf16[2,128,2048]{2,1,0:T(8,128)(2,1)}, u32[]{:S(2)}, u32[]{:S(2)}) collective-permute-start(bf16[2,128,2048]{2,1,0:T(8,128)(2,1)} %pad_maximum_fusion.13), channel_id=1, source_target_pairs={{0,2},{2,0},{4,6},{6,4},{8,10},{10,8},{12,14},{14,12},{16,18},{18,... | collective-permute-start | bytes 3145736 | tf_op jit(solution)/shard_map/ppermute | solution.py:178
  104.5 20.9 %collective-permute-start.6 = (bf16[128,2048]{1,0:T(8,128)(2,1)S(1)}, bf16[128,2048]{1,0:T(8,128)(2,1)}, u32[]{:S(2)}, u32[]{:S(2)}) collective-permute-start(bf16[128,2048]{1,0:T(8,128)(2,1)S(1)} %copy-done.5), channel_id=1, source_target_pairs={{0,4},{2,6},{4,0},{6,2},{8,12},{10,14},{12,8},{14,10},{16,20},{18,... | collective-permute-start | bytes 1572872 | tf_op jit(solution)/shard_map/ppermute | solution.py:178
  117.0 224.2 %all-gather.8.cloned.1.call-start = ((), (), s32[]{:S(2)}) async-start(), calls=%async_computation.13 | async-start | bytes 9830400 | tf_op jit(solution)/shard_map/all_gather | solution.py:223
  150.8 14.3 %collective-permute-start.14 = (bf16[128,2048]{1,0:T(8,128)(2,1)S(1)}, bf16[128,2048]{1,0:T(8,128)(2,1)S(1)}, u32[]{:S(2)}, u32[]{:S(2)}) collective-permute-start(bf16[128,2048]{1,0:T(8,128)(2,1)S(1)} %fusion.57), channel_id=1, source_target_pairs={{0,4},{2,6},{4,0},{6,2},{8,12},{10,14},{12,8},{14,10},{16,20},{18,... | collective-permute-start | bytes 1572872 | tf_op jit(solution)/shard_map/ppermute | solution.py:178
  179.4 315.7 %reduce-scatter.5.cloned.1.call-start = ((), (), s32[]{:S(2)}) async-start(), calls=%async_computation.14 | async-start | bytes 3276800 | tf_op jit(solution)/shard_map/reduce_scatter | solution.py:226
  366.0 210.3 %reduce-scatter.11.cloned.1.call-start = ((), (), s32[]{:S(2)}) async-start(), calls=%async_computation.17 | async-start | bytes 6553600 | tf_op jit(solution)/shard_map/reduce_scatter | solution.py:226
  366.6 230.8 %reduce-scatter.7.cloned.1.call-start = ((), (), s32[]{:S(2)}) async-start(), calls=%async_computation.15 | async-start | bytes 5242880 | tf_op jit(solution)/shard_map/reduce_scatter | solution.py:226
  448.5 14.1 %collective-permute-start.32 = (bf16[128,2048]{1,0:T(8,128)(2,1)S(1)}, bf16[128,2048]{1,0:T(8,128)(2,1)}, u32[]{:S(2)}, u32[]{:S(2)}) collective-permute-start(bf16[128,2048]{1,0:T(8,128)(2,1)S(1)} %fusion.45), channel_id=1, source_target_pairs={{0,4},{2,6},{4,0},{6,2},{8,12},{10,14},{12,8},{14,10},{16,20},{18,... | collective-permute-start | bytes 1572872 | tf_op jit(solution)/shard_map/ppermute | solution.py:178
  465.7 26.7 %collective-permute-start.28 = (bf16[2,128,2048]{2,1,0:T(8,128)(2,1)S(1)}, bf16[2,128,2048]{2,1,0:T(8,128)(2,1)S(1)}, u32[]{:S(2)}, u32[]{:S(2)}) collective-permute-start(bf16[2,128,2048]{2,1,0:T(8,128)(2,1)S(1)} %pad_maximum_fusion.22), channel_id=1, source_target_pairs={{0,2},{2,0},{4,6},{6,4},{8,10},{10,8},{12,14},{14,12},{16,18},{18,... | collective-permute-start | bytes 3145736 | tf_op jit(solution)/shard_map/ppermute | solution.py:178
  492.5 20.1 %collective-permute-start.35 = (bf16[2,128,2048]{2,1,0:T(8,128)(2,1)}, bf16[2,128,2048]{2,1,0:T(8,128)(2,1)}, u32[]{:S(2)}, u32[]{:S(2)}) collective-permute-start(bf16[2,128,2048]{2,1,0:T(8,128)(2,1)} %pad_maximum_fusion.24), channel_id=1, source_target_pairs={{0,2},{2,0},{4,6},{6,4},{8,10},{10,8},{12,14},{14,12},{16,18},{18,... | collective-permute-start | bytes 3145736 | tf_op jit(solution)/shard_map/ppermute | solution.py:178
  493.6 15.0 %collective-permute-start.29 = (bf16[128,2048]{1,0:T(8,128)(2,1)}, bf16[128,2048]{1,0:T(8,128)(2,1)}, u32[]{:S(2)}, u32[]{:S(2)}) collective-permute-start(bf16[128,2048]{1,0:T(8,128)(2,1)} %fusion.48), channel_id=1, source_target_pairs={{0,4},{2,6},{4,0},{6,2},{8,12},{10,14},{12,8},{14,10},{16,20},{18,... | collective-permute-start | bytes 1572872 | tf_op jit(solution)/shard_map/ppermute | solution.py:178
  497.3 46.4 %all-to-all-start.3 = ((bf16[4,128,640]{1,2,0:T(8,128)(2,1)}), bf16[4,128,640]{1,2,0:T(8,128)(2,1)S(1)}, u32[]{:S(2)}, u32[]{:S(2)}) async-start(bf16[4,128,640]{1,2,0:T(8,128)(2,1)} %copy.88), calls=%async_computation.4 | async-start | bytes 1310720 | tf_op jit(solution)/shard_map/all_to_all | solution.py:205
  500.8 170.5 %reduce-scatter.9.cloned.1.call-start = ((), (), s32[]{:S(2)}) async-start(), calls=%async_computation.16 | async-start | bytes 5242880 | tf_op jit(solution)/shard_map/reduce_scatter | solution.py:226
  511.1 51.1 %collective-permute-start.30 = (bf16[128,2048]{1,0:T(8,128)(2,1)}, bf16[128,2048]{1,0:T(8,128)(2,1)}, u32[]{:S(2)}, u32[]{:S(2)}) collective-permute-start(bf16[128,2048]{1,0:T(8,128)(2,1)} %fusion.50), channel_id=1, source_target_pairs={{0,1},{1,0},{2,3},{3,2},{4,5},{5,4},{6,7},{7,6},{8,9},{9,8},{10,11... | collective-permute-start | bytes 1572872 | tf_op jit(solution)/shard_map/ppermute | solution.py:181
  545.3 14.8 %collective-permute-start.37 = (bf16[128,2048]{1,0:T(8,128)(2,1)S(1)}, bf16[128,2048]{1,0:T(8,128)(2,1)S(1)}, u32[]{:S(2)}, u32[]{:S(2)}) collective-permute-start(bf16[128,2048]{1,0:T(8,128)(2,1)S(1)} %fusion.42), channel_id=1, source_target_pairs={{0,4},{2,6},{4,0},{6,2},{8,12},{10,14},{12,8},{14,10},{16,20},{18,... | collective-permute-start | bytes 1572872 | tf_op jit(solution)/shard_map/ppermute | solution.py:178
  548.1 22.8 %collective-permute-start.40 = (bf16[128,2048]{1,0:T(8,128)(2,1)S(1)}, bf16[128,2048]{1,0:T(8,128)(2,1)S(1)}, u32[]{:S(2)}, u32[]{:S(2)}) collective-permute-start(bf16[128,2048]{1,0:T(8,128)(2,1)S(1)} %fusion.39), channel_id=1, source_target_pairs={{0,4},{2,6},{4,0},{6,2},{8,12},{10,14},{12,8},{14,10},{16,20},{18,... | collective-permute-start | bytes 1572872 | tf_op jit(solution)/shard_map/ppermute | solution.py:178
  571.9 14.2 %collective-permute-start.41 = (bf16[128,2048]{1,0:T(8,128)(2,1)}, bf16[128,2048]{1,0:T(8,128)(2,1)}, u32[]{:S(2)}, u32[]{:S(2)}) collective-permute-start(bf16[128,2048]{1,0:T(8,128)(2,1)} %fusion.41), channel_id=1, source_target_pairs={{0,1},{1,0},{2,3},{3,2},{4,5},{5,4},{6,7},{7,6},{8,9},{9,8},{10,11... | collective-permute-start | bytes 1572872 | tf_op jit(solution)/shard_map/ppermute | solution.py:181
  576.3 20.9 %all-to-all-start.6 = ((bf16[4,128,1280]{2,1,0:T(8,128)(2,1)}), bf16[4,128,1280]{2,1,0:T(8,128)(2,1)S(1)}, u32[]{:S(2)}, u32[]{:S(2)}) async-start(bf16[4,128,1280]{2,1,0:T(8,128)(2,1)} %bitcast.364), calls=%async_computation.10 | async-start | bytes 2621440 | tf_op jit(solution)/shard_map/all_to_all | solution.py:205
  599.8 18.0 %all-to-all-start.4 = ((bf16[4,128,1024]{1,2,0:T(8,128)(2,1)}), bf16[4,128,1024]{1,2,0:T(8,128)(2,1)S(1)}, u32[]{:S(2)}, u32[]{:S(2)}) async-start(bf16[4,128,1024]{1,2,0:T(8,128)(2,1)} %copy_bitcast_fusion.1), calls=%async_computation.6 | async-start | bytes 2097152 | tf_op jit(solution)/shard_map/all_to_all | solution.py:205
  618.8 59.6 %collective-permute-start.42 = (f32[3,2048]{1,0:T(4,128)S(1)}, f32[3,2048]{1,0:T(4,128)S(1)}, u32[]{:S(2)}, u32[]{:S(2)}) collective-permute-start(f32[3,2048]{1,0:T(4,128)S(1)} %pad_maximum_fusion.31), channel_id=1, source_target_pairs={{0,2},{2,0},{4,6},{6,4},{8,10},{10,8},{12,14},{14,12},{16,18},{18,... | collective-permute-start | bytes 73736 | tf_op jit(solution)/shard_map/ppermute | solution.py:178
  673.7 29.2 %all-to-all-start.5 = ((bf16[4,128,1024]{1,2,0:T(8,128)(2,1)}), bf16[4,128,1024]{1,2,0:T(8,128)(2,1)S(1)}, u32[]{:S(2)}, u32[]{:S(2)}) async-start(bf16[4,128,1024]{1,2,0:T(8,128)(2,1)} %copy_bitcast_fusion), calls=%async_computation.8 | async-start | bytes 2097152 | tf_op jit(solution)/shard_map/all_to_all | solution.py:205
  (95 other events, 689.7 us)
Sparse Core Ops, SparseCore 0:
  37.1 81.2 all-gather.3
  120.6 79.2 all-gather.5
  201.5 139.5 all-gather.7
  366.2 50.3 reduce-scatter.4
  418.7 93.4 reduce-scatter.10
  514.3 77.2 reduce-scatter.6
  594.0 77.2 reduce-scatter.8

commit v3 on v2

--- a/solution.py
+++ b/solution.py
@@ -3,6 +3,7 @@
 import jax
 import jax.numpy as jnp
 from jax import lax
+from jax.experimental.layout import Layout, with_layout_constraint
 from jax.experimental import pallas as pl
 from jax.experimental.pallas import tpu as pltpu
 from jax.sharding import PartitionSpec as P
@@ -121,6 +122,10 @@
     )(qid, kid, q[0], k[0], v[0], g)
 
 
+def term(source, grad):
+    return with_layout_constraint(dot(source, grad, 0, 0).astype(BF), Layout((0, 1)))
+
+
 def rms(values, gain):
     scale = lax.rsqrt(jnp.mean(values * values, axis=-1, keepdims=True) + EPS)
     return (values * scale * gain).astype(BF), scale
@@ -222,9 +227,10 @@
         shard = shard.reshape(inner * part, -1)
         return lax.all_gather(shard, "dp", axis_index_groups=planes(inner), tiled=True)
 
-    def scatter_weights(whole, widths, inner):
-        held = lax.psum_scatter(whole, "dp", axis_index_groups=planes(inner), tiled=True)
-        pieces = exchange(held.reshape(inner, part, -1), inner)
+    def plane_sum(whole, inner):
+        return lax.psum_scatter(whole, "dp", axis_index_groups=planes(inner), tiled=True)
+
+    def split(pieces, widths):
         out, at = [], 0
         for w in widths:
             cut = slice(at, at + w)
@@ -232,9 +238,16 @@
             at += w
         return out
 
-    shard_self = exchange(pack([wq_self, wk_self, wv_self, wo_self.T], ATTN), ATTN)
+    def scatter_weights(whole, widths, inner):
+        held = plane_sum(whole, inner).reshape(inner, part, -1)
+        return split(exchange(held, inner), widths)
+
+    packed_self = pack([wq_self, wk_self, wv_self, wo_self.T], ATTN)
+    shard_self = exchange(packed_self, ATTN)
     packed_cross = pack([wq_cross, wk_cross, wv_cross, wo_cross.T], ATTN)
-    shard_self, inputs, packed_cross = tie(shard_self, inputs, packed_cross)
+    shard_self, inputs, packed_cross, gain_self, segments = tie(
+        shard_self, inputs, packed_cross, gain_self, segments
+    )
     w_self = over_planes(shard_self, ATTN)
     start_rows = rows_of(inputs, ATTN)
     shard_cross = exchange(packed_cross, ATTN)
@@ -296,12 +309,12 @@
     value, slope = gelu_parts(gate)
     hidden = (value * up).astype(BF)
 
-    term_down = dot(grad_rows, hidden, 0, 0).astype(BF)
+    term_down = term(grad_rows, hidden)
     grad_hidden = dot(grad_rows, w_dn, 1, 0)
     grad_gu = jnp.concatenate(
         [(grad_hidden * up * slope).astype(BF), (grad_hidden * value).astype(BF)], axis=1
     )
-    term_gu = dot(normed_ffn, grad_gu, 0, 0).astype(BF)
+    term_gu = term(normed_ffn, grad_gu)
     grad_gu, term_down, term_gu = tie(grad_gu, term_down, term_gu)
     (grad_w_down,) = scatter_weights(term_down, [fw], FFN)
     grad_w_gate, grad_w_up = scatter_weights(term_gu, [fw, fw], FFN)
@@ -311,11 +324,11 @@
     branch = rows_of(grad_after_cross.astype(BF), ATTN)
     branch, hidden = tie(branch, hidden)
     output = after_cross + reduce_rows(dot(hidden, w_dn, 1, 1), FFN)
-    term_o = dot(branch, mixed_cross, 0, 0).astype(BF)
+    term_o = term(branch, mixed_cross)
     grad_mixed = dot(branch, w_cross[:, 3 * hw :], 1, 0).astype(BF)
     grad_q, grad_kv = attend_back(False, *cross_ids, *cross_args, grad_mixed)
-    term_q = dot(normed_cross, grad_q, 0, 0).astype(BF)
-    term_kv = dot(memory, grad_kv, 0, 0).astype(BF)
+    term_q = term(normed_cross, grad_q)
+    term_kv = term(memory, grad_kv)
     grad_normed = reduce_rows(dot(grad_q, w_cross[:, :hw], 1, 1), ATTN)
     grad_wq_cross, grad_wk_cross, grad_wv_cross, grad_wo_cross = scatter_weights(
         jnp.concatenate([term_q, term_kv, term_o], axis=1), [hw] * 4, ATTN
@@ -326,22 +339,28 @@
     branch, grad_kv = tie(branch, grad_kv)
     grad_memory = reduce_rows(dot(grad_kv, w_cross[:, hw : 3 * hw], 1, 1), ATTN)
     grad_patches = grad_memory.reshape(patches.shape)
-    term_o = dot(branch, mixed_self, 0, 0).astype(BF)
+    term_o = term(branch, mixed_self)
     grad_mixed = dot(branch, w_self[:, 3 * hw :], 1, 0).astype(BF)
     grad_q, grad_kv = attend_back(True, *self_ids, *self_args, grad_mixed)
     grad_qkv = jnp.concatenate([grad_q, grad_kv], axis=1)
-    term_qkv = dot(normed_self, grad_qkv, 0, 0).astype(BF)
+    term_qkv = term(normed_self, grad_qkv)
     term_self = jnp.concatenate([term_qkv, term_o], axis=1)
     grad_qkv, term_self = tie(grad_qkv, term_self)
-    grad_wq_self, grad_wk_self, grad_wv_self, grad_wo_self = scatter_weights(
-        term_self, [hw] * 4, ATTN
-    )
+    term_self = lax.all_to_all(
+        term_self.reshape(-1, ATTN, part, 4 * hw),
+        "dp",
+        1,
+        1,
+        axis_index_groups=[[m + ATTN * i for m in range(ATTN)] for i in range(dp // ATTN)],
+        tiled=True,
+    )
+    term_self = plane_sum(term_self.reshape(width, -1), ATTN).reshape(ATTN, part, -1)
+    grad_wq_self, grad_wk_self, grad_wv_self, grad_wo_self = split(term_self, [hw] * 4)
     grad_normed = reduce_rows(dot(grad_qkv, w_self[:, : 3 * hw], 1, 1), ATTN)
     grad, gain_grad_self = rms_back(start, scale_self, gain_first, grad_normed)
     grad_inputs = grad_after_self + grad
 
     gain_grads = jnp.concatenate([gain_grad_self, gain_grad_cross, gain_grad_ffn], axis=0)
-    gain_grads, grad_w_down, grad_wo_cross = tie(gain_grads, grad_w_down, grad_wo_cross)
     bit = 1
     while bit < dp:
         gain_grads = gain_grads + swap(gain_grads, bit)

time: 725 us -> 694 us (0.957)
  waiting for transfers between devices: 430 us -> 390 us
    reduce_scatter x4, waiting for transfers between devices: 52.6 us -> 1.59 us  [plane_sum(): lax.psum_scatter(whole, 'dp', axis_index_groups=planes(inner), tiled=True)]
    all_to_all x0 -> x1, waiting for transfers between devices: none -> 34.4 us  [on_device(): lax.all_to_all(term_self.reshape(-1, ATTN, part, 4 * hw), 'dp', 1, 1, axi...]
    ppermute x39, waiting for transfers between devices: 198 us -> 169 us  [swap(): return lax.ppermute(value, 'dp', [(i, i ^ distance) for i in range(dp)])]
    all_to_all x7 -> x6, waiting for transfers between devices: 41.2 us -> 48.2 us  [exchange(): lax.all_to_all(blocks, 'dp', 0, 0, axis_index_groups=groups, tiled=True)]
    all_to_all x7 -> x6, starting transfers between devices: 25 us -> 22.5 us  [exchange(): lax.all_to_all(blocks, 'dp', 0, 0, axis_index_groups=groups, tiled=True)]
    unnamed x144 -> x158, local copies, waits for them, and re-layouts: 22.2 us -> 20.2 us
  transfers between devices with their start and end apart: 60 -> 60, of which waited for: 37 -> 37; matrix products, arithmetic and copies ran while one was open for 18% -> 20% of each run, Pallas kernels for 3% -> 3%
where the time goes in v3:
time: 694 us; the launch traced here: 683 us
  waiting for transfers between devices  390 us (56%)
  starting transfers between devices  73.4 us (11%)
  matrix products  67 us (10%)
  other arithmetic  63.9 us (9%)
  local copies, waits for them, and re-layouts  52.2 us (8%)
  Pallas kernels  20.1 us (3%)
  between operations  16.2 us (2%)
    ppermute x39, waiting for transfers between devices, swap(): return lax.ppermute(value, 'dp', [(i, i ^ distance) for i in range(dp)])  169 us
    all_gather x3, waiting for transfers between devices, over_planes(): lax.all_gather(shard, 'dp', axis_index_groups=planes(inner), tiled=True)  80 us
    dot_general x21, matrix products, dot(): lax.dot_general(a, b, (((da,), (db,)), ((), ())), preferred_element_type=...  67 us
    ppermute x7, waiting for transfers between devices, swap_mp(): return lax.ppermute(value, 'mp', [(0, 1), (1, 0)])  56.4 us
    all_to_all x6, waiting for transfers between devices, exchange(): lax.all_to_all(blocks, 'dp', 0, 0, axis_index_groups=groups, tiled=True)  48.2 us
    all_to_all x1, waiting for transfers between devices, on_device(): lax.all_to_all(term_self.reshape(-1, ATTN, part, 4 * hw), 'dp', 1, 1, axi...  34.4 us
    ppermute x39, starting transfers between devices, swap(): return lax.ppermute(value, 'dp', [(i, i ^ distance) for i in range(dp)])  26.6 us
    all_to_all x6, starting transfers between devices, exchange(): lax.all_to_all(blocks, 'dp', 0, 0, axis_index_groups=groups, tiled=True)  22.5 us
  transfers between devices with their start and end apart: 60, of which 37 were waited for; matrix products, arithmetic and copies ran while one was open for 20% of the time, Pallas kernels for 3%

profile of v3, /device:TPU:0, one launch (start us, length us, event | category | flops | bytes accessed | tf_op | source)
XLA Modules:
  0.0 682.6 jit_solution(11410105012112866489)
XLA Ops:
  22.8 7.6 %all-to-all-done = bf16[4,128,1024]{2,1,0:T(8,128)(2,1)S(1)} async-done(((bf16[4,128,1024]{2,1,0:T(8,128)(2,1)}), bf16[4,128,1024]{2,1,0:T(8,128)(2,1)S(1)}, u32[]{:S(2)}, u32[]{:S(2)}) %all-to-all-start) | async-done | bytes 1048608 | tf_op jit(solution)/shard_map/all_to_all | solution.py:210
  45.6 22.3 %collective-permute-done = s32[1,2,128]{2,1,0:T(2,128)S(1)} collective-permute-done((s32[1,2,128]{2,1,0:T(2,128)S(1)}, s32[1,2,128]{2,1,0:T(2,128)S(1)}, u32[]{:S(2)}, u32[]{:S(2)}) %collective-permute-start) | collective-permute-done | bytes 1056 | tf_op jit(solution)/shard_map/ppermute | solution.py:183
  81.8 20.5 %all-to-all-done.2 = bf16[4,128,1920]{2,1,0:T(8,128)(2,1)S(1)} async-done(((bf16[4,128,1920]{2,1,0:T(8,128)(2,1)}), bf16[4,128,1920]{2,1,0:T(8,128)(2,1)S(1)}, u32[]{:S(2)}, u32[]{:S(2)}) %all-to-all-start.2) | async-done | bytes 1966112 | tf_op jit(solution)/shard_map/all_to_all | solution.py:210
  102.4 11.2 %collective-permute-done.4 = bf16[128,2048]{1,0:T(8,128)(2,1)} collective-permute-done((bf16[128,2048]{1,0:T(8,128)(2,1)}, bf16[128,2048]{1,0:T(8,128)(2,1)}, u32[]{:S(2)}, u32[]{:S(2)}) %collective-permute-start.4) | collective-permute-done | bytes 524320 | tf_op jit(solution)/shard_map/ppermute | solution.py:183
  116.0 8.4 %collective-permute-done.6 = bf16[128,2048]{1,0:T(8,128)(2,1)} collective-permute-done((bf16[128,2048]{1,0:T(8,128)(2,1)S(1)}, bf16[128,2048]{1,0:T(8,128)(2,1)}, u32[]{:S(2)}, u32[]{:S(2)}) %collective-permute-start.6) | collective-permute-done | bytes 524320 | tf_op jit(solution)/shard_map/ppermute | solution.py:183
  151.2 13.8 %collective-permute-done.14 = bf16[128,2048]{1,0:T(8,128)(2,1)S(1)} collective-permute-done((bf16[128,2048]{1,0:T(8,128)(2,1)S(1)}, bf16[128,2048]{1,0:T(8,128)(2,1)S(1)}, u32[]{:S(2)}, u32[]{:S(2)}) %collective-permute-start.14) | collective-permute-done | bytes 524320 | tf_op jit(solution)/shard_map/ppermute | solution.py:183
  167.1 11.7 %collective-permute-done.15 = bf16[128,2048]{1,0:T(8,128)(2,1)S(1)} collective-permute-done((bf16[128,2048]{1,0:T(8,128)(2,1)S(1)}, bf16[128,2048]{1,0:T(8,128)(2,1)S(1)}, u32[]{:S(2)}, u32[]{:S(2)}) %collective-permute-start.15) | collective-permute-done | bytes 524320 | tf_op jit(solution)/shard_map/ppermute | solution.py:186
  180.0 12.3 %collective-permute-done.16 = bf16[128,2048]{1,0:T(8,128)(2,1)S(1)} collective-permute-done((bf16[128,2048]{1,0:T(8,128)(2,1)S(1)}, bf16[128,2048]{1,0:T(8,128)(2,1)S(1)}, u32[]{:S(2)}, u32[]{:S(2)}) %collective-permute-start.16) | collective-permute-done | bytes 524320 | tf_op jit(solution)/shard_map/ppermute | solution.py:183
  206.9 4.8 shard_map.315
  218.4 12.5 %collective-permute-done.19 = bf16[128,2048]{1,0:T(8,128)(2,1)S(1)} collective-permute-done((bf16[128,2048]{1,0:T(8,128)(2,1)S(1)}, bf16[128,2048]{1,0:T(8,128)(2,1)S(1)}, u32[]{:S(2)}, u32[]{:S(2)}) %collective-permute-start.19) | collective-permute-done | bytes 524320 | tf_op jit(solution)/shard_map/ppermute | solution.py:183
  232.6 11.7 %collective-permute-done.20 = bf16[128,2048]{1,0:T(8,128)(2,1)S(1)} collective-permute-done((bf16[128,2048]{1,0:T(8,128)(2,1)S(1)}, bf16[128,2048]{1,0:T(8,128)(2,1)S(1)}, u32[]{:S(2)}, u32[]{:S(2)}) %collective-permute-start.20) | collective-permute-done | bytes 524320 | tf_op jit(solution)/shard_map/ppermute | solution.py:186
  246.6 10.8 %collective-permute-done.21 = bf16[128,2048]{1,0:T(8,128)(2,1)S(1)} collective-permute-done((bf16[128,2048]{1,0:T(8,128)(2,1)S(1)}, bf16[128,2048]{1,0:T(8,128)(2,1)S(1)}, u32[]{:S(2)}, u32[]{:S(2)}) %collective-permute-start.21) | collective-permute-done | bytes 524320 | tf_op jit(solution)/shard_map/ppermute | solution.py:183
  262.1 76.7 %all-gather.8.cloned.1.call-done = bf16[2048,1920]{1,0:T(8,128)(2,1)} async-done(((bf16[512,1920]{1,0:T(8,128)(2,1)}), bf16[2048,1920]{1,0:T(8,128)(2,1)}) %all-gather.8.cloned.1.call-update) | async-done | bytes 7864336 | tf_op jit(solution)/shard_map/all_gather | solution.py:228
  338.8 6.1 fusion.2
  344.9 5.3 fusion.28
  357.1 6.5 convolution_convert_fusion
  363.7 9.4 %reduce-scatter.9.cloned.1.call-start = ((), (), s32[]{:S(2)}) async-start(), calls=%async_computation.16 | async-start | bytes 6553600 | tf_op jit(solution)/shard_map/reduce_scatter | solution.py:231
  373.1 5.8 fusion.7
  386.4 12.5 %collective-permute-done.24 = bf16[128,2048]{1,0:T(8,128)(2,1)S(1)} collective-permute-done((bf16[128,2048]{1,0:T(8,128)(2,1)S(1)}, bf16[128,2048]{1,0:T(8,128)(2,1)S(1)}, u32[]{:S(2)}, u32[]{:S(2)}) %collective-permute-start.24) | collective-permute-done | bytes 524320 | tf_op jit(solution)/shard_map/ppermute | solution.py:183
  401.9 11.8 %collective-permute-done.25 = bf16[128,2048]{1,0:T(8,128)(2,1)S(1)} collective-permute-done((bf16[128,2048]{1,0:T(8,128)(2,1)S(1)}, bf16[128,2048]{1,0:T(8,128)(2,1)S(1)}, u32[]{:S(2)}, u32[]{:S(2)}) %collective-permute-start.25) | collective-permute-done | bytes 524320 | tf_op jit(solution)/shard_map/ppermute | solution.py:186
  417.0 10.9 %collective-permute-done.26 = bf16[128,2048]{1,0:T(8,128)(2,1)S(1)} collective-permute-done((bf16[128,2048]{1,0:T(8,128)(2,1)S(1)}, bf16[128,2048]{1,0:T(8,128)(2,1)S(1)}, u32[]{:S(2)}, u32[]{:S(2)}) %collective-permute-start.26) | collective-permute-done | bytes 524320 | tf_op jit(solution)/shard_map/ppermute | solution.py:183
  435.1 5.4 shard_map.316
  452.9 10.6 %collective-permute-done.32 = bf16[128,2048]{1,0:T(8,128)(2,1)S(1)} collective-permute-done((bf16[128,2048]{1,0:T(8,128)(2,1)S(1)}, bf16[128,2048]{1,0:T(8,128)(2,1)S(1)}, u32[]{:S(2)}, u32[]{:S(2)}) %collective-permute-start.32) | collective-permute-done | bytes 524320 | tf_op jit(solution)/shard_map/ppermute | solution.py:183
  468.5 8.7 %collective-permute-done.33 = bf16[128,2048]{1,0:T(8,128)(2,1)} collective-permute-done((bf16[128,2048]{1,0:T(8,128)(2,1)S(1)}, bf16[128,2048]{1,0:T(8,128)(2,1)}, u32[]{:S(2)}, u32[]{:S(2)}) %collective-permute-start.33) | collective-permute-done | bytes 524320 | tf_op jit(solution)/shard_map/ppermute | solution.py:186
  482.6 10.9 %collective-permute-done.34 = bf16[128,2048]{1,0:T(8,128)(2,1)S(1)} collective-permute-done((bf16[128,2048]{1,0:T(8,128)(2,1)S(1)}, bf16[128,2048]{1,0:T(8,128)(2,1)S(1)}, u32[]{:S(2)}, u32[]{:S(2)}) %collective-permute-start.34) | collective-permute-done | bytes 524320 | tf_op jit(solution)/shard_map/ppermute | solution.py:183
  503.3 7.5 %collective-permute-done.29 = bf16[128,2048]{1,0:T(8,128)(2,1)} collective-permute-done((bf16[128,2048]{1,0:T(8,128)(2,1)S(1)}, bf16[128,2048]{1,0:T(8,128)(2,1)}, u32[]{:S(2)}, u32[]{:S(2)}) %collective-permute-start.29) | collective-permute-done | bytes 524320 | tf_op jit(solution)/shard_map/ppermute | solution.py:183
  519.4 5.4 shard_map.317
  535.6 4.9 all-to-all-start.3
  554.8 34.4 %all-to-all-done.3 = bf16[4,4,128,1024]{3,2,0,1:T(8,128)(2,1)} async-done(((bf16[4,4,128,1024]{3,2,0,1:T(8,128)(2,1)}), bf16[4,4,128,1024]{3,2,0,1:T(8,128)(2,1)}, u32[]{:S(2)}, u32[]{:S(2)}) %all-to-all-start.3) | async-done | bytes 4194336 | tf_op jit(solution)/shard_map/all_to_all | solution.py:349
  604.8 10.1 %collective-permute-done.38 = bf16[128,2048]{1,0:T(8,128)(2,1)S(1)} collective-permute-done((bf16[128,2048]{1,0:T(8,128)(2,1)S(1)}, bf16[128,2048]{1,0:T(8,128)(2,1)S(1)}, u32[]{:S(2)}, u32[]{:S(2)}) %collective-permute-start.38) | collective-permute-done | bytes 524320 | tf_op jit(solution)/shard_map/ppermute | solution.py:186
  636.1 8.1 %all-to-all-done.5 = bf16[4,128,1280]{2,1,0:T(8,128)(2,1)S(1)} async-done(((bf16[4,128,1280]{2,1,0:T(8,128)(2,1)}), bf16[4,128,1280]{2,1,0:T(8,128)(2,1)S(1)}, u32[]{:S(2)}, u32[]{:S(2)}) %all-to-all-start.5) | async-done | bytes 1310752 | tf_op jit(solution)/shard_map/all_to_all | solution.py:210
  652.7 12.0 %all-to-all-done.4 = bf16[4,128,1024]{1,2,0:T(8,128)(2,1)S(1)} async-done(((bf16[4,128,1024]{1,2,0:T(8,128)(2,1)}), bf16[4,128,1024]{1,2,0:T(8,128)(2,1)S(1)}, u32[]{:S(2)}, u32[]{:S(2)}) %all-to-all-start.4) | async-done | bytes 1048608 | tf_op jit(solution)/shard_map/all_to_all | solution.py:210
  (437 shorter events, 255.7 us)
Async XLA Ops:
  11.6 18.8 %all-to-all-start = ((bf16[4,128,1024]{2,1,0:T(8,128)(2,1)}), bf16[4,128,1024]{2,1,0:T(8,128)(2,1)S(1)}, u32[]{:S(2)}, u32[]{:S(2)}) async-start(bf16[4,128,1024]{2,1,0:T(8,128)(2,1)} %pad_maximum_fusion.11), calls=%async_computation | async-start | bytes 2097152 | tf_op jit(solution)/shard_map/all_to_all | solution.py:210
  15.9 120.5 %all-gather.4.cloned.1.call-start = ((), (), s32[]{:S(2)}) async-start(), calls=%async_computation.11 | async-start | bytes 5242880 | tf_op jit(solution)/shard_map/all_gather | solution.py:228
  33.6 34.3 %collective-permute-start.8 = (f32[3,128]{1,0:T(4,128)S(1)}, f32[3,128]{1,0:T(4,128)S(1)}, u32[]{:S(2)}, u32[]{:S(2)}) collective-permute-start(f32[3,128]{1,0:T(4,128)S(1)} %maximum_convert_fusion.9), channel_id=1, source_target_pairs={{0,8},{2,10},{4,12},{6,14},{8,0},{10,2},{12,4},{14,6},{16,24},{18,... | collective-permute-start | bytes 4616 | tf_op jit(solution)/shard_map/ppermute | solution.py:183
  36.0 31.9 %collective-permute-start.9 = (f32[3,128]{1,0:T(4,128)S(1)}, f32[3,128]{1,0:T(4,128)S(1)}, u32[]{:S(2)}, u32[]{:S(2)}) collective-permute-start(f32[3,128]{1,0:T(4,128)S(1)} %maximum_convert_fusion.9), channel_id=1, source_target_pairs={{0,16},{2,18},{4,20},{6,22},{8,24},{10,26},{12,28},{14,30},{16,0},... | collective-permute-start | bytes 4616 | tf_op jit(solution)/shard_map/ppermute | solution.py:183
  38.6 29.4 %collective-permute-start.10 = (f32[3,128]{1,0:T(4,128)S(1)}, f32[3,128]{1,0:T(4,128)S(1)}, u32[]{:S(2)}, u32[]{:S(2)}) collective-permute-start(f32[3,128]{1,0:T(4,128)S(1)} %maximum_convert_fusion.9), channel_id=1, source_target_pairs={{0,24},{2,26},{4,28},{6,30},{8,16},{10,18},{12,20},{14,22},{16,8},... | collective-permute-start | bytes 4616 | tf_op jit(solution)/shard_map/ppermute | solution.py:183
  38.6 34.4 %all-to-all-start.1 = ((bf16[4,128,1024]{2,1,0:T(8,128)(2,1)}), bf16[4,128,1024]{2,1,0:T(8,128)(2,1)S(1)}, u32[]{:S(2)}, u32[]{:S(2)}) async-start(bf16[4,128,1024]{2,1,0:T(8,128)(2,1)} %pad_maximum_fusion.12), calls=%async_computation.1 | async-start | bytes 2097152 | tf_op jit(solution)/shard_map/all_to_all | solution.py:210
  42.1 37.6 %collective-permute-start.2 = (bf16[128,2048]{1,0:T(8,128)(2,1)S(1)}, bf16[128,2048]{1,0:T(8,128)(2,1)}, u32[]{:S(2)}, u32[]{:S(2)}) collective-permute-start(bf16[128,2048]{1,0:T(8,128)(2,1)S(1)} %copy-done), channel_id=1, source_target_pairs={{0,4},{2,6},{4,0},{6,2},{8,12},{10,14},{12,8},{14,10},{16,20},{18,... | collective-permute-start | bytes 1572872 | tf_op jit(solution)/shard_map/ppermute | solution.py:183
  45.4 22.5 %collective-permute-start = (s32[1,2,128]{2,1,0:T(2,128)S(1)}, s32[1,2,128]{2,1,0:T(2,128)S(1)}, u32[]{:S(2)}, u32[]{:S(2)}) collective-permute-start(s32[1,2,128]{2,1,0:T(2,128)S(1)} %get-tuple-element.300), channel_id=1, source_target_pairs={{0,4},{2,6},{4,0},{6,2},{8,12},{10,14},{12,8},{14,10},{16,20},{18,... | collective-permute-start | bytes 3080 | tf_op jit(solution)/shard_map/ppermute | solution.py:183
  74.0 28.3 %all-to-all-start.2 = ((bf16[4,128,1920]{2,1,0:T(8,128)(2,1)}), bf16[4,128,1920]{2,1,0:T(8,128)(2,1)S(1)}, u32[]{:S(2)}, u32[]{:S(2)}) async-start(bf16[4,128,1920]{2,1,0:T(8,128)(2,1)} %pad_maximum_fusion.9), calls=%async_computation.2 | async-start | bytes 3932160 | tf_op jit(solution)/shard_map/all_to_all | solution.py:210
  77.6 120.0 %all-gather.6.cloned.1.call-start = ((), (), s32[]{:S(2)}) async-start(), calls=%async_computation.12 | async-start | bytes 5242880 | tf_op jit(solution)/shard_map/all_gather | solution.py:228
  77.7 35.9 %collective-permute-start.4 = (bf16[128,2048]{1,0:T(8,128)(2,1)}, bf16[128,2048]{1,0:T(8,128)(2,1)}, u32[]{:S(2)}, u32[]{:S(2)}) collective-permute-start(bf16[128,2048]{1,0:T(8,128)(2,1)} %bitcast.347), channel_id=1, source_target_pairs={{0,4},{2,6},{4,0},{6,2},{8,12},{10,14},{12,8},{14,10},{16,20},{18,... | collective-permute-start | bytes 1572872 | tf_op jit(solution)/shard_map/ppermute | solution.py:183
  81.8 43.9 %collective-permute-start.3 = (bf16[2,128,2048]{2,1,0:T(8,128)(2,1)}, bf16[2,128,2048]{2,1,0:T(8,128)(2,1)}, u32[]{:S(2)}, u32[]{:S(2)}) collective-permute-start(bf16[2,128,2048]{2,1,0:T(8,128)(2,1)} %pad_maximum_fusion.13), channel_id=1, source_target_pairs={{0,2},{2,0},{4,6},{6,4},{8,10},{10,8},{12,14},{14,12},{16,18},{18,... | collective-permute-start | bytes 3145736 | tf_op jit(solution)/shard_map/ppermute | solution.py:183
  102.3 22.1 %collective-permute-start.6 = (bf16[128,2048]{1,0:T(8,128)(2,1)S(1)}, bf16[128,2048]{1,0:T(8,128)(2,1)}, u32[]{:S(2)}, u32[]{:S(2)}) collective-permute-start(bf16[128,2048]{1,0:T(8,128)(2,1)S(1)} %copy-done.3), channel_id=1, source_target_pairs={{0,4},{2,6},{4,0},{6,2},{8,12},{10,14},{12,8},{14,10},{16,20},{18,... | collective-permute-start | bytes 1572872 | tf_op jit(solution)/shard_map/ppermute | solution.py:183
  116.0 222.8 %all-gather.8.cloned.1.call-start = ((), (), s32[]{:S(2)}) async-start(), calls=%async_computation.13 | async-start | bytes 9830400 | tf_op jit(solution)/shard_map/all_gather | solution.py:228
  150.8 14.3 %collective-permute-start.14 = (bf16[128,2048]{1,0:T(8,128)(2,1)S(1)}, bf16[128,2048]{1,0:T(8,128)(2,1)S(1)}, u32[]{:S(2)}, u32[]{:S(2)}) collective-permute-start(bf16[128,2048]{1,0:T(8,128)(2,1)S(1)} %fusion.57), channel_id=1, source_target_pairs={{0,4},{2,6},{4,0},{6,2},{8,12},{10,14},{12,8},{14,10},{16,20},{18,... | collective-permute-start | bytes 1572872 | tf_op jit(solution)/shard_map/ppermute | solution.py:183
  179.5 317.9 %reduce-scatter.11.cloned.1.call-start = ((), (), s32[]{:S(2)}) async-start(), calls=%async_computation.17 | async-start | bytes 3276800 | tf_op jit(solution)/shard_map/reduce_scatter | solution.py:231
  363.7 259.5 %reduce-scatter.9.cloned.1.call-start = ((), (), s32[]{:S(2)}) async-start(), calls=%async_computation.16 | async-start | bytes 6553600 | tf_op jit(solution)/shard_map/reduce_scatter | solution.py:231
  380.7 263.8 %reduce-scatter.7.cloned.1.call-start = ((), (), s32[]{:S(2)}) async-start(), calls=%async_computation.15 | async-start | bytes 5242880 | tf_op jit(solution)/shard_map/reduce_scatter | solution.py:231
  449.5 14.0 %collective-permute-start.32 = (bf16[128,2048]{1,0:T(8,128)(2,1)S(1)}, bf16[128,2048]{1,0:T(8,128)(2,1)S(1)}, u32[]{:S(2)}, u32[]{:S(2)}) collective-permute-start(bf16[128,2048]{1,0:T(8,128)(2,1)S(1)} %fusion.45), channel_id=1, source_target_pairs={{0,4},{2,6},{4,0},{6,2},{8,12},{10,14},{12,8},{14,10},{16,20},{18,... | collective-permute-start | bytes 1572872 | tf_op jit(solution)/shard_map/ppermute | solution.py:183
  452.1 42.4 %collective-permute-start.28 = (bf16[2,128,2048]{2,1,0:T(8,128)(2,1)}, bf16[2,128,2048]{2,1,0:T(8,128)(2,1)}, u32[]{:S(2)}, u32[]{:S(2)}) collective-permute-start(bf16[2,128,2048]{2,1,0:T(8,128)(2,1)} %pad_maximum_fusion.22), channel_id=1, source_target_pairs={{0,2},{2,0},{4,6},{6,4},{8,10},{10,8},{12,14},{14,12},{16,18},{18,... | collective-permute-start | bytes 3145736 | tf_op jit(solution)/shard_map/ppermute | solution.py:183
  494.5 19.4 %collective-permute-start.35 = (bf16[2,128,2048]{2,1,0:T(8,128)(2,1)}, bf16[2,128,2048]{2,1,0:T(8,128)(2,1)}, u32[]{:S(2)}, u32[]{:S(2)}) collective-permute-start(bf16[2,128,2048]{2,1,0:T(8,128)(2,1)} %pad_maximum_fusion.24), channel_id=1, source_target_pairs={{0,2},{2,0},{4,6},{6,4},{8,10},{10,8},{12,14},{14,12},{16,18},{18,... | collective-permute-start | bytes 3145736 | tf_op jit(solution)/shard_map/ppermute | solution.py:183
  495.9 14.9 %collective-permute-start.29 = (bf16[128,2048]{1,0:T(8,128)(2,1)S(1)}, bf16[128,2048]{1,0:T(8,128)(2,1)}, u32[]{:S(2)}, u32[]{:S(2)}) collective-permute-start(bf16[128,2048]{1,0:T(8,128)(2,1)S(1)} %fusion.48), channel_id=1, source_target_pairs={{0,4},{2,6},{4,0},{6,2},{8,12},{10,14},{12,8},{14,10},{16,20},{18,... | collective-permute-start | bytes 1572872 | tf_op jit(solution)/shard_map/ppermute | solution.py:183
  499.6 36.0 %all-to-all-start.6 = ((bf16[4,128,640]{1,2,0:T(8,128)(2,1)}), bf16[4,128,640]{1,2,0:T(8,128)(2,1)S(1)}, u32[]{:S(2)}, u32[]{:S(2)}) async-start(bf16[4,128,640]{1,2,0:T(8,128)(2,1)} %copy.123), calls=%async_computation.10 | async-start | bytes 1310720 | tf_op jit(solution)/shard_map/all_to_all | solution.py:210
  512.4 90.2 %collective-permute-start.30 = (bf16[128,2048]{1,0:T(8,128)(2,1)S(1)}, bf16[128,2048]{1,0:T(8,128)(2,1)}, u32[]{:S(2)}, u32[]{:S(2)}) collective-permute-start(bf16[128,2048]{1,0:T(8,128)(2,1)S(1)} %fusion.50), channel_id=1, source_target_pairs={{0,1},{1,0},{2,3},{3,2},{4,5},{5,4},{6,7},{7,6},{8,9},{9,8},{10,11... | collective-permute-start | bytes 1572872 | tf_op jit(solution)/shard_map/ppermute | solution.py:186
  535.6 53.6 %all-to-all-start.3 = ((bf16[4,4,128,1024]{3,2,0,1:T(8,128)(2,1)}), bf16[4,4,128,1024]{3,2,0,1:T(8,128)(2,1)}, u32[]{:S(2)}, u32[]{:S(2)}) async-start(bf16[4,4,128,1024]{3,2,0,1:T(8,128)(2,1)} %copy.120), calls=%async_computation.3 | async-start | bytes 8388608 | tf_op jit(solution)/shard_map/all_to_all | solution.py:349
  540.5 129.9 %reduce-scatter.5.cloned.1.call-start = ((), (), s32[]{:S(2)}) async-start(), calls=%async_computation.14 | async-start | bytes 5242880 | tf_op jit(solution)/shard_map/reduce_scatter | solution.py:231
  550.5 43.5 %collective-permute-start.39 = (bf16[2,128,2048]{2,1,0:T(8,128)(2,1)}, bf16[2,128,2048]{2,1,0:T(8,128)(2,1)}, u32[]{:S(2)}, u32[]{:S(2)}) collective-permute-start(bf16[2,128,2048]{2,1,0:T(8,128)(2,1)} %pad_maximum_fusion.26), channel_id=1, source_target_pairs={{0,2},{2,0},{4,6},{6,4},{8,10},{10,8},{12,14},{14,12},{16,18},{18,... | collective-permute-start | bytes 3145736 | tf_op jit(solution)/shard_map/ppermute | solution.py:183
  552.0 48.4 %collective-permute-start.37 = (bf16[128,2048]{1,0:T(8,128)(2,1)S(1)}, bf16[128,2048]{1,0:T(8,128)(2,1)S(1)}, u32[]{:S(2)}, u32[]{:S(2)}) collective-permute-start(bf16[128,2048]{1,0:T(8,128)(2,1)S(1)} %fusion.42), channel_id=1, source_target_pairs={{0,4},{2,6},{4,0},{6,2},{8,12},{10,14},{12,8},{14,10},{16,20},{18,... | collective-permute-start | bytes 1572872 | tf_op jit(solution)/shard_map/ppermute | solution.py:183
  595.3 20.4 %collective-permute-start.40 = (bf16[128,2048]{1,0:T(8,128)(2,1)S(1)}, bf16[128,2048]{1,0:T(8,128)(2,1)S(1)}, u32[]{:S(2)}, u32[]{:S(2)}) collective-permute-start(bf16[128,2048]{1,0:T(8,128)(2,1)S(1)} %fusion.39), channel_id=1, source_target_pairs={{0,4},{2,6},{4,0},{6,2},{8,12},{10,14},{12,8},{14,10},{16,20},{18,... | collective-permute-start | bytes 1572872 | tf_op jit(solution)/shard_map/ppermute | solution.py:183
  618.1 14.6 %collective-permute-start.41 = (bf16[128,2048]{1,0:T(8,128)(2,1)}, bf16[128,2048]{1,0:T(8,128)(2,1)}, u32[]{:S(2)}, u32[]{:S(2)}) collective-permute-start(bf16[128,2048]{1,0:T(8,128)(2,1)} %fusion.41), channel_id=1, source_target_pairs={{0,1},{1,0},{2,3},{3,2},{4,5},{5,4},{6,7},{7,6},{8,9},{9,8},{10,11... | collective-permute-start | bytes 1572872 | tf_op jit(solution)/shard_map/ppermute | solution.py:186
  623.2 21.0 %all-to-all-start.5 = ((bf16[4,128,1280]{2,1,0:T(8,128)(2,1)}), bf16[4,128,1280]{2,1,0:T(8,128)(2,1)S(1)}, u32[]{:S(2)}, u32[]{:S(2)}) async-start(bf16[4,128,1280]{2,1,0:T(8,128)(2,1)} %bitcast.352), calls=%async_computation.8 | async-start | bytes 2621440 | tf_op jit(solution)/shard_map/all_to_all | solution.py:210
  646.7 18.0 %all-to-all-start.4 = ((bf16[4,128,1024]{1,2,0:T(8,128)(2,1)}), bf16[4,128,1024]{1,2,0:T(8,128)(2,1)S(1)}, u32[]{:S(2)}, u32[]{:S(2)}) async-start(bf16[4,128,1024]{1,2,0:T(8,128)(2,1)} %copy.122), calls=%async_computation.6 | async-start | bytes 2097152 | tf_op jit(solution)/shard_map/all_to_all | solution.py:210
  (103 other events, 573.7 us)
Sparse Core Ops, SparseCore 0:
  31.5 81.8 all-gather.3
  116.1 81.4 all-gather.5
  199.2 139.5 all-gather.7
  363.8 50.3 reduce-scatter.10
  416.3 93.4 reduce-scatter.8
  511.9 77.2 reduce-scatter.6
  594.1 76.2 reduce-scatter.4

commit v4 on v3

--- a/solution.py
+++ b/solution.py
@@ -227,6 +227,26 @@
         shard = shard.reshape(inner * part, -1)
         return lax.all_gather(shard, "dp", axis_index_groups=planes(inner), tiled=True)
 
+    def ring_start(own, shard):
+        block = [
+            lax.dynamic_index_in_dim(shard, (place % ATTN) ^ j, 0, keepdims=False)
+            for j in range(1, ATTN)
+        ]
+        return [own[None], block[0][None], jnp.stack(block[1:])]
+
+    def ring_step(held):
+        return [lax.ppermute(h, "dp", [(i, (i + ATTN) % dp) for i in range(dp)]) for h in held]
+
+    def placed(kept):
+        mine, plane, outer = place % ATTN, place // ATTN, dp // ATTN
+        full = jnp.zeros((width, kept[0][0].shape[2]), BF)
+        for step, held in enumerate(kept):
+            for h, js in zip(held, ((0,), (1,), (2, 3))):
+                for n, j in enumerate(js):
+                    at = (((plane - step) % outer) * ATTN + (mine ^ j)) * part
+                    full = lax.dynamic_update_slice(full, h[n], (at, 0))
+        return full
+
     def plane_sum(whole, inner):
         return lax.psum_scatter(whole, "dp", axis_index_groups=planes(inner), tiled=True)
 
@@ -243,22 +263,34 @@
         return split(exchange(held, inner), widths)
 
     packed_self = pack([wq_self, wk_self, wv_self, wo_self.T], ATTN)
+    own_self = lax.dynamic_index_in_dim(packed_self, place % ATTN, 0, keepdims=False)
     shard_self = exchange(packed_self, ATTN)
     packed_cross = pack([wq_cross, wk_cross, wv_cross, wo_cross.T], ATTN)
-    shard_self, inputs, packed_cross, gain_self, segments = tie(
-        shard_self, inputs, packed_cross, gain_self, segments
-    )
-    w_self = over_planes(shard_self, ATTN)
+    ring = dp // ATTN == 4
+    if ring:
+        kept = [ring_start(own_self, shard_self)]
+        kept.append(ring_step(kept[0]))
+        kept[1][2], inputs, packed_cross = tie(kept[1][2], inputs, packed_cross)
+        kept.append(ring_step(kept[1]))
+        kept[2][2], gain_self, segments = tie(kept[2][2], gain_self, segments)
+        kept.append(ring_step(kept[2]))
+    else:
+        shard_self, inputs, packed_cross = tie(shard_self, inputs, packed_cross)
+        w_self = over_planes(shard_self, ATTN)
     start_rows = rows_of(inputs, ATTN)
     shard_cross = exchange(packed_cross, ATTN)
     packed_ffn = pack([w_gate, w_up, w_down.T], FFN)
-    shard_cross, patch_rows, packed_ffn = tie(shard_cross, patches.reshape(-1, width), packed_ffn)
+    patch_rows = patches.reshape(-1, width)
+    if ring:
+        kept[3][2], shard_cross, start_rows, patch_rows, packed_ffn, grad_out = tie(
+            kept[3][2], shard_cross, start_rows, patch_rows, packed_ffn, grad_out
+        )
+        w_self = placed(kept)
     w_cross = over_planes(shard_cross, ATTN)
     memory = rows_of(patch_rows, ATTN)
     shard_ffn = exchange(packed_ffn, FFN)
-    shard_ffn, grad_out = tie(shard_ffn, grad_out)
+    shard_ffn, grad_out, memory = tie(shard_ffn, grad_out, memory)
     grad_rows = rows_of(grad_out, FFN)
-    start_rows, memory, grad_rows, shard_ffn = tie(start_rows, memory, grad_rows, shard_ffn)
     hw = w_self.shape[1] // 4
 
     gains = jnp.stack([gain_self, gain_cross, gain_ffn]).astype(F32)

time: 694 us -> 682 us (0.983)
  waiting for transfers between devices: 390 us -> 349 us
  local copies, waits for them, and re-layouts: 52.2 us -> 77.3 us
  starting transfers between devices: 73.4 us -> 88.8 us
  other arithmetic: 63.9 us -> 54.8 us
    ppermute x39, waiting for transfers between devices: 169 us -> 132 us  [swap(): return lax.ppermute(value, 'dp', [(i, i ^ distance) for i in range(dp)])]
    ppermute x0 -> x9, waiting for transfers between devices: none -> 31.1 us  [ring_step(): lax.ppermute(h, 'dp', [(i, (i + ATTN) % dp) for i in range(dp)])]
    dynamic_update_slice x0 -> x16, local copies, waits for them, and re-layouts: none -> 18.4 us  [placed(): full = lax.dynamic_update_slice(full, h[n], (at, 0))]
    all_to_all x6, waiting for transfers between devices: 48.2 us -> 34.8 us  [exchange(): lax.all_to_all(blocks, 'dp', 0, 0, axis_index_groups=groups, tiled=True)]
    ppermute x7, waiting for transfers between devices: 56.4 us -> 43.6 us  [swap_mp(): return lax.ppermute(value, 'mp', [(0, 1), (1, 0)])]
    all_gather x3 -> x2, waiting for transfers between devices: 80 us -> 71.6 us  [over_planes(): lax.all_gather(shard, 'dp', axis_index_groups=planes(inner), tiled=True)]
    ppermute x39, starting transfers between devices: 26.6 us -> 34.6 us  [swap(): return lax.ppermute(value, 'dp', [(i, i ^ distance) for i in range(dp)])]
    ppermute x0 -> x9, starting transfers between devices: none -> 6.97 us  [ring_step(): lax.ppermute(h, 'dp', [(i, (i + ATTN) % dp) for i in range(dp)])]
  transfers between devices with their start and end apart: 60 -> 68, of which waited for: 37 -> 36; matrix products, arithmetic and copies ran while one was open for 20% -> 22% of each run, Pallas kernels for 3% -> 3%
where the time goes in v4:
time: 682 us; the launch traced here: 671 us
  waiting for transfers between devices  349 us (51%)
  starting transfers between devices  88.8 us (13%)
  local copies, waits for them, and re-layouts  77.3 us (11%)
  matrix products  64.4 us (9%)
  other arithmetic  54.8 us (8%)
  Pallas kernels  19.8 us (3%)
  between operations  16.4 us (2%)
    ppermute x39, waiting for transfers between devices, swap(): return lax.ppermute(value, 'dp', [(i, i ^ distance) for i in range(dp)])  132 us
    all_gather x2, waiting for transfers between devices, over_planes(): lax.all_gather(shard, 'dp', axis_index_groups=planes(inner), tiled=True)  71.6 us
    dot_general x21, matrix products, dot(): lax.dot_general(a, b, (((da,), (db,)), ((), ())), preferred_element_type=...  64.4 us
    ppermute x7, waiting for transfers between devices, swap_mp(): return lax.ppermute(value, 'mp', [(0, 1), (1, 0)])  43.6 us
    all_to_all x6, waiting for transfers between devices, exchange(): lax.all_to_all(blocks, 'dp', 0, 0, axis_index_groups=groups, tiled=True)  34.8 us
    ppermute x39, starting transfers between devices, swap(): return lax.ppermute(value, 'dp', [(i, i ^ distance) for i in range(dp)])  34.6 us
    all_to_all x1, waiting for transfers between devices, on_device(): lax.all_to_all(term_self.reshape(-1, ATTN, part, 4 * hw), 'dp', 1, 1, axi...  34.6 us
    ppermute x9, waiting for transfers between devices, ring_step(): lax.ppermute(h, 'dp', [(i, (i + ATTN) % dp) for i in range(dp)])  31.1 us
  transfers between devices with their start and end apart: 68, of which 36 were waited for; matrix products, arithmetic and copies ran while one was open for 22% of the time, Pallas kernels for 3%

profile of v4, /device:TPU:0, one launch (start us, length us, event | category | flops | bytes accessed | tf_op | source)
XLA Modules:
  0.0 670.8 jit_solution(15605967056745424156)
XLA Ops:
  41.0 4.9 collective-permute-done.14
  47.7 15.1 %collective-permute-done.13 = bf16[1,128,1024]{1,2,0:T(8,128)(2,1)S(1)} collective-permute-done((bf16[1,128,1024]{1,2,0:T(8,128)(2,1)S(1)}, bf16[1,128,1024]{1,2,0:T(8,128)(2,1)S(1)}, u32[]{:S(2)}, u32[]{:S(2)}) %collective-permute-start.13) | collective-permute-done | bytes 262176 | tf_op jit(solution)/shard_map/ppermute | solution.py:238
  75.6 9.8 %collective-permute-done.1 = bf16[2,128,1024]{1,2,0:T(8,128)(2,1)} collective-permute-done((bf16[2,128,1024]{1,2,0:T(8,128)(2,1)S(1)}, bf16[2,128,1024]{1,2,0:T(8,128)(2,1)}, u32[]{:S(2)}, u32[]{:S(2)}) %collective-permute-start.1) | collective-permute-done | bytes 524320 | tf_op jit(solution)/shard_map/ppermute | solution.py:238
  124.9 12.4 %collective-permute-done.21 = bf16[128,2048]{1,0:T(8,128)(2,1)S(1)} collective-permute-done((bf16[128,2048]{1,0:T(8,128)(2,1)S(1)}, bf16[128,2048]{1,0:T(8,128)(2,1)S(1)}, u32[]{:S(2)}, u32[]{:S(2)}) %collective-permute-start.21) | collective-permute-done | bytes 524320 | tf_op jit(solution)/shard_map/ppermute | solution.py:183
  146.1 8.4 %collective-permute-done.19 = bf16[128,2048]{1,0:T(8,128)(2,1)} collective-permute-done((bf16[128,2048]{1,0:T(8,128)(2,1)S(1)}, bf16[128,2048]{1,0:T(8,128)(2,1)}, u32[]{:S(2)}, u32[]{:S(2)}) %collective-permute-start.19) | collective-permute-done | bytes 524320 | tf_op jit(solution)/shard_map/ppermute | solution.py:183
  160.4 14.7 %all-to-all-done.2 = bf16[4,128,1920]{2,1,0:T(8,128)(2,1)} async-done(((bf16[4,128,1920]{2,1,0:T(8,128)(2,1)}), bf16[4,128,1920]{2,1,0:T(8,128)(2,1)}, u32[]{:S(2)}, u32[]{:S(2)}) %all-to-all-start.2) | async-done | bytes 1966112 | tf_op jit(solution)/shard_map/all_to_all | solution.py:210
  177.5 11.9 %collective-permute-done.23 = bf16[128,2048]{1,0:T(8,128)(2,1)S(1)} collective-permute-done((bf16[128,2048]{1,0:T(8,128)(2,1)S(1)}, bf16[128,2048]{1,0:T(8,128)(2,1)S(1)}, u32[]{:S(2)}, u32[]{:S(2)}) %collective-permute-start.23) | collective-permute-done | bytes 524320 | tf_op jit(solution)/shard_map/ppermute | solution.py:183
  214.0 12.4 %collective-permute-done.26 = bf16[128,2048]{1,0:T(8,128)(2,1)S(1)} collective-permute-done((bf16[128,2048]{1,0:T(8,128)(2,1)S(1)}, bf16[128,2048]{1,0:T(8,128)(2,1)S(1)}, u32[]{:S(2)}, u32[]{:S(2)}) %collective-permute-start.26) | collective-permute-done | bytes 524320 | tf_op jit(solution)/shard_map/ppermute | solution.py:183
  229.9 10.1 %collective-permute-done.27 = bf16[128,2048]{1,0:T(8,128)(2,1)S(1)} collective-permute-done((bf16[128,2048]{1,0:T(8,128)(2,1)S(1)}, bf16[128,2048]{1,0:T(8,128)(2,1)S(1)}, u32[]{:S(2)}, u32[]{:S(2)}) %collective-permute-start.27) | collective-permute-done | bytes 524320 | tf_op jit(solution)/shard_map/ppermute | solution.py:186
  242.5 10.5 %collective-permute-done.30 = bf16[128,2048]{1,0:T(8,128)(2,1)S(1)} collective-permute-done((bf16[128,2048]{1,0:T(8,128)(2,1)S(1)}, bf16[128,2048]{1,0:T(8,128)(2,1)S(1)}, u32[]{:S(2)}, u32[]{:S(2)}) %collective-permute-start.30) | collective-permute-done | bytes 524320 | tf_op jit(solution)/shard_map/ppermute | solution.py:183
  257.7 71.6 %all-gather.5.cloned.1.call-done = bf16[2048,1920]{1,0:T(8,128)(2,1)} async-done(((bf16[512,1920]{1,0:T(8,128)(2,1)}), bf16[2048,1920]{1,0:T(8,128)(2,1)}) %all-gather.5.cloned.1.call-update) | async-done | bytes 7864336 | tf_op jit(solution)/shard_map/all_gather | solution.py:228
  329.3 6.1 fusion.2
  335.4 5.1 fusion.28
  347.2 4.9 convolution_convert_fusion.2
  352.1 9.4 %reduce-scatter.9.cloned.1.call-start = ((), (), s32[]{:S(2)}) async-start(), calls=%async_computation.15 | async-start | bytes 6553600 | tf_op jit(solution)/shard_map/reduce_scatter | solution.py:251
  361.5 5.8 fusion.7
  375.6 12.5 %collective-permute-done.33 = bf16[128,2048]{1,0:T(8,128)(2,1)S(1)} collective-permute-done((bf16[128,2048]{1,0:T(8,128)(2,1)S(1)}, bf16[128,2048]{1,0:T(8,128)(2,1)S(1)}, u32[]{:S(2)}, u32[]{:S(2)}) %collective-permute-start.33) | collective-permute-done | bytes 524320 | tf_op jit(solution)/shard_map/ppermute | solution.py:183
  391.1 11.8 %collective-permute-done.34 = bf16[128,2048]{1,0:T(8,128)(2,1)S(1)} collective-permute-done((bf16[128,2048]{1,0:T(8,128)(2,1)S(1)}, bf16[128,2048]{1,0:T(8,128)(2,1)S(1)}, u32[]{:S(2)}, u32[]{:S(2)}) %collective-permute-start.34) | collective-permute-done | bytes 524320 | tf_op jit(solution)/shard_map/ppermute | solution.py:186
  406.2 11.0 %collective-permute-done.35 = bf16[128,2048]{1,0:T(8,128)(2,1)S(1)} collective-permute-done((bf16[128,2048]{1,0:T(8,128)(2,1)S(1)}, bf16[128,2048]{1,0:T(8,128)(2,1)S(1)}, u32[]{:S(2)}, u32[]{:S(2)}) %collective-permute-start.35) | collective-permute-done | bytes 524320 | tf_op jit(solution)/shard_map/ppermute | solution.py:183
  424.3 5.4 shard_map.316
  442.1 10.6 %collective-permute-done.41 = bf16[128,2048]{1,0:T(8,128)(2,1)S(1)} collective-permute-done((bf16[128,2048]{1,0:T(8,128)(2,1)S(1)}, bf16[128,2048]{1,0:T(8,128)(2,1)S(1)}, u32[]{:S(2)}, u32[]{:S(2)}) %collective-permute-start.41) | collective-permute-done | bytes 524320 | tf_op jit(solution)/shard_map/ppermute | solution.py:183
  457.6 8.7 %collective-permute-done.42 = bf16[128,2048]{1,0:T(8,128)(2,1)} collective-permute-done((bf16[128,2048]{1,0:T(8,128)(2,1)S(1)}, bf16[128,2048]{1,0:T(8,128)(2,1)}, u32[]{:S(2)}, u32[]{:S(2)}) %collective-permute-start.42) | collective-permute-done | bytes 524320 | tf_op jit(solution)/shard_map/ppermute | solution.py:186
  471.7 10.8 %collective-permute-done.43 = bf16[128,2048]{1,0:T(8,128)(2,1)S(1)} collective-permute-done((bf16[128,2048]{1,0:T(8,128)(2,1)S(1)}, bf16[128,2048]{1,0:T(8,128)(2,1)S(1)}, u32[]{:S(2)}, u32[]{:S(2)}) %collective-permute-start.43) | collective-permute-done | bytes 524320 | tf_op jit(solution)/shard_map/ppermute | solution.py:183
  492.6 7.3 %collective-permute-done.38 = bf16[128,2048]{1,0:T(8,128)(2,1)} collective-permute-done((bf16[128,2048]{1,0:T(8,128)(2,1)S(1)}, bf16[128,2048]{1,0:T(8,128)(2,1)}, u32[]{:S(2)}, u32[]{:S(2)}) %collective-permute-start.38) | collective-permute-done | bytes 524320 | tf_op jit(solution)/shard_map/ppermute | solution.py:183
  508.9 5.4 shard_map.317
  525.0 4.9 all-to-all-start.3
  544.0 34.6 %all-to-all-done.3 = bf16[4,4,128,1024]{3,2,0,1:T(8,128)(2,1)} async-done(((bf16[4,4,128,1024]{3,2,0,1:T(8,128)(2,1)}), bf16[4,4,128,1024]{3,2,0,1:T(8,128)(2,1)}, u32[]{:S(2)}, u32[]{:S(2)}) %all-to-all-start.3) | async-done | bytes 4194336 | tf_op jit(solution)/shard_map/all_to_all | solution.py:381
  578.6 4.7 copy.154
  584.9 4.9 collective-permute-done.46
  594.0 10.5 %collective-permute-done.47 = bf16[128,2048]{1,0:T(8,128)(2,1)S(1)} collective-permute-done((bf16[128,2048]{1,0:T(8,128)(2,1)S(1)}, bf16[128,2048]{1,0:T(8,128)(2,1)S(1)}, u32[]{:S(2)}, u32[]{:S(2)}) %collective-permute-start.47) | collective-permute-done | bytes 524320 | tf_op jit(solution)/shard_map/ppermute | solution.py:186
  624.8 8.1 %all-to-all-done.5 = bf16[4,128,1280]{2,1,0:T(8,128)(2,1)S(1)} async-done(((bf16[4,128,1280]{2,1,0:T(8,128)(2,1)}), bf16[4,128,1280]{2,1,0:T(8,128)(2,1)S(1)}, u32[]{:S(2)}, u32[]{:S(2)}) %all-to-all-start.5) | async-done | bytes 1310752 | tf_op jit(solution)/shard_map/all_to_all | solution.py:210
  641.3 12.0 %all-to-all-done.4 = bf16[4,128,1024]{1,2,0:T(8,128)(2,1)S(1)} async-done(((bf16[4,128,1024]{1,2,0:T(8,128)(2,1)}), bf16[4,128,1024]{1,2,0:T(8,128)(2,1)S(1)}, u32[]{:S(2)}, u32[]{:S(2)}) %all-to-all-start.4) | async-done | bytes 1048608 | tf_op jit(solution)/shard_map/all_to_all | solution.py:210
  (506 shorter events, 278.2 us)
Async XLA Ops:
  13.7 22.7 %all-to-all-start = ((bf16[4,128,1024]{1,2,0:T(8,128)(2,1)}), bf16[4,128,1024]{1,2,0:T(8,128)(2,1)S(1)}, u32[]{:S(2)}, u32[]{:S(2)}) async-start(bf16[4,128,1024]{1,2,0:T(8,128)(2,1)} %pad_maximum_fusion.11), calls=%async_computation | async-start | bytes 2097152 | tf_op jit(solution)/shard_map/all_to_all | solution.py:210
  38.8 24.8 %collective-permute-start = (bf16[2,128,1024]{1,2,0:T(8,128)(2,1)S(1)}, bf16[2,128,1024]{1,2,0:T(8,128)(2,1)S(1)}, u32[]{:S(2)}, u32[]{:S(2)}) collective-permute-start(bf16[2,128,1024]{1,2,0:T(8,128)(2,1)S(1)} %pad_maximum_fusion.27), channel_id=1, source_target_pairs={{0,8},{2,10},{4,12},{6,14},{8,16},{10,18},{12,20},{14,22},{16,24},... | collective-permute-start | bytes 1572872 | tf_op jit(solution)/shard_map/ppermute | solution.py:238
  40.4 22.4 %collective-permute-start.13 = (bf16[1,128,1024]{1,2,0:T(8,128)(2,1)S(1)}, bf16[1,128,1024]{1,2,0:T(8,128)(2,1)S(1)}, u32[]{:S(2)}, u32[]{:S(2)}) collective-permute-start(bf16[1,128,1024]{1,2,0:T(8,128)(2,1)S(1)} %get-tuple-element.164), channel_id=1, source_target_pairs={{0,8},{2,10},{4,12},{6,14},{8,16},{10,18},{12,20},{14,22},{16,24},... | collective-permute-start | bytes 786440 | tf_op jit(solution)/shard_map/ppermute | solution.py:238
  46.0 45.6 %collective-permute-start.16 = (bf16[1,128,1024]{1,2,0:T(8,128)(2,1)S(1)}, bf16[1,128,1024]{1,2,0:T(8,128)(2,1)S(1)}, u32[]{:S(2)}, u32[]{:S(2)}) collective-permute-start(bf16[1,128,1024]{1,2,0:T(8,128)(2,1)S(1)} %collective-permute-done.14), channel_id=1, source_target_pairs={{0,8},{2,10},{4,12},{6,14},{8,16},{10,18},{12,20},{14,22},{16,24},... | collective-permute-start | bytes 786440 | tf_op jit(solution)/shard_map/ppermute | solution.py:238
  63.6 31.9 %collective-permute-start.5 = (bf16[128,2048]{1,0:T(8,128)(2,1)S(1)}, bf16[128,2048]{1,0:T(8,128)(2,1)S(1)}, u32[]{:S(2)}, u32[]{:S(2)}) collective-permute-start(bf16[128,2048]{1,0:T(8,128)(2,1)S(1)} %copy-done), channel_id=1, source_target_pairs={{0,4},{2,6},{4,0},{6,2},{8,12},{10,14},{12,8},{14,10},{16,20},{18,... | collective-permute-start | bytes 1572872 | tf_op jit(solution)/shard_map/ppermute | solution.py:183
  65.6 19.7 %collective-permute-start.1 = (bf16[2,128,1024]{1,2,0:T(8,128)(2,1)S(1)}, bf16[2,128,1024]{1,2,0:T(8,128)(2,1)}, u32[]{:S(2)}, u32[]{:S(2)}) collective-permute-start(bf16[2,128,1024]{1,2,0:T(8,128)(2,1)S(1)} %collective-permute-done), channel_id=1, source_target_pairs={{0,8},{2,10},{4,12},{6,14},{8,16},{10,18},{12,20},{14,22},{16,24},... | collective-permute-start | bytes 1572872 | tf_op jit(solution)/shard_map/ppermute | solution.py:238
  66.9 40.0 %all-to-all-start.1 = ((bf16[4,128,1024]{2,1,0:T(8,128)(2,1)}), bf16[4,128,1024]{2,1,0:T(8,128)(2,1)}, u32[]{:S(2)}, u32[]{:S(2)}) async-start(bf16[4,128,1024]{2,1,0:T(8,128)(2,1)} %pad_maximum_fusion.12), calls=%async_computation.1 | async-start | bytes 2097152 | tf_op jit(solution)/shard_map/all_to_all | solution.py:210
  71.2 124.6 %all-gather.3.cloned.1.call-start = ((), (), s32[]{:S(2)}) async-start(), calls=%async_computation.11 | async-start | bytes 5242880 | tf_op jit(solution)/shard_map/all_gather | solution.py:228
  74.0 21.7 %collective-permute-start.17 = (bf16[1,128,1024]{1,2,0:T(8,128)(2,1)S(1)}, bf16[1,128,1024]{1,2,0:T(8,128)(2,1)S(1)}, u32[]{:S(2)}, u32[]{:S(2)}) collective-permute-start(bf16[1,128,1024]{1,2,0:T(8,128)(2,1)S(1)} %collective-permute-done.15), channel_id=1, source_target_pairs={{0,8},{2,10},{4,12},{6,14},{8,16},{10,18},{12,20},{14,22},{16,24},... | collective-permute-start | bytes 786440 | tf_op jit(solution)/shard_map/ppermute | solution.py:238
  85.4 21.5 %collective-permute-start.4 = (bf16[2,128,1024]{1,2,0:T(8,128)(2,1)}, bf16[2,128,1024]{1,2,0:T(8,128)(2,1)}, u32[]{:S(2)}, u32[]{:S(2)}) collective-permute-start(bf16[2,128,1024]{1,2,0:T(8,128)(2,1)} %collective-permute-done.1), channel_id=1, source_target_pairs={{0,8},{2,10},{4,12},{6,14},{8,16},{10,18},{12,20},{14,22},{16,24},... | collective-permute-start | bytes 1572872 | tf_op jit(solution)/shard_map/ppermute | solution.py:238
  122.4 16.0 %collective-permute-start.18 = (bf16[2,128,2048]{2,1,0:T(8,128)(2,1)S(1)}, bf16[2,128,2048]{2,1,0:T(8,128)(2,1)S(1)}, u32[]{:S(2)}, u32[]{:S(2)}) collective-permute-start(bf16[2,128,2048]{2,1,0:T(8,128)(2,1)S(1)} %pad_maximum_fusion.14), channel_id=1, source_target_pairs={{0,2},{2,0},{4,6},{6,4},{8,10},{10,8},{12,14},{14,12},{16,18},{18,... | collective-permute-start | bytes 3145736 | tf_op jit(solution)/shard_map/ppermute | solution.py:183
  138.5 19.1 %collective-permute-start.22 = (bf16[2,128,2048]{2,1,0:T(8,128)(2,1)}, bf16[2,128,2048]{2,1,0:T(8,128)(2,1)}, u32[]{:S(2)}, u32[]{:S(2)}) collective-permute-start(bf16[2,128,2048]{2,1,0:T(8,128)(2,1)} %pad_maximum_fusion.15), channel_id=1, source_target_pairs={{0,2},{2,0},{4,6},{6,4},{8,10},{10,8},{12,14},{14,12},{16,18},{18,... | collective-permute-start | bytes 3145736 | tf_op jit(solution)/shard_map/ppermute | solution.py:183
  139.6 14.9 %collective-permute-start.19 = (bf16[128,2048]{1,0:T(8,128)(2,1)S(1)}, bf16[128,2048]{1,0:T(8,128)(2,1)}, u32[]{:S(2)}, u32[]{:S(2)}) collective-permute-start(bf16[128,2048]{1,0:T(8,128)(2,1)S(1)} %fusion.57), channel_id=1, source_target_pairs={{0,4},{2,6},{4,0},{6,2},{8,12},{10,14},{12,8},{14,10},{16,20},{18,... | collective-permute-start | bytes 1572872 | tf_op jit(solution)/shard_map/ppermute | solution.py:183
  141.3 33.8 %all-to-all-start.2 = ((bf16[4,128,1920]{2,1,0:T(8,128)(2,1)}), bf16[4,128,1920]{2,1,0:T(8,128)(2,1)}, u32[]{:S(2)}, u32[]{:S(2)}) async-start(bf16[4,128,1920]{2,1,0:T(8,128)(2,1)} %pad_maximum_fusion.9), calls=%async_computation.2 | async-start | bytes 3932160 | tf_op jit(solution)/shard_map/all_to_all | solution.py:210
  145.7 183.6 %all-gather.5.cloned.1.call-start = ((), (), s32[]{:S(2)}) async-start(), calls=%async_computation.12 | async-start | bytes 9830400 | tf_op jit(solution)/shard_map/all_gather | solution.py:228
  155.9 19.2 %collective-permute-start.20 = (bf16[128,2048]{1,0:T(8,128)(2,1)S(1)}, bf16[128,2048]{1,0:T(8,128)(2,1)S(1)}, u32[]{:S(2)}, u32[]{:S(2)}) collective-permute-start(bf16[128,2048]{1,0:T(8,128)(2,1)S(1)} %fusion.59), channel_id=1, source_target_pairs={{0,1},{1,0},{2,3},{3,2},{4,5},{5,4},{6,7},{7,6},{8,9},{9,8},{10,11... | collective-permute-start | bytes 1572872 | tf_op jit(solution)/shard_map/ppermute | solution.py:186
  175.8 310.8 %reduce-scatter.11.cloned.1.call-start = ((), (), s32[]{:S(2)}) async-start(), calls=%async_computation.16 | async-start | bytes 3276800 | tf_op jit(solution)/shard_map/reduce_scatter | solution.py:251
  352.1 259.7 %reduce-scatter.9.cloned.1.call-start = ((), (), s32[]{:S(2)}) async-start(), calls=%async_computation.15 | async-start | bytes 6553600 | tf_op jit(solution)/shard_map/reduce_scatter | solution.py:251
  369.9 263.2 %reduce-scatter.7.cloned.1.call-start = ((), (), s32[]{:S(2)}) async-start(), calls=%async_computation.14 | async-start | bytes 5242880 | tf_op jit(solution)/shard_map/reduce_scatter | solution.py:251
  441.3 42.3 %collective-permute-start.37 = (bf16[2,128,2048]{2,1,0:T(8,128)(2,1)}, bf16[2,128,2048]{2,1,0:T(8,128)(2,1)}, u32[]{:S(2)}, u32[]{:S(2)}) collective-permute-start(bf16[2,128,2048]{2,1,0:T(8,128)(2,1)} %pad_maximum_fusion.22), channel_id=1, source_target_pairs={{0,2},{2,0},{4,6},{6,4},{8,10},{10,8},{12,14},{14,12},{16,18},{18,... | collective-permute-start | bytes 3145736 | tf_op jit(solution)/shard_map/ppermute | solution.py:183
  483.6 19.4 %collective-permute-start.44 = (bf16[2,128,2048]{2,1,0:T(8,128)(2,1)}, bf16[2,128,2048]{2,1,0:T(8,128)(2,1)}, u32[]{:S(2)}, u32[]{:S(2)}) collective-permute-start(bf16[2,128,2048]{2,1,0:T(8,128)(2,1)} %pad_maximum_fusion.24), channel_id=1, source_target_pairs={{0,2},{2,0},{4,6},{6,4},{8,10},{10,8},{12,14},{14,12},{16,18},{18,... | collective-permute-start | bytes 3145736 | tf_op jit(solution)/shard_map/ppermute | solution.py:183
  485.0 14.9 %collective-permute-start.38 = (bf16[128,2048]{1,0:T(8,128)(2,1)S(1)}, bf16[128,2048]{1,0:T(8,128)(2,1)}, u32[]{:S(2)}, u32[]{:S(2)}) collective-permute-start(bf16[128,2048]{1,0:T(8,128)(2,1)S(1)} %fusion.48), channel_id=1, source_target_pairs={{0,4},{2,6},{4,0},{6,2},{8,12},{10,14},{12,8},{14,10},{16,20},{18,... | collective-permute-start | bytes 1572872 | tf_op jit(solution)/shard_map/ppermute | solution.py:183
  488.7 36.3 %all-to-all-start.6 = ((bf16[4,128,640]{1,2,0:T(8,128)(2,1)}), bf16[4,128,640]{1,2,0:T(8,128)(2,1)S(1)}, u32[]{:S(2)}, u32[]{:S(2)}) async-start(bf16[4,128,640]{1,2,0:T(8,128)(2,1)} %copy.156), calls=%async_computation.10 | async-start | bytes 1310720 | tf_op jit(solution)/shard_map/all_to_all | solution.py:210
  501.5 90.3 %collective-permute-start.39 = (bf16[128,2048]{1,0:T(8,128)(2,1)S(1)}, bf16[128,2048]{1,0:T(8,128)(2,1)}, u32[]{:S(2)}, u32[]{:S(2)}) collective-permute-start(bf16[128,2048]{1,0:T(8,128)(2,1)S(1)} %fusion.50), channel_id=1, source_target_pairs={{0,1},{1,0},{2,3},{3,2},{4,5},{5,4},{6,7},{7,6},{8,9},{9,8},{10,11... | collective-permute-start | bytes 1572872 | tf_op jit(solution)/shard_map/ppermute | solution.py:186
  525.0 53.6 %all-to-all-start.3 = ((bf16[4,4,128,1024]{3,2,0,1:T(8,128)(2,1)}), bf16[4,4,128,1024]{3,2,0,1:T(8,128)(2,1)}, u32[]{:S(2)}, u32[]{:S(2)}) async-start(bf16[4,4,128,1024]{3,2,0,1:T(8,128)(2,1)} %copy.153), calls=%async_computation.3 | async-start | bytes 8388608 | tf_op jit(solution)/shard_map/all_to_all | solution.py:381
  529.9 128.7 %reduce-scatter.5.cloned.1.call-start = ((), (), s32[]{:S(2)}) async-start(), calls=%async_computation.13 | async-start | bytes 5242880 | tf_op jit(solution)/shard_map/reduce_scatter | solution.py:251
  539.6 43.7 %collective-permute-start.48 = (bf16[2,128,2048]{2,1,0:T(8,128)(2,1)}, bf16[2,128,2048]{2,1,0:T(8,128)(2,1)}, u32[]{:S(2)}, u32[]{:S(2)}) collective-permute-start(bf16[2,128,2048]{2,1,0:T(8,128)(2,1)} %pad_maximum_fusion.26), channel_id=1, source_target_pairs={{0,2},{2,0},{4,6},{6,4},{8,10},{10,8},{12,14},{14,12},{16,18},{18,... | collective-permute-start | bytes 3145736 | tf_op jit(solution)/shard_map/ppermute | solution.py:183
  541.0 48.8 %collective-permute-start.46 = (bf16[128,2048]{1,0:T(8,128)(2,1)S(1)}, bf16[128,2048]{1,0:T(8,128)(2,1)}, u32[]{:S(2)}, u32[]{:S(2)}) collective-permute-start(bf16[128,2048]{1,0:T(8,128)(2,1)S(1)} %fusion.42), channel_id=1, source_target_pairs={{0,4},{2,6},{4,0},{6,2},{8,12},{10,14},{12,8},{14,10},{16,20},{18,... | collective-permute-start | bytes 1572872 | tf_op jit(solution)/shard_map/ppermute | solution.py:183
  584.7 20.3 %collective-permute-start.49 = (bf16[128,2048]{1,0:T(8,128)(2,1)S(1)}, bf16[128,2048]{1,0:T(8,128)(2,1)S(1)}, u32[]{:S(2)}, u32[]{:S(2)}) collective-permute-start(bf16[128,2048]{1,0:T(8,128)(2,1)S(1)} %fusion.39), channel_id=1, source_target_pairs={{0,4},{2,6},{4,0},{6,2},{8,12},{10,14},{12,8},{14,10},{16,20},{18,... | collective-permute-start | bytes 1572872 | tf_op jit(solution)/shard_map/ppermute | solution.py:183
  607.3 14.6 %collective-permute-start.50 = (bf16[128,2048]{1,0:T(8,128)(2,1)}, bf16[128,2048]{1,0:T(8,128)(2,1)}, u32[]{:S(2)}, u32[]{:S(2)}) collective-permute-start(bf16[128,2048]{1,0:T(8,128)(2,1)} %fusion.41), channel_id=1, source_target_pairs={{0,1},{1,0},{2,3},{3,2},{4,5},{5,4},{6,7},{7,6},{8,9},{9,8},{10,11... | collective-permute-start | bytes 1572872 | tf_op jit(solution)/shard_map/ppermute | solution.py:186
  611.8 21.0 %all-to-all-start.5 = ((bf16[4,128,1280]{2,1,0:T(8,128)(2,1)}), bf16[4,128,1280]{2,1,0:T(8,128)(2,1)S(1)}, u32[]{:S(2)}, u32[]{:S(2)}) async-start(bf16[4,128,1280]{2,1,0:T(8,128)(2,1)} %bitcast.380), calls=%async_computation.8 | async-start | bytes 2621440 | tf_op jit(solution)/shard_map/all_to_all | solution.py:210
  635.3 18.0 %all-to-all-start.4 = ((bf16[4,128,1024]{1,2,0:T(8,128)(2,1)}), bf16[4,128,1024]{1,2,0:T(8,128)(2,1)S(1)}, u32[]{:S(2)}, u32[]{:S(2)}) async-start(bf16[4,128,1024]{1,2,0:T(8,128)(2,1)} %copy.155), calls=%async_computation.6 | async-start | bytes 2097152 | tf_op jit(solution)/shard_map/all_to_all | solution.py:210
  (124 other events, 883.5 us)
Sparse Core Ops, SparseCore 0:
  107.0 81.0 all-gather.2
  189.7 139.5 all-gather.4
  352.2 50.3 reduce-scatter.10
  404.7 93.4 reduce-scatter.8
  500.4 77.2 reduce-scatter.6
  583.5 75.0 reduce-scatter.4

commit v5 on v4

--- a/solution.py
+++ b/solution.py
@@ -227,12 +227,17 @@
         shard = shard.reshape(inner * part, -1)
         return lax.all_gather(shard, "dp", axis_index_groups=planes(inner), tiled=True)
 
-    def ring_start(own, shard):
-        block = [
-            lax.dynamic_index_in_dim(shard, (place % ATTN) ^ j, 0, keepdims=False)
-            for j in range(1, ATTN)
-        ]
-        return [own[None], block[0][None], jnp.stack(block[1:])]
+    def ring_start(weights):
+        def cut(j):
+            pieces = []
+            for w in weights:
+                columns = w.shape[1] // ATTN
+                at = pl.multiple_of(((place % ATTN) ^ j) * columns, columns)
+                pieces.append(lax.dynamic_slice_in_dim(w, at, columns, axis=1))
+            return jnp.concatenate(pieces, axis=1)
+
+        far = jnp.stack([swap(cut(2), 2), swap(cut(3), 3)])
+        return [cut(0)[None], swap(cut(1), 1)[None], far]
 
     def ring_step(held):
         return [lax.ppermute(h, "dp", [(i, (i + ATTN) % dp) for i in range(dp)]) for h in held]
@@ -262,19 +267,18 @@
         held = plane_sum(whole, inner).reshape(inner, part, -1)
         return split(exchange(held, inner), widths)
 
-    packed_self = pack([wq_self, wk_self, wv_self, wo_self.T], ATTN)
-    own_self = lax.dynamic_index_in_dim(packed_self, place % ATTN, 0, keepdims=False)
-    shard_self = exchange(packed_self, ATTN)
+    first = [wq_self, wk_self, wv_self, wo_self.T]
+    ring = dp // ATTN == 4
     packed_cross = pack([wq_cross, wk_cross, wv_cross, wo_cross.T], ATTN)
-    ring = dp // ATTN == 4
     if ring:
-        kept = [ring_start(own_self, shard_self)]
+        kept = [ring_start(first)]
         kept.append(ring_step(kept[0]))
         kept[1][2], inputs, packed_cross = tie(kept[1][2], inputs, packed_cross)
         kept.append(ring_step(kept[1]))
         kept[2][2], gain_self, segments = tie(kept[2][2], gain_self, segments)
         kept.append(ring_step(kept[2]))
     else:
+        shard_self = exchange(pack(first, ATTN), ATTN)
         shard_self, inputs, packed_cross = tie(shard_self, inputs, packed_cross)
         w_self = over_planes(shard_self, ATTN)
     start_rows = rows_of(inputs, ATTN)
@@ -342,12 +346,13 @@
     hidden = (value * up).astype(BF)
 
     term_down = term(grad_rows, hidden)
+    term_down, grad_rows = tie(term_down, grad_rows)
     grad_hidden = dot(grad_rows, w_dn, 1, 0)
     grad_gu = jnp.concatenate(
         [(grad_hidden * up * slope).astype(BF), (grad_hidden * value).astype(BF)], axis=1
     )
     term_gu = term(normed_ffn, grad_gu)
-    grad_gu, term_down, term_gu = tie(grad_gu, term_down, term_gu)
+    grad_gu, term_gu = tie(grad_gu, term_gu)
     (grad_w_down,) = scatter_weights(term_down, [fw], FFN)
     grad_w_gate, grad_w_up = scatter_weights(term_gu, [fw, fw], FFN)
     grad_normed = reduce_rows(dot(grad_gu, w_gu, 1, 1), FFN)

time: 682 us -> 667 us (0.978)
  starting transfers between devices: 88.8 us -> 76.3 us
    reduce_scatter x4, starting transfers between devices: 9.53 us -> 0.68 us  [plane_sum(): lax.psum_scatter(whole, 'dp', axis_index_groups=planes(inner), tiled=True)]
    slice x11 -> x7, local copies, waits for them, and re-layouts: 10 us -> 2.97 us  [pack(): w[:, i * (w.shape[1] // inner):(i + 1) * (w.shape[1] // inner)]]
    all_to_all x6 -> x5, starting transfers between devices: 24 us -> 19.7 us  [exchange(): lax.all_to_all(blocks, 'dp', 0, 0, axis_index_groups=groups, tiled=True)]
    unnamed x195 -> x185, local copies, waits for them, and re-layouts: 20.5 us -> 23.2 us
    ppermute x39 -> x42, waiting for transfers between devices: 132 us -> 134 us  [swap(): return lax.ppermute(value, 'dp', [(i, i ^ distance) for i in range(dp)])]
    dynamic_update_slice x16 -> x15, local copies, waits for them, and re-layouts: 18.4 us -> 17.3 us  [placed(): full = lax.dynamic_update_slice(full, h[n], (at, 0))]
    ppermute x39 -> x42, starting transfers between devices: 34.6 us -> 34.8 us  [swap(): return lax.ppermute(value, 'dp', [(i, i ^ distance) for i in range(dp)])]
    all_to_all x6 -> x5, waiting for transfers between devices: 34.8 us -> 34.8 us  [exchange(): lax.all_to_all(blocks, 'dp', 0, 0, axis_index_groups=groups, tiled=True)]
  transfers between devices with their start and end apart: 68 -> 70, of which waited for: 36 -> 36; matrix products, arithmetic and copies ran while one was open for 22% -> 25% of each run, Pallas kernels for 3% -> 3%
where the time goes in v5:
time: 667 us; the launch traced here: 656 us
  waiting for transfers between devices  348 us (52%)
  starting transfers between devices  76.3 us (11%)
  local copies, waits for them, and re-layouts  73.2 us (11%)
  matrix products  62.8 us (9%)
  other arithmetic  59.7 us (9%)
  Pallas kernels  19.8 us (3%)
  between operations  16.5 us (2%)
    ppermute x42, waiting for transfers between devices, swap(): return lax.ppermute(value, 'dp', [(i, i ^ distance) for i in range(dp)])  134 us
    all_gather x2, waiting for transfers between devices, over_planes(): lax.all_gather(shard, 'dp', axis_index_groups=planes(inner), tiled=True)  70.3 us
    dot_general x21, matrix products, dot(): lax.dot_general(a, b, (((da,), (db,)), ((), ())), preferred_element_type=...  62.8 us
    ppermute x7, waiting for transfers between devices, swap_mp(): return lax.ppermute(value, 'mp', [(0, 1), (1, 0)])  43.4 us
    all_to_all x5, waiting for transfers between devices, exchange(): lax.all_to_all(blocks, 'dp', 0, 0, axis_index_groups=groups, tiled=True)  34.8 us
    ppermute x42, starting transfers between devices, swap(): return lax.ppermute(value, 'dp', [(i, i ^ distance) for i in range(dp)])  34.8 us
    all_to_all x1, waiting for transfers between devices, on_device(): lax.all_to_all(term_self.reshape(-1, ATTN, part, 4 * hw), 'dp', 1, 1, axi...  34.4 us
    ppermute x9, waiting for transfers between devices, ring_step(): lax.ppermute(h, 'dp', [(i, (i + ATTN) % dp) for i in range(dp)])  30.9 us
  transfers between devices with their start and end apart: 70, of which 36 were waited for; matrix products, arithmetic and copies ran while one was open for 25% of the time, Pallas kernels for 3%

profile of v5, /device:TPU:0, one launch (start us, length us, event | category | flops | bytes accessed | tf_op | source)
XLA Modules:
  0.0 656.2 jit_solution(14223025386566565577)
XLA Ops:
  37.9 14.0 %collective-permute-done.16 = bf16[1,128,1024]{1,2,0:T(8,128)(2,1)S(1)} collective-permute-done((bf16[1,128,1024]{1,2,0:T(8,128)(2,1)}, bf16[1,128,1024]{1,2,0:T(8,128)(2,1)S(1)}, u32[]{:S(2)}, u32[]{:S(2)}) %collective-permute-start.16) | collective-permute-done | bytes 262176 | tf_op jit(solution)/shard_map/ppermute | solution.py:243
  52.0 5.6 collective-permute-done.17
  68.9 11.3 %collective-permute-done.3 = bf16[2,128,1024]{1,2,0:T(8,128)(2,1)} collective-permute-done((bf16[2,128,1024]{1,2,0:T(8,128)(2,1)S(1)}, bf16[2,128,1024]{1,2,0:T(8,128)(2,1)}, u32[]{:S(2)}, u32[]{:S(2)}) %collective-permute-start.3) | collective-permute-done | bytes 524320 | tf_op jit(solution)/shard_map/ppermute | solution.py:243
  105.4 4.6 fusion.19.q_ref.k_ref.v_ref
  119.1 12.6 %collective-permute-done.24 = bf16[128,2048]{1,0:T(8,128)(2,1)S(1)} collective-permute-done((bf16[128,2048]{1,0:T(8,128)(2,1)S(1)}, bf16[128,2048]{1,0:T(8,128)(2,1)S(1)}, u32[]{:S(2)}, u32[]{:S(2)}) %collective-permute-start.24) | collective-permute-done | bytes 524320 | tf_op jit(solution)/shard_map/ppermute | solution.py:183
  140.0 8.8 %collective-permute-done.22 = bf16[128,2048]{1,0:T(8,128)(2,1)} collective-permute-done((bf16[128,2048]{1,0:T(8,128)(2,1)S(1)}, bf16[128,2048]{1,0:T(8,128)(2,1)}, u32[]{:S(2)}, u32[]{:S(2)}) %collective-permute-start.22) | collective-permute-done | bytes 524320 | tf_op jit(solution)/shard_map/ppermute | solution.py:183
  154.7 14.8 %all-to-all-done.1 = bf16[4,128,1920]{2,1,0:T(8,128)(2,1)} async-done(((bf16[4,128,1920]{2,1,0:T(8,128)(2,1)}), bf16[4,128,1920]{2,1,0:T(8,128)(2,1)}, u32[]{:S(2)}, u32[]{:S(2)}) %all-to-all-start.1) | async-done | bytes 1966112 | tf_op jit(solution)/shard_map/all_to_all | solution.py:210
  173.1 12.1 %collective-permute-done.26 = bf16[128,2048]{1,0:T(8,128)(2,1)S(1)} collective-permute-done((bf16[128,2048]{1,0:T(8,128)(2,1)S(1)}, bf16[128,2048]{1,0:T(8,128)(2,1)S(1)}, u32[]{:S(2)}, u32[]{:S(2)}) %collective-permute-start.26) | collective-permute-done | bytes 524320 | tf_op jit(solution)/shard_map/ppermute | solution.py:183
  209.6 12.5 %collective-permute-done.29 = bf16[128,2048]{1,0:T(8,128)(2,1)S(1)} collective-permute-done((bf16[128,2048]{1,0:T(8,128)(2,1)S(1)}, bf16[128,2048]{1,0:T(8,128)(2,1)S(1)}, u32[]{:S(2)}, u32[]{:S(2)}) %collective-permute-start.29) | collective-permute-done | bytes 524320 | tf_op jit(solution)/shard_map/ppermute | solution.py:183
  225.4 10.3 %collective-permute-done.30 = bf16[128,2048]{1,0:T(8,128)(2,1)S(1)} collective-permute-done((bf16[128,2048]{1,0:T(8,128)(2,1)S(1)}, bf16[128,2048]{1,0:T(8,128)(2,1)S(1)}, u32[]{:S(2)}, u32[]{:S(2)}) %collective-permute-start.30) | collective-permute-done | bytes 524320 | tf_op jit(solution)/shard_map/ppermute | solution.py:186
  238.0 10.6 %collective-permute-done.33 = bf16[128,2048]{1,0:T(8,128)(2,1)S(1)} collective-permute-done((bf16[128,2048]{1,0:T(8,128)(2,1)S(1)}, bf16[128,2048]{1,0:T(8,128)(2,1)S(1)}, u32[]{:S(2)}, u32[]{:S(2)}) %collective-permute-start.33) | collective-permute-done | bytes 524320 | tf_op jit(solution)/shard_map/ppermute | solution.py:183
  253.4 70.3 %all-gather.5.cloned.1.call-done = bf16[2048,1920]{1,0:T(8,128)(2,1)} async-done(((bf16[512,1920]{1,0:T(8,128)(2,1)}), bf16[2048,1920]{1,0:T(8,128)(2,1)}) %all-gather.5.cloned.1.call-update) | async-done | bytes 7864336 | tf_op jit(solution)/shard_map/all_gather | solution.py:228
  323.7 6.0 fusion.2
  336.0 5.5 fusion.28
  343.6 4.7 convolution_convert_fusion
  348.2 5.8 fusion.7
  361.5 12.5 %collective-permute-done.36 = bf16[128,2048]{1,0:T(8,128)(2,1)S(1)} collective-permute-done((bf16[128,2048]{1,0:T(8,128)(2,1)S(1)}, bf16[128,2048]{1,0:T(8,128)(2,1)S(1)}, u32[]{:S(2)}, u32[]{:S(2)}) %collective-permute-start.36) | collective-permute-done | bytes 524320 | tf_op jit(solution)/shard_map/ppermute | solution.py:183
  377.0 11.8 %collective-permute-done.37 = bf16[128,2048]{1,0:T(8,128)(2,1)S(1)} collective-permute-done((bf16[128,2048]{1,0:T(8,128)(2,1)S(1)}, bf16[128,2048]{1,0:T(8,128)(2,1)S(1)}, u32[]{:S(2)}, u32[]{:S(2)}) %collective-permute-start.37) | collective-permute-done | bytes 524320 | tf_op jit(solution)/shard_map/ppermute | solution.py:186
  392.1 10.9 %collective-permute-done.38 = bf16[128,2048]{1,0:T(8,128)(2,1)S(1)} collective-permute-done((bf16[128,2048]{1,0:T(8,128)(2,1)S(1)}, bf16[128,2048]{1,0:T(8,128)(2,1)S(1)}, u32[]{:S(2)}, u32[]{:S(2)}) %collective-permute-start.38) | collective-permute-done | bytes 524320 | tf_op jit(solution)/shard_map/ppermute | solution.py:183
  410.1 5.4 shard_map.316
  427.8 10.7 %collective-permute-done.44 = bf16[128,2048]{1,0:T(8,128)(2,1)S(1)} collective-permute-done((bf16[128,2048]{1,0:T(8,128)(2,1)S(1)}, bf16[128,2048]{1,0:T(8,128)(2,1)S(1)}, u32[]{:S(2)}, u32[]{:S(2)}) %collective-permute-start.44) | collective-permute-done | bytes 524320 | tf_op jit(solution)/shard_map/ppermute | solution.py:183
  443.4 8.8 %collective-permute-done.45 = bf16[128,2048]{1,0:T(8,128)(2,1)} collective-permute-done((bf16[128,2048]{1,0:T(8,128)(2,1)S(1)}, bf16[128,2048]{1,0:T(8,128)(2,1)}, u32[]{:S(2)}, u32[]{:S(2)}) %collective-permute-start.45) | collective-permute-done | bytes 524320 | tf_op jit(solution)/shard_map/ppermute | solution.py:186
  457.6 10.9 %collective-permute-done.46 = bf16[128,2048]{1,0:T(8,128)(2,1)S(1)} collective-permute-done((bf16[128,2048]{1,0:T(8,128)(2,1)S(1)}, bf16[128,2048]{1,0:T(8,128)(2,1)S(1)}, u32[]{:S(2)}, u32[]{:S(2)}) %collective-permute-start.46) | collective-permute-done | bytes 524320 | tf_op jit(solution)/shard_map/ppermute | solution.py:183
  478.3 7.5 %collective-permute-done.41 = bf16[128,2048]{1,0:T(8,128)(2,1)} collective-permute-done((bf16[128,2048]{1,0:T(8,128)(2,1)S(1)}, bf16[128,2048]{1,0:T(8,128)(2,1)}, u32[]{:S(2)}, u32[]{:S(2)}) %collective-permute-start.41) | collective-permute-done | bytes 524320 | tf_op jit(solution)/shard_map/ppermute | solution.py:183
  494.5 5.4 shard_map.317
  510.6 4.8 all-to-all-start.2
  529.8 34.4 %all-to-all-done.2 = bf16[4,4,128,1024]{3,2,0,1:T(8,128)(2,1)} async-done(((bf16[4,4,128,1024]{3,2,0,1:T(8,128)(2,1)}), bf16[4,4,128,1024]{3,2,0,1:T(8,128)(2,1)}, u32[]{:S(2)}, u32[]{:S(2)}) %all-to-all-start.2) | async-done | bytes 4194336 | tf_op jit(solution)/shard_map/all_to_all | solution.py:386
  564.2 4.7 copy.154
  570.4 4.9 collective-permute-done.49
  579.8 10.1 %collective-permute-done.50 = bf16[128,2048]{1,0:T(8,128)(2,1)S(1)} collective-permute-done((bf16[128,2048]{1,0:T(8,128)(2,1)S(1)}, bf16[128,2048]{1,0:T(8,128)(2,1)S(1)}, u32[]{:S(2)}, u32[]{:S(2)}) %collective-permute-start.50) | collective-permute-done | bytes 524320 | tf_op jit(solution)/shard_map/ppermute | solution.py:186
  611.1 8.0 %all-to-all-done.4 = bf16[4,128,1280]{2,1,0:T(8,128)(2,1)S(1)} async-done(((bf16[4,128,1280]{2,1,0:T(8,128)(2,1)}), bf16[4,128,1280]{2,1,0:T(8,128)(2,1)S(1)}, u32[]{:S(2)}, u32[]{:S(2)}) %all-to-all-start.4) | async-done | bytes 1310752 | tf_op jit(solution)/shard_map/all_to_all | solution.py:210
  627.5 12.0 %all-to-all-done.3 = bf16[4,128,1024]{1,2,0:T(8,128)(2,1)S(1)} async-done(((bf16[4,128,1024]{1,2,0:T(8,128)(2,1)}), bf16[4,128,1024]{1,2,0:T(8,128)(2,1)S(1)}, u32[]{:S(2)}, u32[]{:S(2)}) %all-to-all-start.3) | async-done | bytes 1048608 | tf_op jit(solution)/shard_map/all_to_all | solution.py:210
  (501 shorter events, 267.6 us)
Async XLA Ops:
  10.5 19.1 %collective-permute-start = (bf16[128,1024]{0,1:T(8,128)(2,1)}, bf16[128,1024]{0,1:T(8,128)(2,1)S(1)}, u32[]{:S(2)}, u32[]{:S(2)}) collective-permute-start(bf16[128,1024]{0,1:T(8,128)(2,1)} %pad_maximum_fusion.31), channel_id=1, source_target_pairs={{0,4},{2,6},{4,0},{6,2},{8,12},{10,14},{12,8},{14,10},{16,20},{18,... | collective-permute-start | bytes 786440 | tf_op jit(solution)/shard_map/ppermute | solution.py:183
  15.6 15.7 %collective-permute-start.14 = (bf16[128,1024]{0,1:T(8,128)(2,1)}, bf16[128,1024]{0,1:T(8,128)(2,1)}, u32[]{:S(2)}, u32[]{:S(2)}) collective-permute-start(bf16[128,1024]{0,1:T(8,128)(2,1)} %pad_maximum_fusion.34), channel_id=1, source_target_pairs={{0,2},{2,0},{4,6},{6,4},{8,10},{10,8},{12,14},{14,12},{16,18},{18,... | collective-permute-start | bytes 786440 | tf_op jit(solution)/shard_map/ppermute | solution.py:183
  29.7 28.7 %collective-permute-start.2 = (bf16[2,128,1024]{1,2,0:T(8,128)(2,1)S(1)}, bf16[2,128,1024]{1,2,0:T(8,128)(2,1)S(1)}, u32[]{:S(2)}, u32[]{:S(2)}) collective-permute-start(bf16[2,128,1024]{1,2,0:T(8,128)(2,1)S(1)} %pad_maximum_fusion.26), channel_id=1, source_target_pairs={{0,8},{2,10},{4,12},{6,14},{8,16},{10,18},{12,20},{14,22},{16,24},... | collective-permute-start | bytes 1572872 | tf_op jit(solution)/shard_map/ppermute | solution.py:243
  31.3 20.7 %collective-permute-start.16 = (bf16[1,128,1024]{1,2,0:T(8,128)(2,1)}, bf16[1,128,1024]{1,2,0:T(8,128)(2,1)S(1)}, u32[]{:S(2)}, u32[]{:S(2)}) collective-permute-start(bf16[1,128,1024]{1,2,0:T(8,128)(2,1)} %bitcast.62), channel_id=1, source_target_pairs={{0,8},{2,10},{4,12},{6,14},{8,16},{10,18},{12,20},{14,22},{16,24},... | collective-permute-start | bytes 786440 | tf_op jit(solution)/shard_map/ppermute | solution.py:243
  32.9 24.7 %collective-permute-start.17 = (bf16[1,128,1024]{1,2,0:T(8,128)(2,1)}, bf16[1,128,1024]{1,2,0:T(8,128)(2,1)S(1)}, u32[]{:S(2)}, u32[]{:S(2)}) collective-permute-start(bf16[1,128,1024]{1,2,0:T(8,128)(2,1)} %collective-permute-done.15), channel_id=1, source_target_pairs={{0,8},{2,10},{4,12},{6,14},{8,16},{10,18},{12,20},{14,22},{16,24},... | collective-permute-start | bytes 786440 | tf_op jit(solution)/shard_map/ppermute | solution.py:243
  52.0 15.3 %collective-permute-start.18 = (bf16[1,128,1024]{1,2,0:T(8,128)(2,1)S(1)}, bf16[1,128,1024]{1,2,0:T(8,128)(2,1)S(1)}, u32[]{:S(2)}, u32[]{:S(2)}) collective-permute-start(bf16[1,128,1024]{1,2,0:T(8,128)(2,1)S(1)} %collective-permute-done.16), channel_id=1, source_target_pairs={{0,8},{2,10},{4,12},{6,14},{8,16},{10,18},{12,20},{14,22},{16,24},... | collective-permute-start | bytes 786440 | tf_op jit(solution)/shard_map/ppermute | solution.py:243
  57.6 28.8 %collective-permute-start.19 = (bf16[1,128,1024]{1,2,0:T(8,128)(2,1)S(1)}, bf16[1,128,1024]{1,2,0:T(8,128)(2,1)S(1)}, u32[]{:S(2)}, u32[]{:S(2)}) collective-permute-start(bf16[1,128,1024]{1,2,0:T(8,128)(2,1)S(1)} %collective-permute-done.17), channel_id=1, source_target_pairs={{0,8},{2,10},{4,12},{6,14},{8,16},{10,18},{12,20},{14,22},{16,24},... | collective-permute-start | bytes 786440 | tf_op jit(solution)/shard_map/ppermute | solution.py:243
  58.4 31.8 %collective-permute-start.7 = (bf16[128,2048]{1,0:T(8,128)(2,1)S(1)}, bf16[128,2048]{1,0:T(8,128)(2,1)S(1)}, u32[]{:S(2)}, u32[]{:S(2)}) collective-permute-start(bf16[128,2048]{1,0:T(8,128)(2,1)S(1)} %copy-done), channel_id=1, source_target_pairs={{0,4},{2,6},{4,0},{6,2},{8,12},{10,14},{12,8},{14,10},{16,20},{18,... | collective-permute-start | bytes 1572872 | tf_op jit(solution)/shard_map/ppermute | solution.py:183
  60.0 20.2 %collective-permute-start.3 = (bf16[2,128,1024]{1,2,0:T(8,128)(2,1)S(1)}, bf16[2,128,1024]{1,2,0:T(8,128)(2,1)}, u32[]{:S(2)}, u32[]{:S(2)}) collective-permute-start(bf16[2,128,1024]{1,2,0:T(8,128)(2,1)S(1)} %collective-permute-done.2), channel_id=1, source_target_pairs={{0,8},{2,10},{4,12},{6,14},{8,16},{10,18},{12,20},{14,22},{16,24},... | collective-permute-start | bytes 1572872 | tf_op jit(solution)/shard_map/ppermute | solution.py:243
  61.3 40.0 %all-to-all-start = ((bf16[4,128,1024]{2,1,0:T(8,128)(2,1)}), bf16[4,128,1024]{2,1,0:T(8,128)(2,1)}, u32[]{:S(2)}, u32[]{:S(2)}) async-start(bf16[4,128,1024]{2,1,0:T(8,128)(2,1)} %pad_maximum_fusion.11), calls=%async_computation | async-start | bytes 2097152 | tf_op jit(solution)/shard_map/all_to_all | solution.py:210
  65.6 126.0 %all-gather.3.cloned.1.call-start = ((), (), s32[]{:S(2)}) async-start(), calls=%async_computation.10 | async-start | bytes 5242880 | tf_op jit(solution)/shard_map/all_gather | solution.py:228
  67.2 23.2 %collective-permute-start.20 = (bf16[1,128,1024]{1,2,0:T(8,128)(2,1)S(1)}, bf16[1,128,1024]{1,2,0:T(8,128)(2,1)S(1)}, u32[]{:S(2)}, u32[]{:S(2)}) collective-permute-start(bf16[1,128,1024]{1,2,0:T(8,128)(2,1)S(1)} %collective-permute-done.18), channel_id=1, source_target_pairs={{0,8},{2,10},{4,12},{6,14},{8,16},{10,18},{12,20},{14,22},{16,24},... | collective-permute-start | bytes 786440 | tf_op jit(solution)/shard_map/ppermute | solution.py:243
  80.2 21.1 %collective-permute-start.6 = (bf16[2,128,1024]{1,2,0:T(8,128)(2,1)}, bf16[2,128,1024]{1,2,0:T(8,128)(2,1)}, u32[]{:S(2)}, u32[]{:S(2)}) collective-permute-start(bf16[2,128,1024]{1,2,0:T(8,128)(2,1)} %collective-permute-done.3), channel_id=1, source_target_pairs={{0,8},{2,10},{4,12},{6,14},{8,16},{10,18},{12,20},{14,22},{16,24},... | collective-permute-start | bytes 1572872 | tf_op jit(solution)/shard_map/ppermute | solution.py:243
  116.8 16.0 %collective-permute-start.21 = (bf16[2,128,2048]{2,1,0:T(8,128)(2,1)S(1)}, bf16[2,128,2048]{2,1,0:T(8,128)(2,1)S(1)}, u32[]{:S(2)}, u32[]{:S(2)}) collective-permute-start(bf16[2,128,2048]{2,1,0:T(8,128)(2,1)S(1)} %pad_maximum_fusion.13), channel_id=1, source_target_pairs={{0,2},{2,0},{4,6},{6,4},{8,10},{10,8},{12,14},{14,12},{16,18},{18,... | collective-permute-start | bytes 3145736 | tf_op jit(solution)/shard_map/ppermute | solution.py:183
  132.8 19.0 %collective-permute-start.25 = (bf16[2,128,2048]{2,1,0:T(8,128)(2,1)}, bf16[2,128,2048]{2,1,0:T(8,128)(2,1)}, u32[]{:S(2)}, u32[]{:S(2)}) collective-permute-start(bf16[2,128,2048]{2,1,0:T(8,128)(2,1)} %pad_maximum_fusion.14), channel_id=1, source_target_pairs={{0,2},{2,0},{4,6},{6,4},{8,10},{10,8},{12,14},{14,12},{16,18},{18,... | collective-permute-start | bytes 3145736 | tf_op jit(solution)/shard_map/ppermute | solution.py:183
  135.5 34.0 %all-to-all-start.1 = ((bf16[4,128,1920]{2,1,0:T(8,128)(2,1)}), bf16[4,128,1920]{2,1,0:T(8,128)(2,1)}, u32[]{:S(2)}, u32[]{:S(2)}) async-start(bf16[4,128,1920]{2,1,0:T(8,128)(2,1)} %pad_maximum_fusion.9), calls=%async_computation.1 | async-start | bytes 3932160 | tf_op jit(solution)/shard_map/all_to_all | solution.py:210
  139.9 183.8 %all-gather.5.cloned.1.call-start = ((), (), s32[]{:S(2)}) async-start(), calls=%async_computation.11 | async-start | bytes 9830400 | tf_op jit(solution)/shard_map/all_gather | solution.py:228
  150.3 19.2 %collective-permute-start.23 = (bf16[128,2048]{1,0:T(8,128)(2,1)S(1)}, bf16[128,2048]{1,0:T(8,128)(2,1)}, u32[]{:S(2)}, u32[]{:S(2)}) collective-permute-start(bf16[128,2048]{1,0:T(8,128)(2,1)S(1)} %fusion.59), channel_id=1, source_target_pairs={{0,1},{1,0},{2,3},{3,2},{4,5},{5,4},{6,7},{7,6},{8,9},{9,8},{10,11... | collective-permute-start | bytes 1572872 | tf_op jit(solution)/shard_map/ppermute | solution.py:186
  171.2 301.3 %reduce-scatter.11.cloned.1.call-start = ((), (), s32[]{:S(2)}) async-start(), calls=%async_computation.15 | async-start | bytes 3276800 | tf_op jit(solution)/shard_map/reduce_scatter | solution.py:256
  336.0 262.0 %reduce-scatter.9.cloned.1.call-start = ((), (), s32[]{:S(2)}) async-start(), calls=%async_computation.14 | async-start | bytes 6553600 | tf_op jit(solution)/shard_map/reduce_scatter | solution.py:256
  355.8 263.5 %reduce-scatter.7.cloned.1.call-start = ((), (), s32[]{:S(2)}) async-start(), calls=%async_computation.13 | async-start | bytes 5242880 | tf_op jit(solution)/shard_map/reduce_scatter | solution.py:256
  427.0 42.6 %collective-permute-start.40 = (bf16[2,128,2048]{2,1,0:T(8,128)(2,1)}, bf16[2,128,2048]{2,1,0:T(8,128)(2,1)}, u32[]{:S(2)}, u32[]{:S(2)}) collective-permute-start(bf16[2,128,2048]{2,1,0:T(8,128)(2,1)} %pad_maximum_fusion.21), channel_id=1, source_target_pairs={{0,2},{2,0},{4,6},{6,4},{8,10},{10,8},{12,14},{14,12},{16,18},{18,... | collective-permute-start | bytes 3145736 | tf_op jit(solution)/shard_map/ppermute | solution.py:183
  469.6 19.4 %collective-permute-start.47 = (bf16[2,128,2048]{2,1,0:T(8,128)(2,1)}, bf16[2,128,2048]{2,1,0:T(8,128)(2,1)}, u32[]{:S(2)}, u32[]{:S(2)}) collective-permute-start(bf16[2,128,2048]{2,1,0:T(8,128)(2,1)} %pad_maximum_fusion.23), channel_id=1, source_target_pairs={{0,2},{2,0},{4,6},{6,4},{8,10},{10,8},{12,14},{14,12},{16,18},{18,... | collective-permute-start | bytes 3145736 | tf_op jit(solution)/shard_map/ppermute | solution.py:183
  474.6 36.0 %all-to-all-start.5 = ((bf16[4,128,640]{1,2,0:T(8,128)(2,1)}), bf16[4,128,640]{1,2,0:T(8,128)(2,1)S(1)}, u32[]{:S(2)}, u32[]{:S(2)}) async-start(bf16[4,128,640]{1,2,0:T(8,128)(2,1)} %copy.156), calls=%async_computation.9 | async-start | bytes 1310720 | tf_op jit(solution)/shard_map/all_to_all | solution.py:210
  487.4 90.2 %collective-permute-start.42 = (bf16[128,2048]{1,0:T(8,128)(2,1)S(1)}, bf16[128,2048]{1,0:T(8,128)(2,1)}, u32[]{:S(2)}, u32[]{:S(2)}) collective-permute-start(bf16[128,2048]{1,0:T(8,128)(2,1)S(1)} %fusion.50), channel_id=1, source_target_pairs={{0,1},{1,0},{2,3},{3,2},{4,5},{5,4},{6,7},{7,6},{8,9},{9,8},{10,11... | collective-permute-start | bytes 1572872 | tf_op jit(solution)/shard_map/ppermute | solution.py:186
  510.6 53.5 %all-to-all-start.2 = ((bf16[4,4,128,1024]{3,2,0,1:T(8,128)(2,1)}), bf16[4,4,128,1024]{3,2,0,1:T(8,128)(2,1)}, u32[]{:S(2)}, u32[]{:S(2)}) async-start(bf16[4,4,128,1024]{3,2,0,1:T(8,128)(2,1)} %copy.153), calls=%async_computation.2 | async-start | bytes 8388608 | tf_op jit(solution)/shard_map/all_to_all | solution.py:386
  515.5 128.5 %reduce-scatter.5.cloned.1.call-start = ((), (), s32[]{:S(2)}) async-start(), calls=%async_computation.12 | async-start | bytes 5242880 | tf_op jit(solution)/shard_map/reduce_scatter | solution.py:256
  525.5 43.4 %collective-permute-start.51 = (bf16[2,128,2048]{2,1,0:T(8,128)(2,1)}, bf16[2,128,2048]{2,1,0:T(8,128)(2,1)}, u32[]{:S(2)}, u32[]{:S(2)}) collective-permute-start(bf16[2,128,2048]{2,1,0:T(8,128)(2,1)} %pad_maximum_fusion.25), channel_id=1, source_target_pairs={{0,2},{2,0},{4,6},{6,4},{8,10},{10,8},{12,14},{14,12},{16,18},{18,... | collective-permute-start | bytes 3145736 | tf_op jit(solution)/shard_map/ppermute | solution.py:183
  526.9 48.3 %collective-permute-start.49 = (bf16[128,2048]{1,0:T(8,128)(2,1)S(1)}, bf16[128,2048]{1,0:T(8,128)(2,1)S(1)}, u32[]{:S(2)}, u32[]{:S(2)}) collective-permute-start(bf16[128,2048]{1,0:T(8,128)(2,1)S(1)} %fusion.42), channel_id=1, source_target_pairs={{0,4},{2,6},{4,0},{6,2},{8,12},{10,14},{12,8},{14,10},{16,20},{18,... | collective-permute-start | bytes 1572872 | tf_op jit(solution)/shard_map/ppermute | solution.py:183
  570.3 20.5 %collective-permute-start.52 = (bf16[128,2048]{1,0:T(8,128)(2,1)S(1)}, bf16[128,2048]{1,0:T(8,128)(2,1)S(1)}, u32[]{:S(2)}, u32[]{:S(2)}) collective-permute-start(bf16[128,2048]{1,0:T(8,128)(2,1)S(1)} %fusion.39), channel_id=1, source_target_pairs={{0,4},{2,6},{4,0},{6,2},{8,12},{10,14},{12,8},{14,10},{16,20},{18,... | collective-permute-start | bytes 1572872 | tf_op jit(solution)/shard_map/ppermute | solution.py:183
  598.0 21.0 %all-to-all-start.4 = ((bf16[4,128,1280]{2,1,0:T(8,128)(2,1)}), bf16[4,128,1280]{2,1,0:T(8,128)(2,1)S(1)}, u32[]{:S(2)}, u32[]{:S(2)}) async-start(bf16[4,128,1280]{2,1,0:T(8,128)(2,1)} %bitcast.378), calls=%async_computation.7 | async-start | bytes 2621440 | tf_op jit(solution)/shard_map/all_to_all | solution.py:210
  621.6 18.0 %all-to-all-start.3 = ((bf16[4,128,1024]{1,2,0:T(8,128)(2,1)}), bf16[4,128,1024]{1,2,0:T(8,128)(2,1)S(1)}, u32[]{:S(2)}, u32[]{:S(2)}) async-start(bf16[4,128,1024]{1,2,0:T(8,128)(2,1)} %copy.155), calls=%async_computation.5 | async-start | bytes 2097152 | tf_op jit(solution)/shard_map/all_to_all | solution.py:210
  (121 other events, 780.9 us)
Sparse Core Ops, SparseCore 0:
  101.4 81.0 all-gather.2
  184.1 139.5 all-gather.4
  336.1 50.3 reduce-scatter.10
  388.6 93.4 reduce-scatter.8
  484.2 77.2 reduce-scatter.6
  569.1 74.8 reduce-scatter.4

commit v6 on v5

--- a/solution.py
+++ b/solution.py
@@ -275,7 +275,6 @@
         kept.append(ring_step(kept[0]))
         kept[1][2], inputs, packed_cross = tie(kept[1][2], inputs, packed_cross)
         kept.append(ring_step(kept[1]))
-        kept[2][2], gain_self, segments = tie(kept[2][2], gain_self, segments)
         kept.append(ring_step(kept[2]))
     else:
         shard_self = exchange(pack(first, ATTN), ATTN)
@@ -289,6 +288,7 @@
         kept[3][2], shard_cross, start_rows, patch_rows, packed_ffn, grad_out = tie(
             kept[3][2], shard_cross, start_rows, patch_rows, packed_ffn, grad_out
         )
+        kept[3][2], gain_self, segments = tie(kept[3][2], gain_self, segments)
         w_self = placed(kept)
     w_cross = over_planes(shard_cross, ATTN)
     memory = rows_of(patch_rows, ATTN)

time: 667 us -> 666 us (level)
  starting transfers between devices: 76.3 us -> 68.2 us
  waiting for transfers between devices: 348 us -> 355 us
    all_gather x2, waiting for transfers between devices: 70.3 us -> 61.9 us  [over_planes(): lax.all_gather(shard, 'dp', axis_index_groups=planes(inner), tiled=True)]
    ppermute x42, starting transfers between devices: 34.8 us -> 26.4 us  [swap(): return lax.ppermute(value, 'dp', [(i, i ^ distance) for i in range(dp)])]
    ppermute x9, waiting for transfers between devices: 30.9 us -> 38 us  [ring_step(): lax.ppermute(h, 'dp', [(i, (i + ATTN) % dp) for i in range(dp)])]
    ppermute x42, waiting for transfers between devices: 134 us -> 140 us  [swap(): return lax.ppermute(value, 'dp', [(i, i ^ distance) for i in range(dp)])]
    unnamed x185 -> x187, local copies, waits for them, and re-layouts: 23.2 us -> 22.1 us
  transfers between devices with their start and end apart: 70 -> 70, of which waited for: 36 -> 39; matrix products, arithmetic and copies ran while one was open for 25% -> 25% of each run, Pallas kernels for 3% -> 3%
where the time goes in v6:
time: 666 us; the launch traced here: 655 us
  waiting for transfers between devices  355 us (53%)
  local copies, waits for them, and re-layouts  73.3 us (11%)
  starting transfers between devices  68.2 us (10%)
  matrix products  62.6 us (9%)
  other arithmetic  59.8 us (9%)
  Pallas kernels  19.8 us (3%)
  between operations  16.5 us (2%)
    ppermute x42, waiting for transfers between devices, swap(): return lax.ppermute(value, 'dp', [(i, i ^ distance) for i in range(dp)])  140 us
    dot_general x21, matrix products, dot(): lax.dot_general(a, b, (((da,), (db,)), ((), ())), preferred_element_type=...  62.6 us
    all_gather x2, waiting for transfers between devices, over_planes(): lax.all_gather(shard, 'dp', axis_index_groups=planes(inner), tiled=True)  61.9 us
    ppermute x7, waiting for transfers between devices, swap_mp(): return lax.ppermute(value, 'mp', [(0, 1), (1, 0)])  44.6 us
    ppermute x9, waiting for transfers between devices, ring_step(): lax.ppermute(h, 'dp', [(i, (i + ATTN) % dp) for i in range(dp)])  38 us
    all_to_all x5, waiting for transfers between devices, exchange(): lax.all_to_all(blocks, 'dp', 0, 0, axis_index_groups=groups, tiled=True)  35 us
    all_to_all x1, waiting for transfers between devices, on_device(): lax.all_to_all(term_self.reshape(-1, ATTN, part, 4 * hw), 'dp', 1, 1, axi...  34.4 us
    ppermute x42, starting transfers between devices, swap(): return lax.ppermute(value, 'dp', [(i, i ^ distance) for i in range(dp)])  26.4 us
  transfers between devices with their start and end apart: 70, of which 39 were waited for; matrix products, arithmetic and copies ran while one was open for 25% of the time, Pallas kernels for 3%

profile of v6, /device:TPU:0, one launch (start us, length us, event | category | flops | bytes accessed | tf_op | source)
XLA Modules:
  0.0 655.0 jit_solution(1428968502899495416)
XLA Ops:
  39.7 14.1 %collective-permute-done.16 = bf16[1,128,1024]{1,2,0:T(8,128)(2,1)S(1)} collective-permute-done((bf16[1,128,1024]{1,2,0:T(8,128)(2,1)}, bf16[1,128,1024]{1,2,0:T(8,128)(2,1)S(1)}, u32[]{:S(2)}, u32[]{:S(2)}) %collective-permute-start.16) | collective-permute-done | bytes 262176 | tf_op jit(solution)/shard_map/ppermute | solution.py:243
  53.8 5.6 collective-permute-done.17
  74.0 8.0 %collective-permute-done.3 = bf16[2,128,1024]{1,2,0:T(8,128)(2,1)} collective-permute-done((bf16[2,128,1024]{1,2,0:T(8,128)(2,1)S(1)}, bf16[2,128,1024]{1,2,0:T(8,128)(2,1)}, u32[]{:S(2)}, u32[]{:S(2)}) %collective-permute-start.3) | collective-permute-done | bytes 524320 | tf_op jit(solution)/shard_map/ppermute | solution.py:243
  88.6 9.0 %collective-permute-done.4 = bf16[2,128,1024]{1,2,0:T(8,128)(2,1)} collective-permute-done((bf16[2,128,1024]{1,2,0:T(8,128)(2,1)}, bf16[2,128,1024]{1,2,0:T(8,128)(2,1)}, u32[]{:S(2)}, u32[]{:S(2)}) %collective-permute-start.4) | collective-permute-done | bytes 524320 | tf_op jit(solution)/shard_map/ppermute | solution.py:243
  127.0 13.7 %collective-permute-done.24 = bf16[128,2048]{1,0:T(8,128)(2,1)S(1)} collective-permute-done((bf16[128,2048]{1,0:T(8,128)(2,1)S(1)}, bf16[128,2048]{1,0:T(8,128)(2,1)S(1)}, u32[]{:S(2)}, u32[]{:S(2)}) %collective-permute-start.24) | collective-permute-done | bytes 524320 | tf_op jit(solution)/shard_map/ppermute | solution.py:183
  147.9 9.9 %collective-permute-done.22 = bf16[128,2048]{1,0:T(8,128)(2,1)} collective-permute-done((bf16[128,2048]{1,0:T(8,128)(2,1)S(1)}, bf16[128,2048]{1,0:T(8,128)(2,1)}, u32[]{:S(2)}, u32[]{:S(2)}) %collective-permute-start.22) | collective-permute-done | bytes 524320 | tf_op jit(solution)/shard_map/ppermute | solution.py:183
  163.8 14.7 %all-to-all-done.1 = bf16[4,128,1920]{2,1,0:T(8,128)(2,1)} async-done(((bf16[4,128,1920]{2,1,0:T(8,128)(2,1)}), bf16[4,128,1920]{2,1,0:T(8,128)(2,1)}, u32[]{:S(2)}, u32[]{:S(2)}) %all-to-all-start.1) | async-done | bytes 1966112 | tf_op jit(solution)/shard_map/all_to_all | solution.py:210
  179.9 13.2 %collective-permute-done.26 = bf16[128,2048]{1,0:T(8,128)(2,1)S(1)} collective-permute-done((bf16[128,2048]{1,0:T(8,128)(2,1)S(1)}, bf16[128,2048]{1,0:T(8,128)(2,1)S(1)}, u32[]{:S(2)}, u32[]{:S(2)}) %collective-permute-start.26) | collective-permute-done | bytes 524320 | tf_op jit(solution)/shard_map/ppermute | solution.py:183
  215.7 13.6 %collective-permute-done.29 = bf16[128,2048]{1,0:T(8,128)(2,1)S(1)} collective-permute-done((bf16[128,2048]{1,0:T(8,128)(2,1)S(1)}, bf16[128,2048]{1,0:T(8,128)(2,1)S(1)}, u32[]{:S(2)}, u32[]{:S(2)}) %collective-permute-start.29) | collective-permute-done | bytes 524320 | tf_op jit(solution)/shard_map/ppermute | solution.py:183
  231.5 11.4 %collective-permute-done.30 = bf16[128,2048]{1,0:T(8,128)(2,1)S(1)} collective-permute-done((bf16[128,2048]{1,0:T(8,128)(2,1)S(1)}, bf16[128,2048]{1,0:T(8,128)(2,1)S(1)}, u32[]{:S(2)}, u32[]{:S(2)}) %collective-permute-start.30) | collective-permute-done | bytes 524320 | tf_op jit(solution)/shard_map/ppermute | solution.py:186
  244.5 11.4 %collective-permute-done.33 = bf16[128,2048]{1,0:T(8,128)(2,1)S(1)} collective-permute-done((bf16[128,2048]{1,0:T(8,128)(2,1)S(1)}, bf16[128,2048]{1,0:T(8,128)(2,1)S(1)}, u32[]{:S(2)}, u32[]{:S(2)}) %collective-permute-start.33) | collective-permute-done | bytes 524320 | tf_op jit(solution)/shard_map/ppermute | solution.py:183
  260.6 61.9 %all-gather.5.cloned.1.call-done = bf16[2048,1920]{1,0:T(8,128)(2,1)} async-done(((bf16[512,1920]{1,0:T(8,128)(2,1)}), bf16[2048,1920]{1,0:T(8,128)(2,1)}) %all-gather.5.cloned.1.call-update) | async-done | bytes 7864336 | tf_op jit(solution)/shard_map/all_gather | solution.py:228
  322.5 6.0 fusion.2
  334.8 5.5 fusion.28
  342.3 4.7 convolution_convert_fusion
  347.0 5.8 fusion.7
  360.3 12.5 %collective-permute-done.36 = bf16[128,2048]{1,0:T(8,128)(2,1)S(1)} collective-permute-done((bf16[128,2048]{1,0:T(8,128)(2,1)S(1)}, bf16[128,2048]{1,0:T(8,128)(2,1)S(1)}, u32[]{:S(2)}, u32[]{:S(2)}) %collective-permute-start.36) | collective-permute-done | bytes 524320 | tf_op jit(solution)/shard_map/ppermute | solution.py:183
  375.8 11.8 %collective-permute-done.37 = bf16[128,2048]{1,0:T(8,128)(2,1)S(1)} collective-permute-done((bf16[128,2048]{1,0:T(8,128)(2,1)S(1)}, bf16[128,2048]{1,0:T(8,128)(2,1)S(1)}, u32[]{:S(2)}, u32[]{:S(2)}) %collective-permute-start.37) | collective-permute-done | bytes 524320 | tf_op jit(solution)/shard_map/ppermute | solution.py:186
  390.9 10.9 %collective-permute-done.38 = bf16[128,2048]{1,0:T(8,128)(2,1)S(1)} collective-permute-done((bf16[128,2048]{1,0:T(8,128)(2,1)S(1)}, bf16[128,2048]{1,0:T(8,128)(2,1)S(1)}, u32[]{:S(2)}, u32[]{:S(2)}) %collective-permute-start.38) | collective-permute-done | bytes 524320 | tf_op jit(solution)/shard_map/ppermute | solution.py:183
  408.8 5.4 shard_map.316
  426.6 10.7 %collective-permute-done.44 = bf16[128,2048]{1,0:T(8,128)(2,1)S(1)} collective-permute-done((bf16[128,2048]{1,0:T(8,128)(2,1)S(1)}, bf16[128,2048]{1,0:T(8,128)(2,1)S(1)}, u32[]{:S(2)}, u32[]{:S(2)}) %collective-permute-start.44) | collective-permute-done | bytes 524320 | tf_op jit(solution)/shard_map/ppermute | solution.py:183
  442.2 8.8 %collective-permute-done.45 = bf16[128,2048]{1,0:T(8,128)(2,1)} collective-permute-done((bf16[128,2048]{1,0:T(8,128)(2,1)S(1)}, bf16[128,2048]{1,0:T(8,128)(2,1)}, u32[]{:S(2)}, u32[]{:S(2)}) %collective-permute-start.45) | collective-permute-done | bytes 524320 | tf_op jit(solution)/shard_map/ppermute | solution.py:186
  456.4 10.9 %collective-permute-done.46 = bf16[128,2048]{1,0:T(8,128)(2,1)S(1)} collective-permute-done((bf16[128,2048]{1,0:T(8,128)(2,1)S(1)}, bf16[128,2048]{1,0:T(8,128)(2,1)S(1)}, u32[]{:S(2)}, u32[]{:S(2)}) %collective-permute-start.46) | collective-permute-done | bytes 524320 | tf_op jit(solution)/shard_map/ppermute | solution.py:183
  477.1 7.5 %collective-permute-done.41 = bf16[128,2048]{1,0:T(8,128)(2,1)} collective-permute-done((bf16[128,2048]{1,0:T(8,128)(2,1)S(1)}, bf16[128,2048]{1,0:T(8,128)(2,1)}, u32[]{:S(2)}, u32[]{:S(2)}) %collective-permute-start.41) | collective-permute-done | bytes 524320 | tf_op jit(solution)/shard_map/ppermute | solution.py:183
  493.3 5.4 shard_map.317
  509.4 4.8 all-to-all-start.2
  528.6 34.4 %all-to-all-done.2 = bf16[4,4,128,1024]{3,2,0,1:T(8,128)(2,1)} async-done(((bf16[4,4,128,1024]{3,2,0,1:T(8,128)(2,1)}), bf16[4,4,128,1024]{3,2,0,1:T(8,128)(2,1)}, u32[]{:S(2)}, u32[]{:S(2)}) %all-to-all-start.2) | async-done | bytes 4194336 | tf_op jit(solution)/shard_map/all_to_all | solution.py:386
  563.0 4.7 copy.154
  569.3 4.9 collective-permute-done.49
  578.6 10.1 %collective-permute-done.50 = bf16[128,2048]{1,0:T(8,128)(2,1)S(1)} collective-permute-done((bf16[128,2048]{1,0:T(8,128)(2,1)S(1)}, bf16[128,2048]{1,0:T(8,128)(2,1)S(1)}, u32[]{:S(2)}, u32[]{:S(2)}) %collective-permute-start.50) | collective-permute-done | bytes 524320 | tf_op jit(solution)/shard_map/ppermute | solution.py:186
  609.6 8.3 %all-to-all-done.4 = bf16[4,128,1280]{2,1,0:T(8,128)(2,1)S(1)} async-done(((bf16[4,128,1280]{2,1,0:T(8,128)(2,1)}), bf16[4,128,1280]{2,1,0:T(8,128)(2,1)S(1)}, u32[]{:S(2)}, u32[]{:S(2)}) %all-to-all-start.4) | async-done | bytes 1310752 | tf_op jit(solution)/shard_map/all_to_all | solution.py:210
  626.3 12.0 %all-to-all-done.3 = bf16[4,128,1024]{1,2,0:T(8,128)(2,1)S(1)} async-done(((bf16[4,128,1024]{1,2,0:T(8,128)(2,1)}), bf16[4,128,1024]{1,2,0:T(8,128)(2,1)S(1)}, u32[]{:S(2)}, u32[]{:S(2)}) %all-to-all-start.3) | async-done | bytes 1048608 | tf_op jit(solution)/shard_map/all_to_all | solution.py:210
  (503 shorter events, 267.0 us)
Async XLA Ops:
  10.5 20.9 %collective-permute-start = (bf16[128,1024]{0,1:T(8,128)(2,1)}, bf16[128,1024]{0,1:T(8,128)(2,1)S(1)}, u32[]{:S(2)}, u32[]{:S(2)}) collective-permute-start(bf16[128,1024]{0,1:T(8,128)(2,1)} %pad_maximum_fusion.31), channel_id=1, source_target_pairs={{0,4},{2,6},{4,0},{6,2},{8,12},{10,14},{12,8},{14,10},{16,20},{18,... | collective-permute-start | bytes 786440 | tf_op jit(solution)/shard_map/ppermute | solution.py:183
  14.5 16.9 %collective-permute-start.1 = (bf16[128,1024]{0,1:T(8,128)(2,1)}, bf16[128,1024]{0,1:T(8,128)(2,1)S(1)}, u32[]{:S(2)}, u32[]{:S(2)}) collective-permute-start(bf16[128,1024]{0,1:T(8,128)(2,1)} %pad_maximum_fusion.32), channel_id=1, source_target_pairs={{0,6},{2,4},{4,2},{6,0},{8,14},{10,12},{12,10},{14,8},{16,22},{18,... | collective-permute-start | bytes 786440 | tf_op jit(solution)/shard_map/ppermute | solution.py:183
  15.6 17.5 %collective-permute-start.14 = (bf16[128,1024]{0,1:T(8,128)(2,1)}, bf16[128,1024]{0,1:T(8,128)(2,1)}, u32[]{:S(2)}, u32[]{:S(2)}) collective-permute-start(bf16[128,1024]{0,1:T(8,128)(2,1)} %pad_maximum_fusion.34), channel_id=1, source_target_pairs={{0,2},{2,0},{4,6},{6,4},{8,10},{10,8},{12,14},{14,12},{16,18},{18,... | collective-permute-start | bytes 786440 | tf_op jit(solution)/shard_map/ppermute | solution.py:183
  19.5 15.2 %collective-permute-start.15 = (bf16[1,128,1024]{1,2,0:T(8,128)(2,1)}, bf16[1,128,1024]{1,2,0:T(8,128)(2,1)}, u32[]{:S(2)}, u32[]{:S(2)}) collective-permute-start(bf16[1,128,1024]{1,2,0:T(8,128)(2,1)} %get-tuple-element.256), channel_id=1, source_target_pairs={{0,8},{2,10},{4,12},{6,14},{8,16},{10,18},{12,20},{14,22},{16,24},... | collective-permute-start | bytes 786440 | tf_op jit(solution)/shard_map/ppermute | solution.py:243
  31.5 28.7 %collective-permute-start.2 = (bf16[2,128,1024]{1,2,0:T(8,128)(2,1)S(1)}, bf16[2,128,1024]{1,2,0:T(8,128)(2,1)S(1)}, u32[]{:S(2)}, u32[]{:S(2)}) collective-permute-start(bf16[2,128,1024]{1,2,0:T(8,128)(2,1)S(1)} %pad_maximum_fusion.26), channel_id=1, source_target_pairs={{0,8},{2,10},{4,12},{6,14},{8,16},{10,18},{12,20},{14,22},{16,24},... | collective-permute-start | bytes 1572872 | tf_op jit(solution)/shard_map/ppermute | solution.py:243
  33.1 20.7 %collective-permute-start.16 = (bf16[1,128,1024]{1,2,0:T(8,128)(2,1)}, bf16[1,128,1024]{1,2,0:T(8,128)(2,1)S(1)}, u32[]{:S(2)}, u32[]{:S(2)}) collective-permute-start(bf16[1,128,1024]{1,2,0:T(8,128)(2,1)} %bitcast.62), channel_id=1, source_target_pairs={{0,8},{2,10},{4,12},{6,14},{8,16},{10,18},{12,20},{14,22},{16,24},... | collective-permute-start | bytes 786440 | tf_op jit(solution)/shard_map/ppermute | solution.py:243
  34.7 24.7 %collective-permute-start.17 = (bf16[1,128,1024]{1,2,0:T(8,128)(2,1)}, bf16[1,128,1024]{1,2,0:T(8,128)(2,1)S(1)}, u32[]{:S(2)}, u32[]{:S(2)}) collective-permute-start(bf16[1,128,1024]{1,2,0:T(8,128)(2,1)} %collective-permute-done.15), channel_id=1, source_target_pairs={{0,8},{2,10},{4,12},{6,14},{8,16},{10,18},{12,20},{14,22},{16,24},... | collective-permute-start | bytes 786440 | tf_op jit(solution)/shard_map/ppermute | solution.py:243
  59.4 26.1 %collective-permute-start.19 = (bf16[1,128,1024]{1,2,0:T(8,128)(2,1)S(1)}, bf16[1,128,1024]{1,2,0:T(8,128)(2,1)S(1)}, u32[]{:S(2)}, u32[]{:S(2)}) collective-permute-start(bf16[1,128,1024]{1,2,0:T(8,128)(2,1)S(1)} %collective-permute-done.17), channel_id=1, source_target_pairs={{0,8},{2,10},{4,12},{6,14},{8,16},{10,18},{12,20},{14,22},{16,24},... | collective-permute-start | bytes 786440 | tf_op jit(solution)/shard_map/ppermute | solution.py:243
  61.7 20.3 %collective-permute-start.3 = (bf16[2,128,1024]{1,2,0:T(8,128)(2,1)S(1)}, bf16[2,128,1024]{1,2,0:T(8,128)(2,1)}, u32[]{:S(2)}, u32[]{:S(2)}) collective-permute-start(bf16[2,128,1024]{1,2,0:T(8,128)(2,1)S(1)} %collective-permute-done.2), channel_id=1, source_target_pairs={{0,8},{2,10},{4,12},{6,14},{8,16},{10,18},{12,20},{14,22},{16,24},... | collective-permute-start | bytes 1572872 | tf_op jit(solution)/shard_map/ppermute | solution.py:243
  63.0 25.5 %all-to-all-start = ((bf16[4,128,1024]{2,1,0:T(8,128)(2,1)}), bf16[4,128,1024]{2,1,0:T(8,128)(2,1)}, u32[]{:S(2)}, u32[]{:S(2)}) async-start(bf16[4,128,1024]{2,1,0:T(8,128)(2,1)} %pad_maximum_fusion.11), calls=%async_computation | async-start | bytes 2097152 | tf_op jit(solution)/shard_map/all_to_all | solution.py:210
  67.3 132.0 %all-gather.3.cloned.1.call-start = ((), (), s32[]{:S(2)}) async-start(), calls=%async_computation.10 | async-start | bytes 5242880 | tf_op jit(solution)/shard_map/all_gather | solution.py:228
  68.1 19.4 %collective-permute-start.20 = (bf16[1,128,1024]{1,2,0:T(8,128)(2,1)S(1)}, bf16[1,128,1024]{1,2,0:T(8,128)(2,1)S(1)}, u32[]{:S(2)}, u32[]{:S(2)}) collective-permute-start(bf16[1,128,1024]{1,2,0:T(8,128)(2,1)S(1)} %collective-permute-done.18), channel_id=1, source_target_pairs={{0,8},{2,10},{4,12},{6,14},{8,16},{10,18},{12,20},{14,22},{16,24},... | collective-permute-start | bytes 786440 | tf_op jit(solution)/shard_map/ppermute | solution.py:243
  82.0 15.6 %collective-permute-start.4 = (bf16[2,128,1024]{1,2,0:T(8,128)(2,1)}, bf16[2,128,1024]{1,2,0:T(8,128)(2,1)}, u32[]{:S(2)}, u32[]{:S(2)}) collective-permute-start(bf16[2,128,1024]{1,2,0:T(8,128)(2,1)} %collective-permute-done.3), channel_id=1, source_target_pairs={{0,8},{2,10},{4,12},{6,14},{8,16},{10,18},{12,20},{14,22},{16,24},... | collective-permute-start | bytes 1572872 | tf_op jit(solution)/shard_map/ppermute | solution.py:243
  125.8 16.0 %collective-permute-start.21 = (bf16[2,128,2048]{2,1,0:T(8,128)(2,1)S(1)}, bf16[2,128,2048]{2,1,0:T(8,128)(2,1)S(1)}, u32[]{:S(2)}, u32[]{:S(2)}) collective-permute-start(bf16[2,128,2048]{2,1,0:T(8,128)(2,1)S(1)} %pad_maximum_fusion.13), channel_id=1, source_target_pairs={{0,2},{2,0},{4,6},{6,4},{8,10},{10,8},{12,14},{14,12},{16,18},{18,... | collective-permute-start | bytes 3145736 | tf_op jit(solution)/shard_map/ppermute | solution.py:183
  141.8 19.0 %collective-permute-start.25 = (bf16[2,128,2048]{2,1,0:T(8,128)(2,1)}, bf16[2,128,2048]{2,1,0:T(8,128)(2,1)}, u32[]{:S(2)}, u32[]{:S(2)}) collective-permute-start(bf16[2,128,2048]{2,1,0:T(8,128)(2,1)} %pad_maximum_fusion.14), channel_id=1, source_target_pairs={{0,2},{2,0},{4,6},{6,4},{8,10},{10,8},{12,14},{14,12},{16,18},{18,... | collective-permute-start | bytes 3145736 | tf_op jit(solution)/shard_map/ppermute | solution.py:183
  143.3 35.1 %all-to-all-start.1 = ((bf16[4,128,1920]{2,1,0:T(8,128)(2,1)}), bf16[4,128,1920]{2,1,0:T(8,128)(2,1)}, u32[]{:S(2)}, u32[]{:S(2)}) async-start(bf16[4,128,1920]{2,1,0:T(8,128)(2,1)} %pad_maximum_fusion.9), calls=%async_computation.1 | async-start | bytes 3932160 | tf_op jit(solution)/shard_map/all_to_all | solution.py:210
  147.8 174.7 %all-gather.5.cloned.1.call-start = ((), (), s32[]{:S(2)}) async-start(), calls=%async_computation.11 | async-start | bytes 9830400 | tf_op jit(solution)/shard_map/all_gather | solution.py:228
  159.2 19.2 %collective-permute-start.23 = (bf16[128,2048]{1,0:T(8,128)(2,1)S(1)}, bf16[128,2048]{1,0:T(8,128)(2,1)S(1)}, u32[]{:S(2)}, u32[]{:S(2)}) collective-permute-start(bf16[128,2048]{1,0:T(8,128)(2,1)S(1)} %fusion.59), channel_id=1, source_target_pairs={{0,1},{1,0},{2,3},{3,2},{4,5},{5,4},{6,7},{7,6},{8,9},{9,8},{10,11... | collective-permute-start | bytes 1572872 | tf_op jit(solution)/shard_map/ppermute | solution.py:186
  179.1 292.1 %reduce-scatter.11.cloned.1.call-start = ((), (), s32[]{:S(2)}) async-start(), calls=%async_computation.15 | async-start | bytes 3276800 | tf_op jit(solution)/shard_map/reduce_scatter | solution.py:256
  334.8 262.0 %reduce-scatter.9.cloned.1.call-start = ((), (), s32[]{:S(2)}) async-start(), calls=%async_computation.14 | async-start | bytes 6553600 | tf_op jit(solution)/shard_map/reduce_scatter | solution.py:256
  354.6 263.5 %reduce-scatter.7.cloned.1.call-start = ((), (), s32[]{:S(2)}) async-start(), calls=%async_computation.13 | async-start | bytes 5242880 | tf_op jit(solution)/shard_map/reduce_scatter | solution.py:256
  425.8 42.6 %collective-permute-start.40 = (bf16[2,128,2048]{2,1,0:T(8,128)(2,1)}, bf16[2,128,2048]{2,1,0:T(8,128)(2,1)}, u32[]{:S(2)}, u32[]{:S(2)}) collective-permute-start(bf16[2,128,2048]{2,1,0:T(8,128)(2,1)} %pad_maximum_fusion.21), channel_id=1, source_target_pairs={{0,2},{2,0},{4,6},{6,4},{8,10},{10,8},{12,14},{14,12},{16,18},{18,... | collective-permute-start | bytes 3145736 | tf_op jit(solution)/shard_map/ppermute | solution.py:183
  468.4 19.4 %collective-permute-start.47 = (bf16[2,128,2048]{2,1,0:T(8,128)(2,1)}, bf16[2,128,2048]{2,1,0:T(8,128)(2,1)}, u32[]{:S(2)}, u32[]{:S(2)}) collective-permute-start(bf16[2,128,2048]{2,1,0:T(8,128)(2,1)} %pad_maximum_fusion.23), channel_id=1, source_target_pairs={{0,2},{2,0},{4,6},{6,4},{8,10},{10,8},{12,14},{14,12},{16,18},{18,... | collective-permute-start | bytes 3145736 | tf_op jit(solution)/shard_map/ppermute | solution.py:183
  473.4 36.0 %all-to-all-start.5 = ((bf16[4,128,640]{1,2,0:T(8,128)(2,1)}), bf16[4,128,640]{1,2,0:T(8,128)(2,1)S(1)}, u32[]{:S(2)}, u32[]{:S(2)}) async-start(bf16[4,128,640]{1,2,0:T(8,128)(2,1)} %copy.156), calls=%async_computation.9 | async-start | bytes 1310720 | tf_op jit(solution)/shard_map/all_to_all | solution.py:210
  486.2 90.2 %collective-permute-start.42 = (bf16[128,2048]{1,0:T(8,128)(2,1)S(1)}, bf16[128,2048]{1,0:T(8,128)(2,1)}, u32[]{:S(2)}, u32[]{:S(2)}) collective-permute-start(bf16[128,2048]{1,0:T(8,128)(2,1)S(1)} %fusion.50), channel_id=1, source_target_pairs={{0,1},{1,0},{2,3},{3,2},{4,5},{5,4},{6,7},{7,6},{8,9},{9,8},{10,11... | collective-permute-start | bytes 1572872 | tf_op jit(solution)/shard_map/ppermute | solution.py:186
  509.4 53.5 %all-to-all-start.2 = ((bf16[4,4,128,1024]{3,2,0,1:T(8,128)(2,1)}), bf16[4,4,128,1024]{3,2,0,1:T(8,128)(2,1)}, u32[]{:S(2)}, u32[]{:S(2)}) async-start(bf16[4,4,128,1024]{3,2,0,1:T(8,128)(2,1)} %copy.153), calls=%async_computation.2 | async-start | bytes 8388608 | tf_op jit(solution)/shard_map/all_to_all | solution.py:386
  514.3 128.5 %reduce-scatter.5.cloned.1.call-start = ((), (), s32[]{:S(2)}) async-start(), calls=%async_computation.12 | async-start | bytes 5242880 | tf_op jit(solution)/shard_map/reduce_scatter | solution.py:256
  524.3 43.4 %collective-permute-start.51 = (bf16[2,128,2048]{2,1,0:T(8,128)(2,1)}, bf16[2,128,2048]{2,1,0:T(8,128)(2,1)}, u32[]{:S(2)}, u32[]{:S(2)}) collective-permute-start(bf16[2,128,2048]{2,1,0:T(8,128)(2,1)} %pad_maximum_fusion.25), channel_id=1, source_target_pairs={{0,2},{2,0},{4,6},{6,4},{8,10},{10,8},{12,14},{14,12},{16,18},{18,... | collective-permute-start | bytes 3145736 | tf_op jit(solution)/shard_map/ppermute | solution.py:183
  525.8 48.3 %collective-permute-start.49 = (bf16[128,2048]{1,0:T(8,128)(2,1)S(1)}, bf16[128,2048]{1,0:T(8,128)(2,1)S(1)}, u32[]{:S(2)}, u32[]{:S(2)}) collective-permute-start(bf16[128,2048]{1,0:T(8,128)(2,1)S(1)} %fusion.42), channel_id=1, source_target_pairs={{0,4},{2,6},{4,0},{6,2},{8,12},{10,14},{12,8},{14,10},{16,20},{18,... | collective-permute-start | bytes 1572872 | tf_op jit(solution)/shard_map/ppermute | solution.py:183
  569.1 20.6 %collective-permute-start.52 = (bf16[128,2048]{1,0:T(8,128)(2,1)S(1)}, bf16[128,2048]{1,0:T(8,128)(2,1)S(1)}, u32[]{:S(2)}, u32[]{:S(2)}) collective-permute-start(bf16[128,2048]{1,0:T(8,128)(2,1)S(1)} %fusion.39), channel_id=1, source_target_pairs={{0,4},{2,6},{4,0},{6,2},{8,12},{10,14},{12,8},{14,10},{16,20},{18,... | collective-permute-start | bytes 1572872 | tf_op jit(solution)/shard_map/ppermute | solution.py:183
  596.8 21.0 %all-to-all-start.4 = ((bf16[4,128,1280]{2,1,0:T(8,128)(2,1)}), bf16[4,128,1280]{2,1,0:T(8,128)(2,1)S(1)}, u32[]{:S(2)}, u32[]{:S(2)}) async-start(bf16[4,128,1280]{2,1,0:T(8,128)(2,1)} %bitcast.382), calls=%async_computation.7 | async-start | bytes 2621440 | tf_op jit(solution)/shard_map/all_to_all | solution.py:210
  620.4 18.0 %all-to-all-start.3 = ((bf16[4,128,1024]{1,2,0:T(8,128)(2,1)}), bf16[4,128,1024]{1,2,0:T(8,128)(2,1)S(1)}, u32[]{:S(2)}, u32[]{:S(2)}) async-start(bf16[4,128,1024]{1,2,0:T(8,128)(2,1)} %copy.155), calls=%async_computation.5 | async-start | bytes 2097152 | tf_op jit(solution)/shard_map/all_to_all | solution.py:210
  (122 other events, 782.0 us)
Sparse Core Ops, SparseCore 0:
  102.2 79.0 all-gather.2
  182.8 139.5 all-gather.4
  334.9 50.3 reduce-scatter.10
  387.4 93.3 reduce-scatter.8
  483.0 77.2 reduce-scatter.6
  567.9 74.8 reduce-scatter.4
